TPU v7x, 32 devices: a whole 2x2x4 slice. The times are simulated.
32 devices in a mesh: rep: 8 (over y, x, core), shard: 4 (over z).
Axes of the slice: x: 2, y: 2, z: 4, core: 2. Of those that a mesh axis runs over, the one named last changes fastest.
Arguments:
- hidden_in: bfloat16 [16384, 960], P(('rep', 'shard')), may hold values from -6 to 6
- cotangent: bfloat16 [16384, 960], P(('rep', 'shard')), may hold values from -6 to 6
- destination: int32 [16384], P(('rep', 'shard')), may hold values from 0 to 16383, as said below
- seq_lengths: int32 [4, 8], P('shard'), may hold values from 1 to 3584, 3840 in all within a row
- gate_mask: int32 [16384], P(('rep', 'shard')), may hold values 0 or 1
- query_weight: bfloat16 [960, 960], P('shard'), may hold values from -0.1875 to 0.1875
- key_matrix: bfloat16 [960, 320], P('shard'), may hold values from -0.1875 to 0.1875
- value_matrix: bfloat16 [960, 320], P('shard'), may hold values from -0.1875 to 0.1875
- out_weight: bfloat16 [960, 960], P('shard'), may hold values from -0.75 to 0.75
- gate_weight: bfloat16 [960, 2560], P('shard'), may hold values from -0.1875 to 0.1875
- up_weight: bfloat16 [960, 2560], P('shard'), may hold values from -0.1875 to 0.1875
- down_weight: bfloat16 [2560, 960], P('shard'), may hold values from -0.125 to 0.125
- attn_gain: bfloat16 [960], P('shard'), may hold values from 0.099609375 to 1.8984375
- ffn_gain: bfloat16 [960], P('shard'), may hold values from 0.099609375 to 1.8984375
- router_weight: bfloat16 [960], P('shard'), may hold values from -0.1875 to 0.1875
Outputs:
- outputs: bfloat16 [16384, 960], P(('rep', 'shard'))
- hidden_grad: bfloat16 [16384, 960], P(('rep', 'shard'))
- query_weight_grad: float32 [960, 960], P('shard')
- key_weight_grad: float32 [960, 320], P('shard')
- value_weight_grad: float32 [960, 320], P('shard')
- out_weight_grad: float32 [960, 960], P('shard')
- gate_weight_grad: float32 [960, 2560], P('shard')
- up_weight_grad: float32 [960, 2560], P('shard')
- down_weight_grad: float32 [2560, 960], P('shard')
- attn_gain_grad: float32 [960], P('shard')
- ffn_gain_grad: float32 [960], P('shard')
- router_weight_grad: float32 [960], P('shard')
Inputs may be any that keep to these rules, and one draw needn't show every extreme that they name: Each balanced position is the destination of exactly one token, and each device's 512 initial tokens go exactly 16 to each device's block of 512 balanced positions. `seq_lengths`: each line's lengths sum to 3840; the line's last 256 places are padding; the longest is 3584.
All inputs are finite; a program needn't handle non-finite values. No bound on the sum of `gate_mask` on one device may be relied on, other than what follows from the above.
Results may differ from a plain program's by a relative error of at most 0.023.
Values may be sent and summed in bfloat16 or wider, within the bound.
A program may use at most 192 MiB of HBM per device.

v0:
```python
import jax
import jax.numpy as jnp
from jax import lax
from jax.sharding import PartitionSpec as P

QUERY_HEADS = 15
KEY_VALUE_HEADS = 5
HEAD_DIM = 64


EPSILON = 1e-05
NEGATIVE_HUGE = -1e30
ROPE_BASE = 10000.0


def rms_scale(value_rows, gain_vec):
    return (
        value_rows
        * lax.rsqrt(jnp.mean(value_rows * value_rows, axis=-1, keepdims=True) + EPSILON)
        * gain_vec
    )


def apply_rotary(value_rows, rotary_angles):
    middle = value_rows.shape[-1] // 2
    leading = value_rows[..., :middle]
    trailing = value_rows[..., middle:]
    cosines = jnp.cos(rotary_angles)[:, None, :]
    sine_part = jnp.sin(rotary_angles)[:, None, :]
    return jnp.concatenate(
        [leading * cosines - trailing * sine_part, trailing * cosines + leading * sine_part],
        axis=-1,
    )


def rope_angles(within, head_size):
    steps_idx = jnp.arange(head_size // 2).astype(jnp.float32)
    frequency = jnp.power(ROPE_BASE, -2.0 * steps_idx / head_size)
    return within.astype(jnp.float32)[:, None] * frequency[None, :]


def line_layout(lengths_row, positions):
    seq_ends = jnp.cumsum(lengths_row, dtype=jnp.int32)
    reached = seq_ends[None, :] <= positions[:, None]
    segment = jnp.sum(reached.astype(jnp.int32), axis=1)
    starts = jnp.max(jnp.where(reached, seq_ends[None, :], 0), axis=1)
    within = positions - starts
    is_valid = positions < seq_ends[-1]
    return (segment, within, is_valid)


def score_block(
    query_block_tile, key_block_tile, query_pos, key_pos, query_codes, key_codes, score_scale
):
    scores = (
        jnp.einsum(
            "bnae,lne->nabl", query_block_tile, key_block_tile, preferred_element_type=jnp.float32
        )
        * score_scale
    )
    allowed = (key_pos[None, :] == query_pos[:, None]) | (
        key_codes[None, :] == query_codes[:, None]
    ) & (key_pos[None, :] <= query_pos[:, None])
    return (jnp.where(allowed[None, None], scores, NEGATIVE_HUGE), allowed)


def in_blocks(members, block_rows):
    total_rows = members[0].shape[0]
    count_blocks = total_rows // block_rows
    shaped = tuple(
        (member.reshape((count_blocks, block_rows) + member.shape[1:]) for member in members)
    )
    return shaped + (jnp.arange(count_blocks, dtype=jnp.int32) * block_rows,)


def local(
    hidden_in,
    cotangent,
    destination,
    seq_lengths,
    gate_mask,
    query_weight,
    key_matrix,
    value_matrix,
    out_weight,
    gate_weight,
    up_weight,
    down_weight,
    attn_gain,
    ffn_gain,
    router_weight,
):
    rows_per_device, model_width = hidden_in.shape
    devices = lax.axis_size(("rep", "shard"))
    per_pair = rows_per_device // devices
    row_index = jnp.arange(rows_per_device, dtype=jnp.int32)
    target = destination // rows_per_device
    earlier = (target[None, :] == target[:, None]) & (row_index[None, :] < row_index[:, None])
    slot_of_row = target * per_pair + jnp.sum(earlier.astype(jnp.int32), axis=1)
    row_of_slot = jnp.zeros((rows_per_device,), jnp.int32).at[slot_of_row].set(row_index)
    place_sent = (destination % rows_per_device)[row_of_slot].reshape(devices, per_pair)
    sent_hidden = hidden_in[row_of_slot].reshape(devices, per_pair, model_width)
    sent_grad = cotangent[row_of_slot].reshape(devices, per_pair, model_width)
    got_hidden, got_grad, got_place = (
        lax.all_to_all(sent_hidden, ("rep", "shard"), split_axis=0, concat_axis=0, tiled=True),
        lax.all_to_all(sent_grad, ("rep", "shard"), split_axis=0, concat_axis=0, tiled=True),
        lax.all_to_all(place_sent, ("rep", "shard"), split_axis=0, concat_axis=0, tiled=True),
    )
    got_place = got_place.reshape(rows_per_device)
    hidden = (
        jnp.zeros((rows_per_device, model_width), jnp.bfloat16)
        .at[got_place]
        .set(got_hidden.reshape(rows_per_device, model_width))
    )
    out_cot = (
        jnp.zeros((rows_per_device, model_width), jnp.bfloat16)
        .at[got_place]
        .set(got_grad.reshape(rows_per_device, model_width))
    )
    replicas = lax.axis_size("rep")
    sequence_rows = rows_per_device * replicas
    positions = lax.axis_index("rep") * rows_per_device + row_index
    segment, within, is_valid = line_layout(seq_lengths[0], positions)
    active = is_valid & (gate_mask == 1)
    key_code = jnp.where(active, segment, -1)
    (
        full_query,
        full_key,
        full_value,
        full_out,
        full_gate,
        full_up,
        full_down,
        gain_attn,
        gain_ffn,
        full_router,
    ) = (
        lax.all_gather(query_weight, "shard", axis=0, tiled=True),
        lax.all_gather(key_matrix, "shard", axis=0, tiled=True),
        lax.all_gather(value_matrix, "shard", axis=0, tiled=True),
        lax.all_gather(out_weight, "shard", axis=0, tiled=True),
        lax.all_gather(gate_weight, "shard", axis=0, tiled=True),
        lax.all_gather(up_weight, "shard", axis=0, tiled=True),
        lax.all_gather(down_weight, "shard", axis=0, tiled=True),
        lax.all_gather(attn_gain, "shard", axis=0, tiled=True),
        lax.all_gather(ffn_gain, "shard", axis=0, tiled=True),
        lax.all_gather(router_weight, "shard", axis=0, tiled=True),
    )
    head_repeats = QUERY_HEADS // KEY_VALUE_HEADS
    score_scale = HEAD_DIM ** (-0.5)
    rotary_angles = rope_angles(within, HEAD_DIM)
    hidden_f = hidden.astype(jnp.float32)
    gain_one = gain_attn.astype(jnp.float32)
    gain_two = gain_ffn.astype(jnp.float32)
    first_normalized = rms_scale(hidden_f, gain_one).astype(jnp.bfloat16)
    router_logit = jnp.dot(hidden, full_router, preferred_element_type=jnp.float32)
    gate_value = jax.nn.sigmoid(router_logit)
    active_f = active.astype(jnp.float32)
    branch_scale = active_f * gate_value
    query_before_rotary = jnp.dot(first_normalized, full_query, preferred_element_type=jnp.float32)
    key_before_rotary = jnp.dot(first_normalized, full_key, preferred_element_type=jnp.float32)
    value_batch = (
        jnp.dot(first_normalized, full_value, preferred_element_type=jnp.float32)
        .astype(jnp.bfloat16)
        .reshape(rows_per_device, KEY_VALUE_HEADS, HEAD_DIM)
    )
    query_batch = (
        apply_rotary(
            query_before_rotary.reshape(rows_per_device, QUERY_HEADS, HEAD_DIM), rotary_angles
        )
        .astype(jnp.bfloat16)
        .reshape(rows_per_device, KEY_VALUE_HEADS, head_repeats, HEAD_DIM)
    )
    key_batch = apply_rotary(
        key_before_rotary.reshape(rows_per_device, KEY_VALUE_HEADS, HEAD_DIM), rotary_angles
    ).astype(jnp.bfloat16)
    start_state = (
        jnp.full((KEY_VALUE_HEADS, head_repeats, rows_per_device), NEGATIVE_HUGE, jnp.float32),
        jnp.zeros((KEY_VALUE_HEADS, head_repeats, rows_per_device), jnp.float32),
        jnp.zeros((rows_per_device, KEY_VALUE_HEADS, head_repeats, HEAD_DIM), jnp.float32),
    )
    shard_piece = (
        lax.all_gather(key_batch, "rep", axis=0, tiled=True),
        lax.all_gather(value_batch, "rep", axis=0, tiled=True),
        lax.all_gather(key_code, "rep", axis=0, tiled=True),
    )
    block_rows = min(rows_per_device, shard_piece[0].shape[0])

    def forward_one_block(running, block_items):
        key_block_tile, value_block_tile, code_blk, offset = block_items
        key_pos = offset + jnp.arange(block_rows, dtype=jnp.int32)
        scores, allowed = score_block(
            query_batch, key_block_tile, positions, key_pos, segment, code_blk, score_scale
        )
        run_max, run_sum, accumulated = running
        new_max = jnp.maximum(run_max, jnp.max(scores, axis=-1))
        weights_now = jnp.where(allowed[None, None], jnp.exp(scores - new_max[..., None]), 0.0)
        factor = jnp.exp(run_max - new_max)
        run_sum = run_sum * factor + jnp.sum(weights_now, axis=-1)
        added_part = jnp.einsum(
            "impq,qil->piml",
            weights_now.astype(jnp.bfloat16),
            value_block_tile,
            preferred_element_type=jnp.float32,
        )
        accumulated = accumulated * jnp.transpose(factor, (2, 0, 1))[..., None] + added_part
        return ((new_max, run_sum, accumulated), None)

    result_state, unused = lax.scan(
        forward_one_block, start_state, in_blocks(shard_piece, block_rows)
    )
    run_max, run_sum, accumulated = result_state
    log_sum = run_max + jnp.log(run_sum)
    attention = accumulated / jnp.transpose(run_sum, (2, 0, 1))[..., None]
    attn_out_b = attention.reshape(rows_per_device, model_width).astype(jnp.bfloat16)
    attn_branch = jnp.dot(attn_out_b, full_out, preferred_element_type=jnp.float32)
    middle_state = hidden_f + attn_branch
    normed_two = rms_scale(middle_state, gain_two).astype(jnp.bfloat16)
    gate_pre = jnp.dot(normed_two, full_gate, preferred_element_type=jnp.float32)
    up_pre = jnp.dot(normed_two, full_up, preferred_element_type=jnp.float32)
    hidden_ffn = (jax.nn.silu(gate_pre) * up_pre).astype(jnp.bfloat16)
    ffn_branch = jnp.dot(hidden_ffn, full_down, preferred_element_type=jnp.float32)
    branch_sum = attn_branch + ffn_branch
    result = (hidden_f + branch_scale[:, None] * branch_sum).astype(jnp.bfloat16)
    grad_out = out_cot.astype(jnp.float32)
    grad_branch = branch_scale[:, None] * grad_out
    grad_logit = active_f * jnp.sum(grad_out * branch_sum, axis=1) * gate_value * (1.0 - gate_value)
    grad_ffn_b = grad_branch.astype(jnp.bfloat16)
    grad_hidden_ffn = jnp.einsum(
        "te,fe->tf", grad_ffn_b, full_down, preferred_element_type=jnp.float32
    )
    unused_out, silu_back = jax.vjp(
        lambda gate_part, up_part: jax.nn.silu(gate_part) * up_part, gate_pre, up_pre
    )
    grad_gate, grad_up = silu_back(grad_hidden_ffn)
    grad_gate_b = grad_gate.astype(jnp.bfloat16)
    grad_up_b = grad_up.astype(jnp.bfloat16)
    grad_normed_two = jnp.einsum(
        "tf,ef->te", grad_gate_b, full_gate, preferred_element_type=jnp.float32
    ) + jnp.einsum("tf,ef->te", grad_up_b, full_up, preferred_element_type=jnp.float32)
    unused_two, norm_two_back = jax.vjp(rms_scale, middle_state, gain_two)
    grad_middle, grad_gain_ffn = norm_two_back(grad_normed_two)
    grad_attn_b = (grad_branch + grad_middle).astype(jnp.bfloat16)
    grad_attention_b = (
        jnp.einsum("te,de->td", grad_attn_b, full_out, preferred_element_type=jnp.float32)
        .astype(jnp.bfloat16)
        .reshape(rows_per_device, KEY_VALUE_HEADS, head_repeats, HEAD_DIM)
    )
    delta_row = jnp.transpose(
        jnp.sum(grad_attention_b.astype(jnp.float32) * attention, axis=-1), (1, 2, 0)
    )

    def block_grads(
        query_block_tile,
        gradient_block,
        lse_blk,
        delta_blk,
        key_block_tile,
        value_block_tile,
        query_pos,
        key_pos,
        query_codes,
        key_codes,
    ):
        scores, allowed = score_block(
            query_block_tile,
            key_block_tile,
            query_pos,
            key_pos,
            query_codes,
            key_codes,
            score_scale,
        )
        softmax_probabilities = jnp.where(
            allowed[None, None], jnp.exp(scores - lse_blk[..., None]), 0.0
        )
        dprobs = jnp.einsum(
            "bnae,lne->nabl", gradient_block, value_block_tile, preferred_element_type=jnp.float32
        )
        score_gradient = (
            softmax_probabilities * (dprobs - delta_blk[..., None]) * score_scale
        ).astype(jnp.bfloat16)
        return (softmax_probabilities, score_gradient)

    start_back = (
        jnp.zeros((rows_per_device, KEY_VALUE_HEADS, head_repeats, HEAD_DIM), jnp.float32),
        jnp.zeros((sequence_rows, KEY_VALUE_HEADS, HEAD_DIM), jnp.float32),
        jnp.zeros((sequence_rows, KEY_VALUE_HEADS, HEAD_DIM), jnp.float32),
    )
    shard_piece = (
        lax.all_gather(key_batch, "rep", axis=0, tiled=True),
        lax.all_gather(value_batch, "rep", axis=0, tiled=True),
        lax.all_gather(key_code, "rep", axis=0, tiled=True),
    )
    both_block_rows = min(rows_per_device, shard_piece[0].shape[0])

    def both_one_block(running, block_items):
        key_block_tile, value_block_tile, code_blk, offset = block_items
        key_pos = offset + jnp.arange(both_block_rows, dtype=jnp.int32)
        softmax_probabilities, score_gradient = block_grads(
            query_batch,
            grad_attention_b,
            log_sum,
            delta_row,
            key_block_tile,
            value_block_tile,
            positions,
            key_pos,
            segment,
            code_blk,
        )
        grad_query_now, key_all, value_all = running
        grad_query_now = grad_query_now + jnp.einsum(
            "impq,qil->piml", score_gradient, key_block_tile, preferred_element_type=jnp.float32
        )
        key_increment = jnp.einsum(
            "eylj,leyn->jen", score_gradient, query_batch, preferred_element_type=jnp.float32
        )
        value_add = jnp.einsum(
            "eylj,leyn->jen",
            softmax_probabilities.astype(jnp.bfloat16),
            grad_attention_b,
            preferred_element_type=jnp.float32,
        )
        key_all = lax.dynamic_update_slice_in_dim(
            key_all,
            lax.dynamic_slice_in_dim(key_all, offset, both_block_rows, 0) + key_increment,
            offset,
            0,
        )
        value_all = lax.dynamic_update_slice_in_dim(
            value_all,
            lax.dynamic_slice_in_dim(value_all, offset, both_block_rows, 0) + value_add,
            offset,
            0,
        )
        return ((grad_query_now, key_all, value_all), None)

    result_state, unused = lax.scan(
        both_one_block, start_back, in_blocks(shard_piece, both_block_rows)
    )
    grad_query_rot, key_all, value_all = result_state
    rotated_key_gradient, value_gradient_float = (
        lax.psum_scatter(
            key_all.astype(jnp.bfloat16), "rep", scatter_dimension=0, tiled=True
        ).astype(jnp.float32),
        lax.psum_scatter(
            value_all.astype(jnp.bfloat16), "rep", scatter_dimension=0, tiled=True
        ).astype(jnp.float32),
    )
    unused_q, query_rot_back = jax.vjp(
        lambda value_rows: apply_rotary(value_rows, rotary_angles),
        query_before_rotary.reshape(rows_per_device, QUERY_HEADS, HEAD_DIM),
    )
    grad_query_b = (
        query_rot_back(grad_query_rot.reshape(rows_per_device, QUERY_HEADS, HEAD_DIM))[0]
        .reshape(rows_per_device, QUERY_HEADS * HEAD_DIM)
        .astype(jnp.bfloat16)
    )
    unused_k, key_unrotate = jax.vjp(
        lambda value_rows: apply_rotary(value_rows, rotary_angles),
        key_before_rotary.reshape(rows_per_device, KEY_VALUE_HEADS, HEAD_DIM),
    )
    key_gradient_batch = (
        key_unrotate(rotated_key_gradient)[0]
        .reshape(rows_per_device, KEY_VALUE_HEADS * HEAD_DIM)
        .astype(jnp.bfloat16)
    )
    value_gradient_batch = value_gradient_float.reshape(
        rows_per_device, KEY_VALUE_HEADS * HEAD_DIM
    ).astype(jnp.bfloat16)
    grad_normed_one = (
        jnp.einsum("tf,ef->te", grad_query_b, full_query, preferred_element_type=jnp.float32)
        + jnp.einsum("tf,ef->te", key_gradient_batch, full_key, preferred_element_type=jnp.float32)
        + jnp.einsum(
            "tf,ef->te", value_gradient_batch, full_value, preferred_element_type=jnp.float32
        )
    )
    unused_one, norm_one_back = jax.vjp(rms_scale, hidden_f, gain_one)
    grad_norm_x, grad_gain_attn = norm_one_back(grad_normed_one)
    grad_hidden = (
        grad_out + grad_middle + grad_norm_x + grad_logit[:, None] * full_router.astype(jnp.float32)
    )
    grad_terms = (
        jnp.einsum("td,te->de", first_normalized, grad_query_b, preferred_element_type=jnp.float32),
        jnp.einsum(
            "td,te->de", first_normalized, key_gradient_batch, preferred_element_type=jnp.float32
        ),
        jnp.einsum(
            "td,te->de", first_normalized, value_gradient_batch, preferred_element_type=jnp.float32
        ),
        jnp.einsum("td,te->de", attn_out_b, grad_attn_b, preferred_element_type=jnp.float32),
        jnp.einsum("td,tf->df", normed_two, grad_gate_b, preferred_element_type=jnp.float32),
        jnp.einsum("td,tf->df", normed_two, grad_up_b, preferred_element_type=jnp.float32),
        jnp.einsum("tf,te->fe", hidden_ffn, grad_ffn_b, preferred_element_type=jnp.float32),
        grad_gain_attn,
        grad_gain_ffn,
        jnp.sum(grad_logit[:, None] * hidden_f, axis=0),
    )
    group_sums = (
        lax.psum_scatter(
            grad_terms[0].astype(jnp.bfloat16), "shard", scatter_dimension=0, tiled=True
        ).astype(jnp.float32),
        lax.psum_scatter(
            grad_terms[1].astype(jnp.bfloat16), "shard", scatter_dimension=0, tiled=True
        ).astype(jnp.float32),
        lax.psum_scatter(
            grad_terms[2].astype(jnp.bfloat16), "shard", scatter_dimension=0, tiled=True
        ).astype(jnp.float32),
        lax.psum_scatter(
            grad_terms[3].astype(jnp.bfloat16), "shard", scatter_dimension=0, tiled=True
        ).astype(jnp.float32),
        lax.psum_scatter(
            grad_terms[4].astype(jnp.bfloat16), "shard", scatter_dimension=0, tiled=True
        ).astype(jnp.float32),
        lax.psum_scatter(
            grad_terms[5].astype(jnp.bfloat16), "shard", scatter_dimension=0, tiled=True
        ).astype(jnp.float32),
        lax.psum_scatter(
            grad_terms[6].astype(jnp.bfloat16), "shard", scatter_dimension=0, tiled=True
        ).astype(jnp.float32),
        lax.psum_scatter(
            grad_terms[7].astype(jnp.bfloat16), "shard", scatter_dimension=0, tiled=True
        ).astype(jnp.float32),
        lax.psum_scatter(
            grad_terms[8].astype(jnp.bfloat16), "shard", scatter_dimension=0, tiled=True
        ).astype(jnp.float32),
        lax.psum_scatter(
            grad_terms[9].astype(jnp.bfloat16), "shard", scatter_dimension=0, tiled=True
        ).astype(jnp.float32),
    )
    totals = (
        lax.psum(group_sums[0].astype(jnp.bfloat16), "rep").astype(jnp.float32),
        lax.psum(group_sums[1].astype(jnp.bfloat16), "rep").astype(jnp.float32),
        lax.psum(group_sums[2].astype(jnp.bfloat16), "rep").astype(jnp.float32),
        lax.psum(group_sums[3].astype(jnp.bfloat16), "rep").astype(jnp.float32),
        lax.psum(group_sums[4].astype(jnp.bfloat16), "rep").astype(jnp.float32),
        lax.psum(group_sums[5].astype(jnp.bfloat16), "rep").astype(jnp.float32),
        lax.psum(group_sums[6].astype(jnp.bfloat16), "rep").astype(jnp.float32),
        lax.psum(group_sums[7].astype(jnp.bfloat16), "rep").astype(jnp.float32),
        lax.psum(group_sums[8].astype(jnp.bfloat16), "rep").astype(jnp.float32),
        lax.psum(group_sums[9].astype(jnp.bfloat16), "rep").astype(jnp.float32),
    )
    back_out = result[got_place].reshape(devices, per_pair, model_width)
    back_grad = grad_hidden.astype(jnp.bfloat16)[got_place].reshape(devices, per_pair, model_width)
    home_out, home_grad = (
        lax.all_to_all(back_out, ("rep", "shard"), split_axis=0, concat_axis=0, tiled=True),
        lax.all_to_all(back_grad, ("rep", "shard"), split_axis=0, concat_axis=0, tiled=True),
    )
    final_out = home_out.reshape(rows_per_device, model_width)[slot_of_row]
    final_grad = home_grad.reshape(rows_per_device, model_width)[slot_of_row]
    return (
        final_out,
        final_grad,
        totals[0],
        totals[1],
        totals[2],
        totals[3],
        totals[4],
        totals[5],
        totals[6],
        totals[7],
        totals[8],
        totals[9],
    )


def solution(mesh):
    placed = (
        P(("rep", "shard"), None),
        P(("rep", "shard"), None),
        P(("rep", "shard")),
        P("shard", None),
        P(("rep", "shard")),
        P("shard", None),
        P("shard", None),
        P("shard", None),
        P("shard", None),
        P("shard", None),
        P("shard", None),
        P("shard", None),
        P("shard"),
        P("shard"),
        P("shard"),
    )
    return jax.shard_map(
        local,
        mesh=mesh,
        in_specs=placed,
        out_specs=(
            P(("rep", "shard"), None),
            P(("rep", "shard"), None),
            P("shard", None),
            P("shard", None),
            P("shard", None),
            P("shard", None),
            P("shard", None),
            P("shard", None),
            P("shard", None),
            P("shard"),
            P("shard"),
            P("shard"),
        ),
        check_vma=False,
    )
```

profile of v0, /device:TPU:0, one launch (start us, length us, event | category | flops | bytes accessed | tf_op | source)
XLA Modules:
  0.0 1561.5 jit_solution(4653557165505151471)
XLA Ops:
  35.0 39.3 %all-reduce.13 = (bf16[960]{0:T(1024)(128)(2,1)S(1)}, bf16[960]{0:T(1024)(128)(2,1)S(1)}, bf16[960]{0:T(1024)(128)(2,1)S(1)}) all-reduce(bf16[960]{0:T(1024)(128)(2,1)S(1)} %dynamic-update-slice.1, bf16[960]{0:T(1024)(128)(2,1)S(1)} %dynamic-update-slice.2, ...), channel_id=1, replica_groups=mesh['rep'=8,'shard'=4] {'shard'}, use_global_device_ids=true, to_apply=%add.5 | all-reduce | flops 2880 | bytes 11520
  74.4 22.4 %all-gather.2 = bf16[4,240,320]{1,2,0:T(8,128)(2,1)S(1)} all-gather(bf16[1,240,320]{1,2,0:T(8,128)(2,1)S(1)} %bitcast.269), channel_id=1, replica_groups=mesh['rep'=8,'shard'=4] {'shard'}, dimensions={0}, use_global_device_ids=true | all-gather | bytes 768000 | tf_op jit(solution)/shard_map/all_gather | solution.py:140
  106.2 16.1 %all-gather.1 = bf16[4,240,320]{1,2,0:T(8,128)(2,1)S(1)} all-gather(bf16[1,240,320]{1,2,0:T(8,128)(2,1)S(1)} %bitcast.270), channel_id=1, replica_groups=mesh['rep'=8,'shard'=4] {'shard'}, dimensions={0}, use_global_device_ids=true | all-gather | bytes 768000 | tf_op jit(solution)/shard_map/all_gather | solution.py:139
  148.7 13.2 all-to-all-done.3
  177.3 224.9 %while.30 = (s32[]{:T(128)}, f32[5,3,512]{2,1,0:T(4,128)S(1)}, f32[5,3,512]{2,1,0:T(4,128)S(1)}, f32[512,5,3,64]{0,3,2,1:T(8,128)}, s32[8]{0:T(128)S(1)}, /*inde...) while((s32[]{:T(128)}, f32[5,3,512]{2,1,0:T(4,128)S(1)}, ...), condition=%wide.region_10.11_spmd.clone, body=%wide.region_7.10_spmd.clone.sunk | while | flops 1060583424 | bytes 70041832 | solution.py:209
  186.8 9.4 fusion.173
  214.9 9.4 fusion.173
  243.5 9.5 fusion.173
  271.6 9.4 fusion.173
  327.6 9.5 fusion.173
  355.7 9.5 fusion.173
  423.6 70.5 %all-gather.23.cloned.1.call-done = bf16[2560,960]{0,1:T(8,128)(2,1)} async-done(((bf16[640,960]{0,1:T(8,128)(2,1)}), bf16[2560,960]{0,1:T(8,128)(2,1)}) %all-gather.23.cloned.1.call-update) | async-done | bytes 4915216 | tf_op jit(solution)/shard_map/all_gather | solution.py:144
  494.2 9.5 multiply_convert_fusion
  527.8 385.6 %while.31 = (s32[]{:T(128)}, f32[512,5,3,64]{0,3,2,1:T(8,128)}, f32[4096,5,64]{0,2,1:T(8,128)}, f32[4096,5,64]{0,2,1:T(8,128)}, bf16[8,512,5,64]{1,3,2,0:T(8,128...) while((s32[]{:T(128)}, f32[512,5,3,64]{0,3,2,1:T(8,128)}, ...), condition=%wide.region_16.17_spmd.clone, body=%wide.region_15.16_spmd.clone.sunk | while | flops 2570322944 | bytes 85764352 | solution.py:339
  540.2 9.9 fusion.188
  587.8 9.9 fusion.188
  636.2 9.9 fusion.188
  684.7 9.9 fusion.188
  733.1 9.9 fusion.188
  781.5 9.9 fusion.188
  829.9 9.9 fusion.188
  878.3 9.8 fusion.188
  922.4 37.5 %reduce-scatter.18.cloned.1.call-done = bf16[512,5,64]{0,2,1:T(8,128)(2,1)} async-done(((bf16[4096,5,64]{0,2,1:T(8,128)(2,1)}), bf16[512,5,64]{0,2,1:T(8,128)(2,1)}) %reduce-scatter.18.cloned.1.call-update) | async-done | bytes 327696 | tf_op jit(solution)/shard_map/reduce_scatter | solution.py:347
  962.7 44.0 %reduce-scatter.16.cloned.1.call-done = bf16[512,5,64]{0,2,1:T(8,128)(2,1)} async-done(((bf16[4096,5,64]{0,2,1:T(8,128)(2,1)}), bf16[512,5,64]{0,2,1:T(8,128)(2,1)}) %reduce-scatter.16.cloned.1.call-update) | async-done | bytes 327696 | tf_op jit(solution)/shard_map/reduce_scatter | solution.py:344
  1067.8 95.1 %reduce-scatter.32.cloned.1.call-done = bf16[640,960]{1,0:T(8,128)(2,1)} async-done(((bf16[2560,960]{1,0:T(8,128)(2,1)}), bf16[640,960]{1,0:T(8,128)(2,1)}) %reduce-scatter.32.cloned.1.call-update) | async-done | bytes 1228816
  1165.4 46.2 %reduce-scatter.22.cloned.1.call-done = bf16[240,960]{1,0:T(8,128)(2,1)} async-done(((bf16[960,960]{1,0:T(8,128)(2,1)}), bf16[240,960]{1,0:T(8,128)(2,1)}) %reduce-scatter.22.cloned.1.call-update) | async-done | bytes 460816 | tf_op jit(solution)/shard_map/reduce_scatter | solution.py:410
  1211.6 43.5 %reduce-scatter.20.cloned.1.call-done = bf16[240,960]{1,0:T(8,128)(2,1)} async-done(((bf16[960,960]{1,0:T(8,128)(2,1)}), bf16[240,960]{1,0:T(8,128)(2,1)}) %reduce-scatter.20.cloned.1.call-update) | async-done | bytes 460816 | tf_op jit(solution)/shard_map/reduce_scatter | solution.py:401
  1255.1 89.8 %reduce-scatter.26.cloned.1.call-done = bf16[240,2560]{1,0:T(8,128)(2,1)} async-done(((bf16[960,2560]{1,0:T(8,128)(2,1)}), bf16[240,2560]{1,0:T(8,128)(2,1)}) %reduce-scatter.26.cloned.1.call-update) | async-done | bytes 1228816 | tf_op jit(solution)/shard_map/reduce_scatter | solution.py:416
  1344.9 91.2 %reduce-scatter.24.cloned.1.call-done = bf16[240,2560]{1,0:T(8,128)(2,1)} async-done(((bf16[960,2560]{1,0:T(8,128)(2,1)}), bf16[240,2560]{1,0:T(8,128)(2,1)}) %reduce-scatter.24.cloned.1.call-update) | async-done | bytes 1228816 | tf_op jit(solution)/shard_map/reduce_scatter | solution.py:413
  1456.0 18.3 %all-reduce.12 = (bf16[960]{0:T(1024)(128)(2,1)S(1)}, bf16[960]{0:T(1024)(128)(2,1)S(1)}, bf16[960]{0:T(1024)(128)(2,1)S(1)}) all-reduce(bf16[960]{0:T(1024)(128)(2,1)S(1)} %get-tuple-element.388, bf16[960]{0:T(1024)(128)(2,1)S(1)} %copy-done.55, bf16[960]{0:T(1024)(128)(2,1)S(1)} %copy-done.56), channel_id=11, replica_groups=mesh['rep'=8,'shard'=4] {'shard'}, use_global_device_ids=true, to_apply=%region_36.37.clone | all-reduce | flops 2880 | bytes 11520
  1474.6 12.5 all-reduce.10
  1492.1 51.1 %all-reduce.16.cloned.1.call-done = (bf16[240,960]{1,0:T(8,128)(2,1)}, bf16[240,320]{0,1:T(8,128)(2,1)}, bf16[240,320]{0,1:T(8,128)(2,1)}, bf16[240,960]{1,0:T(8...) async-done(((bf16[240,960]{1,0:T(8,128)(2,1)}, bf16[240,320]{0,1:T(8,128)(2,1)}, bf16[240,320]{0,1:T(8,128)(2,1)}, ...) | async-done | bytes 4915216 | tf_op jit(solution)/shard_map/psum | solution.py:433
  (503 shorter events, 692.2 us)
Async XLA Ops:
  7.2 159.5 %all-gather.13.cloned.1.call-start = ((), (), s32[]{:S(2)}) async-start(), calls=%async_computation.15 | async-start | bytes 2457600 | tf_op jit(solution)/shard_map/all_gather | solution.py:138
  15.6 14.8 all-to-all-start
  26.2 48.2 %copy-start.31 = (bf16[240,320]{0,1:T(8,128)(2,1)S(1)}, bf16[240,320]{0,1:T(8,128)(2,1)}, u32[]{:S(2)}) copy-start(bf16[240,320]{0,1:T(8,128)(2,1)} %param.26) | copy-start | bytes 460804
  30.3 68.9 %all-to-all-start.1 = ((bf16[32,16,960]{2,1,0:T(8,128)(2,1)}), bf16[32,16,960]{2,1,0:T(8,128)(2,1)S(1)}, u32[]{:S(2)}, u32[]{:S(2)}) async-start(bf16[32,16,960]{2,1,0:T(8,128)(2,1)} %bitcast.2), calls=%async_computation.1 | async-start | bytes 2097152 | tf_op jit(solution)/shard_map/all_to_all | solution.py:105
  33.0 137.1 %all-gather.15.cloned.1.call-start = ((), (), s32[]{:S(2)}) async-start(), calls=%async_computation.16 | async-start | bytes 2949120 | tf_op jit(solution)/shard_map/all_gather | solution.py:184
  74.4 64.0 %copy-start.51 = (bf16[960]{0:T(1024)(128)(2,1)}, bf16[960]{0:T(1024)(128)(2,1)S(1)}, u32[]{:S(2)}) copy-start(bf16[960]{0:T(1024)(128)(2,1)S(1)} %get-tuple-element.458) | copy-start | bytes 5764
  74.4 92.3 %copy-start.35 = (f32[960]{0:T(1024)}, f32[960]{0:T(1024)S(1)}, u32[]{:S(2)}) copy-start(f32[960]{0:T(1024)S(1)} %convert_element_type.199) | copy-start | bytes 11524
  99.3 62.6 %copy-start.53 = (s32[512,1]{0,1:T(1,128)}, s32[512,1]{0,1:T(1,128)S(1)}, u32[]{:S(2)}) copy-start(s32[512,1]{0,1:T(1,128)S(1)} %compare_select_fusion.1) | copy-start | bytes 6148
  104.3 411.6 %copy-start = (bf16[512,960]{0,1:T(8,128)(2,1)}, bf16[512,960]{0,1:T(8,128)(2,1)S(1)}, u32[]{:S(2)}) copy-start(bf16[512,960]{0,1:T(8,128)(2,1)S(1)} %copy.84) | copy-start | bytes 2949124
  104.6 62.1 %copy-start.41 = (f32[512]{0:T(512)}, f32[512]{0:T(512)S(1)}, u32[]{:S(2)}) copy-start(f32[512]{0:T(512)S(1)} %fusion.85) | copy-start | bytes 6148
  105.9 67.7 %all-gather.11.cloned.1.call-start = ((), (), s32[]{:S(2)}) async-start(), calls=%async_computation.14 | async-start | bytes 2949120 | tf_op jit(solution)/shard_map/all_gather | solution.py:183
  127.3 276.7 %all-gather.17.cloned.1.call-start = ((), (), s32[]{:S(2)}) async-start(), calls=%async_computation.17 | async-start | bytes 2457600 | tf_op jit(solution)/shard_map/all_gather | solution.py:141
  127.8 281.0 %all-gather.21.cloned.1.call-start = ((), (), s32[]{:S(2)}) async-start(), calls=%async_computation.19 | async-start | bytes 6144000 | tf_op jit(solution)/shard_map/all_gather | solution.py:143
  128.4 288.2 %all-gather.19.cloned.1.call-start = ((), (), s32[]{:S(2)}) async-start(), calls=%async_computation.18 | async-start | bytes 6144000 | tf_op jit(solution)/shard_map/all_gather | solution.py:142
  133.3 28.7 %all-to-all-start.3 = ((bf16[32,16,960]{2,1,0:T(8,128)(2,1)}), bf16[32,16,960]{2,1,0:T(8,128)(2,1)}, u32[]{:S(2)}, u32[]{:S(2)}) async-start(bf16[32,16,960]{2,1,0:T(8,128)(2,1)} %bitcast.247), calls=%async_computation.3 | async-start | bytes 2097152 | tf_op jit(solution)/shard_map/all_to_all | solution.py:106
  137.0 357.2 %all-gather.23.cloned.1.call-start = ((), (), s32[]{:S(2)}) async-start(), calls=%async_computation.20 | async-start | bytes 6144000 | tf_op jit(solution)/shard_map/all_gather | solution.py:144
  137.8 822.1 %reduce-scatter.18.cloned.1.call-start = ((), (), s32[]{:S(2)}) async-start(), calls=%async_computation.22 | async-start | bytes 2949120 | tf_op jit(solution)/shard_map/reduce_scatter | solution.py:347
  138.4 377.5 %copy-start.33 = (f32[960]{0:T(1024)}, f32[960]{0:T(1024)S(1)}, u32[]{:S(2)}) copy-start(f32[960]{0:T(1024)S(1)} %convert_element_type.206) | copy-start | bytes 11524
  139.5 376.4 %copy-start.45 = (f32[512]{0:T(512)}, f32[512]{0:T(512)S(1)}, u32[]{:S(2)}) copy-start(f32[512]{0:T(512)S(1)} %get-tuple-element.461) | copy-start | bytes 6148
  407.2 108.7 %copy-start.37 = (f32[512]{0:T(512)}, f32[512]{0:T(512)S(1)}, u32[]{:S(2)}) copy-start(f32[512]{0:T(512)S(1)} %fusion.86) | copy-start | bytes 6148
  917.8 88.9 %reduce-scatter.16.cloned.1.call-start = ((), (), s32[]{:S(2)}) async-start(), calls=%async_computation.21 | async-start | bytes 2949120 | tf_op jit(solution)/shard_map/reduce_scatter | solution.py:344
  922.3 142.0 %reduce-scatter.30.cloned.1.call-start = ((), (), s32[]{:S(2)}) async-start(), calls=%async_computation.28 | async-start | bytes 921600
  961.5 46.3 %copy-start.17 = (f32[512,32]{0,1:T(8,128)S(1)}, f32[512,32]{0,1:T(8,128)}, u32[]{:S(2)}) copy-start(f32[512,32]{0,1:T(8,128)} %copy-done.16) | copy-start | bytes 196612
  962.7 103.4 %reduce-scatter.28.cloned.1.call-start = ((), (), s32[]{:S(2)}) async-start(), calls=%async_computation.27 | async-start | bytes 921600
  1009.8 153.2 %reduce-scatter.32.cloned.1.call-start = ((), (), s32[]{:S(2)}) async-start(), calls=%async_computation.29 | async-start | bytes 6553600
  1023.9 187.7 %reduce-scatter.22.cloned.1.call-start = ((), (), s32[]{:S(2)}) async-start(), calls=%async_computation.24 | async-start | bytes 2457600 | tf_op jit(solution)/shard_map/reduce_scatter | solution.py:410
  1028.9 226.2 %reduce-scatter.20.cloned.1.call-start = ((), (), s32[]{:S(2)}) async-start(), calls=%async_computation.23 | async-start | bytes 2457600 | tf_op jit(solution)/shard_map/reduce_scatter | solution.py:401
  1034.4 310.5 %reduce-scatter.26.cloned.1.call-start = ((), (), s32[]{:S(2)}) async-start(), calls=%async_computation.26 | async-start | bytes 6144000 | tf_op jit(solution)/shard_map/reduce_scatter | solution.py:416
  1041.7 394.3 %reduce-scatter.24.cloned.1.call-start = ((), (), s32[]{:S(2)}) async-start(), calls=%async_computation.25 | async-start | bytes 6144000 | tf_op jit(solution)/shard_map/reduce_scatter | solution.py:413
  1052.8 392.3 %all-to-all-start.2 = ((bf16[32,16,960]{2,1,0:T(8,128)(2,1)}), bf16[32,16,960]{2,1,0:T(8,128)(2,1)S(1)}, u32[]{:S(2)}, u32[]{:S(2)}) async-start(bf16[32,16,960]{2,1,0:T(8,128)(2,1)} %bitcast.245), calls=%async_computation.2 | async-start | bytes 2097152 | tf_op jit(solution)/shard_map/all_to_all | solution.py:447
  1057.4 485.7 %all-reduce.16.cloned.1.call-start = ((), (), s32[]{:S(2)}) async-start(), calls=%async_computation.30 | async-start | bytes 9994240 | tf_op jit(solution)/shard_map/psum | solution.py:433
  1445.2 43.6 %all-to-all-start.4 = ((bf16[32,16,960]{2,1,0:T(8,128)(2,1)}), bf16[32,16,960]{2,1,0:T(8,128)(2,1)S(1)}, u32[]{:S(2)}, u32[]{:S(2)}) async-start(bf16[32,16,960]{2,1,0:T(8,128)(2,1)} %bitcast.246), calls=%async_computation.6 | async-start | bytes 2097152 | tf_op jit(solution)/shard_map/all_to_all | solution.py:448
  (74 other events, 559.2 us)
Sparse Core Ops, SparseCore 0:
  9.6 67.9 all-gather.12
  106.1 29.6 all-gather.14
  138.2 33.1 all-gather.10
  172.8 43.2 all-gather.16
  217.6 91.4 all-gather.20
  310.5 91.0 all-gather.18
  403.2 90.9 all-gather.22
  918.0 41.8 reduce-scatter.17
  963.2 43.4 reduce-scatter.15
  1009.4 23.0 reduce-scatter.29
  1035.4 22.1 reduce-scatter.27
  1059.8 103.1 reduce-scatter.31
  1165.3 46.2 reduce-scatter.21
  1214.3 40.7 reduce-scatter.19
  1257.3 87.5 reduce-scatter.25
  1347.0 88.9 reduce-scatter.23
  1440.8 102.3 all-reduce.15
where the time goes:
time: 1570 us; the launch traced here: 1560 us
  waiting for transfers between devices  589 us (38%)
  matrix products  491 us (31%)
  local copies, waits for them, and re-layouts  175 us (11%)
  other arithmetic  130 us (8%)
  blocking collectives  118 us (8%)
  starting transfers between devices  24.8 us (2%)
  loops' own time  16.9 us (1%)
  between operations  16.5 us (1%)
    dot_general x16, matrix products, score_block(): jnp.einsum('bnae,lne->nabl', query_block_tile, key_block_tile, preferred_...  132 us
    unnamed x20, waiting for transfers between devices  97.8 us
    reduce_scatter x1, waiting for transfers between devices, local(): lax.psum_scatter(grad_terms[4].astype(jnp.bfloat16), 'shard', scatter_dim...  91.2 us
    reduce_scatter x1, waiting for transfers between devices, local(): lax.psum_scatter(grad_terms[5].astype(jnp.bfloat16), 'shard', scatter_dim...  89.8 us
    dot_general x8, matrix products, both_one_block(): jnp.einsum('eylj,leyn->jen', softmax_probabilities.astype(jnp.bfloat16),...  79 us
    reduce_sum x8, other arithmetic, forward_one_block(): run_sum = run_sum * factor + jnp.sum(weights_now, axis=-1)  75.4 us
    dot_general x8, matrix products, block_grads(): jnp.einsum('bnae,lne->nabl', gradient_block, value_block_tile, preferred_...  74.1 us
    all_gather x1, waiting for transfers between devices, local(): lax.all_gather(down_weight, 'shard', axis=0, tiled=True)  70.5 us
  transfers between devices with their start and end apart: 22, of which 11 were waited for; matrix products, arithmetic and copies ran while one was open for 23% of the time, Pallas kernels for 0%

commit v1 on v0

v1 whole, which is shorter than its diff:
```python
import functools

import jax
import jax.numpy as jnp
from jax import lax
from jax.experimental import pallas as pl
from jax.experimental.pallas import tpu as pltpu
from jax.sharding import Mesh
from jax.sharding import PartitionSpec as P

QUERY_HEADS = 15
KEY_VALUE_HEADS = 5
HEAD_DIM = 64
GROUP = QUERY_HEADS // KEY_VALUE_HEADS
EPSILON = 1e-05
NEGATIVE_HUGE = -1e30
ROPE_BASE = 10000.0
bf16 = jnp.bfloat16
f32 = jnp.float32
MESH = pl.DeviceIdType.MESH
REP = ("chip", "core")
ALL = ("chip", "core", "shard")
VMEM_SPEC = pl.BlockSpec(memory_space=pltpu.VMEM)


def dot(a, b, ca=1, cb=0):
    return lax.dot_general(a, b, (((ca,), (cb,)), ((), ())), preferred_element_type=f32)


def peer_coords(index, axes, sizes):
    coords = {}
    for name in reversed(axes):
        coords[name] = lax.rem(index, sizes[name])
        index = index // sizes[name]
    return coords


def exchange_kernel(specs, sizes, *refs):
    n = len(specs)
    ins, outs, sems = refs[:n], refs[n : 2 * n], refs[2 * n :]
    barrier = pltpu.get_barrier_semaphore()
    widest = max((axes for axes, _ in specs), key=lambda axes: len(axes))
    total = 1
    for name in widest:
        total *= sizes[name]
    me_all = lax.axis_index(widest)

    def greet(k, carry):
        peer = lax.rem(me_all + k, total)
        pl.semaphore_signal(
            barrier, inc=1, device_id=peer_coords(peer, widest, sizes), device_id_type=MESH
        )
        return carry

    lax.fori_loop(1, total, greet, 0)
    pl.semaphore_wait(barrier, total - 1)

    def copy_to(i, k):
        axes, spread = specs[i]
        count = 1
        for name in axes:
            count *= sizes[name]
        me = lax.axis_index(axes)
        peer = lax.rem(me + k, count)
        return pltpu.make_async_remote_copy(
            src_ref=ins[i] if spread else ins[i].at[peer],
            dst_ref=outs[i].at[me],
            send_sem=sems[2 * i].at[k],
            recv_sem=sems[2 * i + 1].at[k],
            device_id=peer_coords(peer, axes, sizes),
            device_id_type=MESH,
        )

    counts = []
    for i, (axes, spread) in enumerate(specs):
        count = 1
        for name in axes:
            count *= sizes[name]
        counts.append(count)

        def send(k, carry, i=i):
            copy_to(i, k).start()
            return carry

        lax.fori_loop(1, count, send, 0)
    for i, (axes, spread) in enumerate(specs):
        me = lax.axis_index(axes)
        outs[i][me] = ins[i][...] if spread else ins[i][me]
    for i in range(n):

        def finish(k, carry, i=i):
            copy_to(i, k).wait()
            return carry

        lax.fori_loop(1, counts[i], finish, 0)


def exchange(collective_id, sizes, items):
    specs = tuple((axes, spread) for _, axes, spread in items)
    out_shape, scratch = [], []
    for array, axes, spread in items:
        count = 1
        for name in axes:
            count *= sizes[name]
        shape = (count,) + array.shape if spread else array.shape
        out_shape.append(jax.ShapeDtypeStruct(shape, array.dtype))
        scratch += [pltpu.SemaphoreType.DMA((count,)), pltpu.SemaphoreType.DMA((count,))]
    return pl.pallas_call(
        functools.partial(exchange_kernel, specs, sizes),
        out_shape=out_shape,
        in_specs=[VMEM_SPEC] * len(items),
        out_specs=[VMEM_SPEC] * len(items),
        scratch_shapes=scratch,
        compiler_params=pltpu.CompilerParams(collective_id=collective_id, has_side_effects=True),
        name="exchange_%d" % collective_id,
    )(*[array for array, _, _ in items])


def mask_rows(code_row):
    index = lax.broadcasted_iota(jnp.int32, (16, code_row.shape[1]), 0)
    return jnp.where(index == code_row, 0.0, NEGATIVE_HUGE).astype(bf16)


def segment_rows(segment_row):
    index = lax.broadcasted_iota(jnp.int32, (16, segment_row.shape[1]), 0)
    return jnp.where(index == segment_row, 1.0, 0.0).astype(bf16)


def as_column(row):
    return jnp.transpose(jnp.broadcast_to(row, (128, row.shape[1])))[:, :1]


def diagonal_bias(info):
    code, place = as_column(info[0:1]), as_column(info[2:3])
    allowed = (place == info[2:3]) | ((code == info[1:2]) & (place <= info[2:3]))
    return jnp.where(allowed, 0.0, NEGATIVE_HUGE)


def forward_kernel(qkv_ref, info_ref, out_ref, keep_ref, lse_ref, bias, acc, stat):
    slots = qkv_ref.shape[2]
    i = pl.program_id(0)
    bias[...] = diagonal_bias(info_ref[i])
    seg = segment_rows(info_ref[i, 1:2])
    qa = [jnp.concatenate([qkv_ref[i, 0, m], seg], axis=0) for m in range(slots)]
    for m in range(slots):
        s = dot(jnp.transpose(qkv_ref[i, 1, m]), qkv_ref[i, 0, m]) + bias[...]
        top = jnp.max(s, axis=0, keepdims=True)
        p = jnp.exp(s - top)
        stat[2 * m : 2 * m + 1] = top
        stat[2 * m + 1 : 2 * m + 2] = jnp.sum(p, axis=0, keepdims=True)
        acc[m] = dot(qkv_ref[i, 2, m], p.astype(bf16))

    @pl.loop(0, i)
    def _(j):
        mask = mask_rows(info_ref[j, 0:1])
        for m in range(slots):
            ka = jnp.transpose(jnp.concatenate([qkv_ref[j, 1, m], mask], axis=0))
            s = dot(ka, qa[m])
            old = stat[2 * m : 2 * m + 1]
            top = jnp.maximum(old, jnp.max(s, axis=0, keepdims=True))
            p = jnp.exp(s - top)
            factor = jnp.exp(old - top)
            stat[2 * m : 2 * m + 1] = top
            stat[2 * m + 1 : 2 * m + 2] = stat[2 * m + 1 : 2 * m + 2] * factor + jnp.sum(
                p, axis=0, keepdims=True
            )
            acc[m] = acc[m] * factor + dot(qkv_ref[j, 2, m], p.astype(bf16))

    for m in range(slots):
        total = stat[2 * m + 1 : 2 * m + 2]
        result = acc[m] / total
        out_ref[i, m] = result.astype(bf16)
        keep_ref[i, m] = result
        lse_ref[i, m : m + 1] = stat[2 * m : 2 * m + 1] + jnp.log(total)


def attention_forward(qkv, info):
    blocks, _, slots, width, rows = qkv.shape
    return pl.pallas_call(
        forward_kernel,
        grid=(blocks,),
        in_specs=[VMEM_SPEC, VMEM_SPEC],
        out_specs=[VMEM_SPEC] * 3,
        out_shape=[
            jax.ShapeDtypeStruct((blocks, slots, width, rows), bf16),
            jax.ShapeDtypeStruct((blocks, slots, width, rows), f32),
            jax.ShapeDtypeStruct((blocks, 8, rows), f32),
        ],
        scratch_shapes=[
            pltpu.VMEM((rows, rows), f32),
            pltpu.VMEM((slots, width, rows), f32),
            pltpu.VMEM((8, rows), f32),
        ],
        name="attention_forward",
    )(qkv, info)


def backward_kernel(qkv_ref, do_ref, keep_ref, lse_ref, info_ref, out_ref, bias, dq, qn, don, delta):
    blocks, _, slots = qkv_ref.shape[:3]
    j = pl.program_id(0)

    @pl.when(j == 0)
    def _():
        @pl.loop(0, blocks)
        def _(i):
            for m in range(slots):
                qn[i, m] = jnp.transpose(qkv_ref[i, 0, m])
                don[i, m] = jnp.transpose(do_ref[i, m])
                delta[i, m : m + 1] = jnp.sum(
                    do_ref[i, m].astype(f32) * keep_ref[i, m], axis=0, keepdims=True
                )
                dq[i, m] = jnp.zeros_like(dq[i, m])

    bias[...] = diagonal_bias(info_ref[j])
    mask = mask_rows(info_ref[j, 0:1])
    kn = [jnp.transpose(qkv_ref[j, 1, m]) for m in range(slots)]
    ka = [
        jnp.transpose(jnp.concatenate([qkv_ref[j, 1, m], mask], axis=0)) for m in range(slots)
    ]
    vn = [jnp.transpose(qkv_ref[j, 2, m]) for m in range(slots)]

    def tile(i, m, s):
        p = jnp.exp(s - lse_ref[i, m : m + 1])
        dp = dot(vn[m], do_ref[i, m])
        ds = (p * (dp - delta[i, m : m + 1])).astype(bf16)
        dq[i, m] += dot(qkv_ref[j, 1, m], ds)
        return dot(ds, qn[i, m]), dot(p.astype(bf16), don[i, m])

    start = []
    for m in range(slots):
        start += list(tile(j, m, dot(kn[m], qkv_ref[j, 0, m]) + bias[...]))

    def later(i, carry):
        seg = segment_rows(info_ref[i, 1:2])
        new = []
        for m in range(slots):
            qa = jnp.concatenate([qkv_ref[i, 0, m], seg], axis=0)
            a, b = tile(i, m, dot(ka[m], qa))
            new += [carry[2 * m] + a, carry[2 * m + 1] + b]
        return tuple(new)

    done = lax.fori_loop(j + 1, blocks, later, tuple(start))
    for m in range(slots):
        out_ref[j, 1, m] = jnp.transpose(done[2 * m]).astype(bf16)
        out_ref[j, 2, m] = jnp.transpose(done[2 * m + 1]).astype(bf16)

    @pl.when(j == blocks - 1)
    def _():
        @pl.loop(0, blocks)
        def _(i):
            for m in range(slots):
                out_ref[i, 0, m] = (dq[i, m] * HEAD_DIM ** (-0.5)).astype(bf16)


def attention_backward(qkv, grad, keep, lse, info):
    blocks, _, slots, width, rows = qkv.shape
    return pl.pallas_call(
        backward_kernel,
        grid=(blocks,),
        in_specs=[VMEM_SPEC] * 5,
        out_specs=VMEM_SPEC,
        out_shape=jax.ShapeDtypeStruct(qkv.shape, bf16),
        scratch_shapes=[
            pltpu.VMEM((rows, rows), f32),
            pltpu.VMEM((blocks, slots, width, rows), f32),
            pltpu.VMEM((blocks, slots, rows, width), bf16),
            pltpu.VMEM((blocks, slots, rows, width), bf16),
            pltpu.VMEM((blocks, 8, rows), f32),
        ],
        name="attention_backward",
    )(qkv, grad, keep, lse, info)


def ffn_kernel(x_ref, gf_ref, gu_ref, down_ref, part_ref, gu_grad_ref, down_grad_ref, ffn, dx):
    k = pl.program_id(0)
    half = gu_ref.shape[1] // 2
    x, gf = x_ref[...], gf_ref[...]
    both = dot(x, gu_ref[...])
    gate, up = both[:, :half], both[:, half:]
    sig = 1.0 / (1.0 + jnp.exp(-gate))
    act = gate * sig
    hidden = (act * up).astype(bf16)
    grad_hidden = dot(gf, down_ref[...], 1, 1)
    grad_gate = (grad_hidden * up * (sig * (1.0 + gate * (1.0 - sig)))).astype(bf16)
    grad_up = (grad_hidden * act).astype(bf16)
    grads = jnp.concatenate([grad_gate, grad_up], axis=1)
    ffn_now = dot(hidden, down_ref[...])
    dx_now = dot(grads, gu_ref[...], 1, 1)

    @pl.when(k == 0)
    def _():
        ffn[...] = ffn_now
        dx[...] = dx_now

    @pl.when(k > 0)
    def _():
        ffn[...] += ffn_now
        dx[...] += dx_now

    gu_grad_ref[...] = dot(x, grads, 0, 0).astype(bf16)
    down_grad_ref[...] = dot(hidden, gf, 0, 0).astype(bf16)

    @pl.when(k == pl.num_programs(0) - 1)
    def _():
        rows = part_ref.shape[2]
        for c in range(2):
            part_ref[c, 0] = dx[c * rows : (c + 1) * rows].astype(bf16)
            part_ref[c, 1] = ffn[c * rows : (c + 1) * rows].astype(bf16)


def feed_forward(x, gf, gate_up, down):
    tokens, width = x.shape
    chunks, _, columns = gate_up.shape
    hidden = columns // 2
    return pl.pallas_call(
        ffn_kernel,
        grid=(chunks,),
        in_specs=[
            pl.BlockSpec((tokens, width), lambda k: (0, 0)),
            pl.BlockSpec((tokens, width), lambda k: (0, 0)),
            pl.BlockSpec((None, width, columns), lambda k: (k, 0, 0)),
            pl.BlockSpec((None, hidden, width), lambda k: (k, 0, 0)),
        ],
        out_specs=[
            pl.BlockSpec((2, 2, tokens // 2, width), lambda k: (0, 0, 0, 0)),
            pl.BlockSpec((None, width, columns), lambda k: (k, 0, 0)),
            pl.BlockSpec((None, hidden, width), lambda k: (k, 0, 0)),
        ],
        out_shape=[
            jax.ShapeDtypeStruct((2, 2, tokens // 2, width), bf16),
            jax.ShapeDtypeStruct((chunks, width, columns), bf16),
            jax.ShapeDtypeStruct((chunks, hidden, width), bf16),
        ],
        scratch_shapes=[pltpu.VMEM((tokens, width), f32), pltpu.VMEM((tokens, width), f32)],
        name="feed_forward",
    )(x, gf, gate_up, down)


def rms_scale(rows, gain):
    return rows * lax.rsqrt(jnp.mean(rows * rows, axis=-1, keepdims=True) + EPSILON) * gain


def norm_back(rows, gain, grad):
    r = lax.rsqrt(jnp.mean(rows * rows, axis=-1, keepdims=True) + EPSILON)
    scaled = gain * grad
    back = r * scaled - rows * (r * r * r) * jnp.mean(scaled * rows, axis=-1, keepdims=True)
    return back, jnp.sum(grad * rows * r, axis=0)


def line_layout(lengths_row, positions):
    seq_ends = jnp.cumsum(lengths_row, dtype=jnp.int32)
    reached = seq_ends[None, :] <= positions[:, None]
    segment = jnp.sum(reached.astype(jnp.int32), axis=1)
    starts = jnp.max(jnp.where(reached, seq_ends[None, :], 0), axis=1)
    return segment, positions - starts, positions < seq_ends[-1]


def rotate(heads, cosines, sines):
    half = HEAD_DIM // 2
    a, b = heads[:, :half], heads[:, half:]
    return jnp.concatenate([a * cosines - b * sines, b * cosines + a * sines], axis=1)


def local(
    sizes,
    hidden_in,
    cotangent,
    destination,
    seq_lengths,
    gate_mask,
    query_weight,
    key_matrix,
    value_matrix,
    out_weight,
    gate_weight,
    up_weight,
    down_weight,
    attn_gain,
    ffn_gain,
    router_weight,
):
    rows, width = hidden_in.shape
    chips, shards = sizes["chip"], sizes["shard"]
    reps = 2 * chips
    devices = reps * shards
    per_pair = rows // devices
    slots = -(-QUERY_HEADS // reps)
    padded_heads = slots * reps
    chip, core = lax.axis_index("chip"), lax.axis_index("core")
    rep = lax.axis_index(REP)
    shard_rows = query_weight.shape[0]

    def column_slice(weight, index, count):
        size = weight.shape[1] // count
        return lax.dynamic_slice_in_dim(weight, index * size, size, 1)

    qkv_shard = jnp.concatenate([query_weight, key_matrix, value_matrix], axis=1)
    vectors = jnp.stack([attn_gain, ffn_gain, router_weight], axis=1)
    qkv_piece = jnp.concatenate(
        [column_slice(qkv_shard, rep, reps), jnp.pad(vectors, ((0, 0), (0, 5)))], axis=1
    )
    qkv_all = lax.all_gather(qkv_piece, ALL, axis=0, tiled=True)
    qkv_columns = qkv_piece.shape[1] - 8
    qkv_all = qkv_all.reshape(reps, width, qkv_columns + 8)
    full_qkv = jnp.transpose(qkv_all[:, :, :qkv_columns], (1, 0, 2)).reshape(width, -1)
    vector_rows = jnp.transpose(qkv_all[0, :, qkv_columns : qkv_columns + 3]).astype(f32)
    gain_one, gain_two, full_router = vector_rows[0], vector_rows[1], vector_rows[2]

    out_piece = column_slice(out_weight, rep, reps)
    out_all = lax.all_gather(out_piece, ALL, axis=0, tiled=True)
    out_columns = out_piece.shape[1]
    full_out = jnp.transpose(out_all.reshape(reps, width, out_columns), (1, 0, 2)).reshape(
        width, -1
    )
    gate_up_piece = jnp.concatenate(
        [column_slice(gate_weight, rep, reps), column_slice(up_weight, rep, reps)], axis=1
    )
    ff_chunk = gate_up_piece.shape[1] // 2
    gate_up = lax.all_gather(gate_up_piece, ("chip", "shard"), axis=0, tiled=True)
    gate_up = gate_up.reshape(chips, width, 2 * ff_chunk)
    down_rows = down_weight.shape[0] // reps
    down_piece = lax.dynamic_slice_in_dim(down_weight, (core * chips + chip) * down_rows, down_rows, 0)
    down = lax.all_gather(down_piece, ("shard", "chip"), axis=0, tiled=True)
    down = down.reshape(shards, ff_chunk, width)

    row_index = jnp.arange(rows, dtype=jnp.int32)
    target = destination // rows
    earlier = (target[None, :] == target[:, None]) & (row_index[None, :] < row_index[:, None])
    slot_of_row = target * per_pair + jnp.sum(earlier.astype(jnp.int32), axis=1)
    to_slot = slot_of_row[None, :] == row_index[:, None]
    to_slot_b = to_slot.astype(bf16)
    place_sent = jnp.sum(jnp.where(to_slot, (destination % rows)[None, :], 0), axis=1)
    place_sent = jnp.pad(place_sent.reshape(devices, 1, per_pair), ((0, 0), (0, 0), (0, 128 - per_pair)))
    sent_hidden = jnp.dot(to_slot_b, hidden_in, preferred_element_type=f32).astype(bf16)
    sent_grad = jnp.dot(to_slot_b, cotangent, preferred_element_type=f32).astype(bf16)
    got_hidden, got_place = exchange(
        1,
        sizes,
        [
            (sent_hidden.reshape(devices, per_pair, width), ALL, False),
            (place_sent, ALL, False),
        ],
    )
    got_grad = lax.all_to_all(
        sent_grad.reshape(devices, per_pair, width), ALL, split_axis=0, concat_axis=0, tiled=True
    )
    hidden = got_hidden.reshape(rows, width)
    place = got_place[:, 0, :per_pair].reshape(rows)

    positions = rep * rows + place
    segment, within, is_valid = line_layout(seq_lengths[0], positions)
    gate_here = jnp.sum(jnp.where(place[:, None] == row_index[None, :], gate_mask[None, :], 0), axis=1)
    active = is_valid & (gate_here == 1)
    key_code = jnp.where(active, segment, -1)
    active_f = active.astype(f32)

    hidden_f = hidden.astype(f32)
    first_normalized = rms_scale(hidden_f, gain_one).astype(bf16)
    router_logit = jnp.sum(hidden_f * full_router, axis=1)
    gate_value = jax.nn.sigmoid(router_logit)
    branch_scale = active_f * gate_value

    steps = jnp.arange(HEAD_DIM // 2).astype(f32)
    frequency = jnp.power(ROPE_BASE, -2.0 * steps / HEAD_DIM)
    angles = frequency[:, None] * within.astype(f32)[None, :]
    cosines, sines = jnp.cos(angles), jnp.sin(angles)
    qkv_t = jnp.einsum("te,ed->dt", first_normalized, full_qkv, preferred_element_type=f32)
    qkv_t = qkv_t.reshape(QUERY_HEADS + 2 * KEY_VALUE_HEADS, HEAD_DIM, rows)
    rotated = rotate(qkv_t[: QUERY_HEADS + KEY_VALUE_HEADS], cosines, sines).astype(bf16)
    query = rotated[:QUERY_HEADS] * jnp.asarray(HEAD_DIM ** (-0.5), bf16)
    key_t = jnp.repeat(rotated[QUERY_HEADS:], GROUP, axis=0)
    value_t = jnp.repeat(qkv_t[QUERY_HEADS + KEY_VALUE_HEADS :].astype(bf16), GROUP, axis=0)

    def by_owner(heads):
        heads = jnp.pad(heads, ((0, padded_heads - QUERY_HEADS), (0, 0), (0, 0)))
        return heads.reshape(reps, slots, HEAD_DIM, rows)

    qkv_sent = jnp.stack([by_owner(query), by_owner(key_t), by_owner(value_t)], axis=1)
    info = jnp.pad(jnp.stack([key_code, segment, place]), ((0, 5), (0, 0)))
    qkv_got, info_got = exchange(2, sizes, [(qkv_sent, REP, False), (info, REP, True)])
    att_out, att_keep, lse = attention_forward(qkv_got, info_got)
    (att_home,) = exchange(3, sizes, [(att_out, REP, False)])
    attn_out_t = att_home.reshape(padded_heads * HEAD_DIM, rows)[:width]

    attn_branch = jnp.einsum("dt,de->te", attn_out_t, full_out, preferred_element_type=f32)
    middle = hidden_f + attn_branch
    normed_two = rms_scale(middle, gain_two).astype(bf16)
    grad_out = got_grad.reshape(rows, width).astype(f32)
    grad_branch = branch_scale[:, None] * grad_out
    grad_ffn = grad_branch.astype(bf16)
    x_pair, gf_pair = exchange(
        4, sizes, [(normed_two, ("core",), True), (grad_ffn, ("core",), True)]
    )
    parts, gate_up_grad, down_grad = feed_forward(
        x_pair.reshape(2 * rows, width), gf_pair.reshape(2 * rows, width), gate_up, down
    )
    (parts_got,) = exchange(5, sizes, [(parts, ("core",), False)])
    grad_normed_two = parts_got[0, 0].astype(f32) + parts_got[1, 0].astype(f32)
    ffn_branch = parts_got[0, 1].astype(f32) + parts_got[1, 1].astype(f32)

    gate_up_sum = lax.psum_scatter(
        gate_up_grad.reshape(chips * shards, shard_rows, 2 * ff_chunk),
        ("chip", "shard"),
        scatter_dimension=0,
        tiled=True,
    )
    down_sum = lax.psum_scatter(
        down_grad.reshape(shards * chips, down_rows, width),
        ("shard", "chip"),
        scatter_dimension=0,
        tiled=True,
    )
    gate_up_total = lax.all_gather(gate_up_sum, REP, axis=0, tiled=True)
    down_total = lax.all_gather(down_sum, ("core", "chip"), axis=0, tiled=True)

    branch_sum = attn_branch + ffn_branch
    result = (hidden_f + branch_scale[:, None] * branch_sum).astype(bf16)
    home_out = lax.all_to_all(
        result.reshape(devices, per_pair, width), ALL, split_axis=0, concat_axis=0, tiled=True
    )
    grad_logit = active_f * jnp.sum(grad_out * branch_sum, axis=1) * gate_value * (1.0 - gate_value)
    grad_middle, grad_gain_ffn = norm_back(middle, gain_two, grad_normed_two)
    grad_attn = (grad_branch + grad_middle).astype(bf16)
    grad_attention_t = jnp.einsum("te,de->dt", grad_attn, full_out, preferred_element_type=f32)
    grad_attention_t = grad_attention_t.astype(bf16).reshape(QUERY_HEADS, HEAD_DIM, rows)
    (grad_got,) = exchange(6, sizes, [(by_owner(grad_attention_t), REP, False)])
    grads_sent = attention_backward(qkv_got, grad_got, att_keep, lse, info_got)
    (grads_home,) = exchange(7, sizes, [(grads_sent, REP, False)])
    grads_home = jnp.transpose(grads_home, (1, 0, 2, 3, 4)).reshape(3, padded_heads, HEAD_DIM, rows)
    grads_home = grads_home[:, :QUERY_HEADS].astype(f32)
    grouped = grads_home[1:].reshape(2, KEY_VALUE_HEADS, GROUP, HEAD_DIM, rows).sum(axis=2)
    back = rotate(jnp.concatenate([grads_home[0], grouped[0]], axis=0), cosines, -sines)
    qkv_grad_t = jnp.concatenate([back, grouped[1]], axis=0).astype(bf16).reshape(-1, rows)
    grad_normed_one = jnp.einsum("ct,ec->te", qkv_grad_t, full_qkv, preferred_element_type=f32)
    grad_norm_x, grad_gain_attn = norm_back(hidden_f, gain_one, grad_normed_one)
    grad_hidden = grad_out + grad_middle + grad_norm_x + grad_logit[:, None] * full_router
    home_grad = lax.all_to_all(
        grad_hidden.astype(bf16).reshape(devices, per_pair, width),
        ALL,
        split_axis=0,
        concat_axis=0,
        tiled=True,
    )

    qkv_grad = jnp.einsum("te,ct->ec", first_normalized, qkv_grad_t, preferred_element_type=f32)
    out_grad = jnp.einsum("dt,te->de", attn_out_t, grad_attn, preferred_element_type=f32)
    router_grad = jnp.sum(grad_logit[:, None] * hidden_f, axis=0)

    def by_columns(grad, columns):
        return jnp.transpose(grad.astype(bf16).reshape(width, reps, columns), (1, 0, 2))

    vector_grads = jnp.stack([grad_gain_attn, grad_gain_ffn, router_grad], axis=1).astype(bf16)
    vector_grads = jnp.pad(vector_grads[None], ((0, reps - 1), (0, 0), (0, 5)))
    proj_grad = jnp.concatenate(
        [by_columns(qkv_grad, qkv_columns), by_columns(out_grad, out_columns), vector_grads], axis=2
    )
    proj_sum = lax.psum_scatter(
        proj_grad.reshape(devices, shard_rows, -1), ALL, scatter_dimension=0, tiled=True
    )
    proj_total = lax.all_gather(proj_sum, REP, axis=0, tiled=True)
    proj_total = proj_total.reshape(reps, shard_rows, -1).astype(f32)

    def joined(piece):
        return jnp.transpose(piece, (1, 0, 2)).reshape(shard_rows, -1)

    qkv_total = joined(proj_total[:, :, :qkv_columns])
    out_total = joined(proj_total[:, :, qkv_columns : qkv_columns + out_columns])
    vector_total = jnp.transpose(proj_total[0, :, qkv_columns + out_columns :])
    gate_up_total = gate_up_total.reshape(reps, shard_rows, 2 * ff_chunk).astype(f32)
    q_end, k_end = query_weight.shape[1], query_weight.shape[1] + key_matrix.shape[1]

    def home_rows(home):
        return jnp.dot(
            to_slot_b.T, home.reshape(rows, width), preferred_element_type=f32
        ).astype(bf16)

    return (
        home_rows(home_out),
        home_rows(home_grad),
        qkv_total[:, :q_end],
        qkv_total[:, q_end:k_end],
        qkv_total[:, k_end:],
        out_total,
        joined(gate_up_total[:, :, :ff_chunk]),
        joined(gate_up_total[:, :, ff_chunk:]),
        down_total.reshape(-1, width).astype(f32),
        vector_total[0],
        vector_total[1],
        vector_total[2],
    )


def solution(mesh):
    reps, shards = mesh.shape["rep"], mesh.shape["shard"]
    sizes = {"chip": reps // 2, "core": 2, "shard": shards}
    split_mesh = Mesh(mesh.devices.reshape(reps // 2, 2, shards), ALL)
    tokens, tokens_1d = P(ALL, None), P(ALL)
    weight, vector = P("shard", None), P("shard")
    return jax.shard_map(
        functools.partial(local, sizes),
        mesh=split_mesh,
        in_specs=(tokens, tokens, tokens_1d, weight, tokens_1d) + (weight,) * 7 + (vector,) * 3,
        out_specs=(tokens, tokens) + (weight,) * 7 + (vector,) * 3,
        check_vma=False,
    )
```

time: 1570 us -> 1020 us (0.65)
  matrix products: 491 us -> 27.1 us
  Pallas kernels: 0 us -> 385 us
  waiting for transfers between devices: 589 us -> 418 us
  blocking collectives: 118 us -> 0 us
  other arithmetic: 130 us -> 41.1 us
  local copies, waits for them, and re-layouts: 175 us -> 108 us
  loops' own time: 16.9 us -> 0 us
    dot_general x78 -> x10, matrix products: 491 us -> 27.1 us  [the longest x1 5.89 us: local(): jnp.einsum('te,ed->dt', first_normalized, full_qkv, preferred_element_typ...]
    pallas_call x0 -> x10, Pallas kernels: none -> 385 us  [the longest x7 220 us: exchange(): pl.pallas_call(functools.partial(exchange_kernel, specs, sizes), out_shap...]
    unnamed x20 -> x10, waiting for transfers between devices: 97.8 us -> 1.5 us
    dynamic_update_slice x16 -> x0, local copies, waits for them, and re-layouts: 71.1 us -> none  [the longest x8 35.6 us: both_one_block(): lax.dynamic_update_slice_in_dim(value_all, lax.dynamic_slice_in_dim(value...]
    reduce_sum x10 -> x7, other arithmetic: 77.3 us -> 8.89 us  [the longest x1 3.86 us: norm_back(): return (back, jnp.sum(grad * rows * r, axis=0))]
    unnamed x2 -> x0, blocking collectives: 57.7 us -> none
    psum x1 -> x0, waiting for transfers between devices: 51.1 us -> none  [local(): lax.psum(group_sums[0].astype(jnp.bfloat16), 'rep').astype(jnp.float32)]
    reduce_scatter x6 -> x3, waiting for transfers between devices: 352 us -> 303 us  [the longest x1 157 us: local(): lax.psum_scatter(proj_grad.reshape(devices, shard_rows, -1), ALL, scatter...]
  transfers between devices with their start and end apart: 22 -> 13, of which waited for: 11 -> 7; matrix products, arithmetic and copies ran while one was open for 23% -> 15% of each run, Pallas kernels for 0% -> 33%
where the time goes in v1:
time: 1020 us; the launch traced here: 1010 us
  waiting for transfers between devices  418 us (41%)
  Pallas kernels  385 us (38%)
  local copies, waits for them, and re-layouts  108 us (11%)
  other arithmetic  41.1 us (4%)
  matrix products  27.1 us (3%)
  starting transfers between devices  16.4 us (2%)
  between operations  15.1 us (1%)
    pallas_call x7, Pallas kernels, exchange(): pl.pallas_call(functools.partial(exchange_kernel, specs, sizes), out_shap...  220 us
    reduce_scatter x1, waiting for transfers between devices, local(): lax.psum_scatter(proj_grad.reshape(devices, shard_rows, -1), ALL, scatter...  157 us
    reduce_scatter x1, waiting for transfers between devices, local(): lax.psum_scatter(gate_up_grad.reshape(chips * shards, shard_rows, 2 * ff_...  146 us
    pallas_call x1, Pallas kernels, attention_backward(): pl.pallas_call(backward_kernel, grid=(blocks,), in_specs=[VMEM_SPEC] * 5,...  74 us
    pallas_call x1, Pallas kernels, attention_forward(): pl.pallas_call(forward_kernel, grid=(blocks,), in_specs=[VMEM_SPEC, VMEM_...  48.3 us
    all_gather x1, waiting for transfers between devices, local(): qkv_all = lax.all_gather(qkv_piece, ALL, axis=0, tiled=True)  43.1 us
    pallas_call x1, Pallas kernels, feed_forward(): pl.pallas_call(ffn_kernel, grid=(chunks,), in_specs=[pl.BlockSpec((tokens...  42.5 us
    all_gather x1, waiting for transfers between devices, local(): gate_up_total = lax.all_gather(gate_up_sum, REP, axis=0, tiled=True)  23.2 us
  transfers between devices with their start and end apart: 13, of which 7 were waited for; matrix products, arithmetic and copies ran while one was open for 15% of the time, Pallas kernels for 33%

profile of v1, /device:TPU:0, one launch (start us, length us, event | category | flops | bytes accessed | tf_op | source)
XLA Modules:
  0.0 1010.9 jit_solution(10192785235435517591)
XLA Ops:
  18.7 8.3 all-to-all-start
  31.0 57.3 %exchange_1.1 = (bf16[32,16,960]{2,1,0:T(8,128)(2,1)}, s32[32,1,128]{2,1,0:T(1,128)}) custom-call(bf16[32,16,960]{2,1,0:T(8,128)(2,1)} %bitcast.181, s32[32,1,128]{2,1,0:T(1,128)} %pad.29.refs_1_), custom_call_target="tpu_custom_call" | custom-call | tf_op jit(solution)/shard_map/exchange_1/pallas_call | solution.py:108
  91.0 3.9 copy.181
  94.9 43.1 %all-gather.21.cloned.1.call-done = bf16[32,240,208]{1,2,0:T(8,128)(2,1)} async-done(((bf16[1,240,208]{1,2,0:T(8,128)(2,1)}), bf16[32,240,208]{1,2,0:T(8,128)(2,1)}) %all-gather.21.cloned.1.call-update) | async-done | bytes 3194896 | tf_op jit(solution)/shard_map/all_gather | solution.py:402
  137.9 4.9 copy.178
  142.8 8.5 reshape.477
  160.2 5.9 fusion.56
  172.4 52.1 %exchange_2.1 = (bf16[8,3,2,64,512]{4,3,2,1,0:T(8,128)(2,1)}, s32[8,8,512]{2,1,0:T(8,128)}) custom-call(bf16[8,3,2,64,512]{4,3,2,1,0:T(8,128)(2,1)} %pad_maximum_fusion.1.refs_0_, s32[8,512]{1,0:T(8,128)} %pad.34.refs_1_), custom_call_target="tpu_custom_call" | custom-call | tf_op jit(solution)/shard_map/exchange_2/pallas_call | solution.py:108
  224.6 48.3 %attention_forward.1 = (bf16[8,2,64,512]{3,2,1,0:T(8,128)(2,1)}, f32[8,2,64,512]{3,2,1,0:T(8,128)}, f32[8,8,512]{2,1,0:T(8,128)}) custom-call(bf16[8,3,2,64,512]{4,3,2,1,0:T(8,128)(2,1)} %get-tuple-element.26.qkv_ref, s32[8,8,512]{2,1,0:T(8,128)} %get-tuple-element.27.info_ref), custom_call_target="tpu_custom_call" | custom-call | tf_op jit(solution)/shard_map/attention_forward/pallas_call | solution.py:179
  272.9 22.3 %exchange_3.1 = bf16[8,2,64,512]{3,2,1,0:T(8,128)(2,1)} custom-call(bf16[8,2,64,512]{3,2,1,0:T(8,128)(2,1)} %get-tuple-element.28.refs_0_), custom_call_target="tpu_custom_call" | custom-call | tf_op jit(solution)/shard_map/exchange_3/pallas_call | solution.py:108
  302.4 8.6 exchange_4.1
  311.0 6.6 all-gather.11.cloned.1.call-done
  317.7 42.5 %feed_forward.1 = (bf16[2,2,512,960]{3,2,1,0:T(8,128)(2,1)}, bf16[4,960,640]{2,1,0:T(8,128)(2,1)}, bf16[4,320,960]{2,1,0:T(8,128)(2,1)}) custom-call(bf16[1024,960]{1,0:T(8,128)(2,1)} %bitcast.194, bf16[1024,960]{1,0:T(8,128)(2,1)} %bitcast.195, bf16[4,960,640]{2,1,0:T(8,128)(2,1)} %bitcast.179, bf16[4,320,960]{2,1,0:T(8,128)(2,1)} %bitcast.193), custom_call_target="tpu_custom_call" | custom-call | tf_op jit(solution)/shard_map/feed_forward/pallas_call | solution.py:315
  360.2 8.4 exchange_5.1
  368.7 3.9 fusion.8
  373.0 4.7 fusion.2
  380.2 29.9 %exchange_6.1.do_ref = bf16[8,2,64,512]{3,2,1,0:T(8,128)(2,1)} custom-call(bf16[8,2,64,512]{3,2,1,0:T(8,128)(2,1)} %bitcast.182), custom_call_target="tpu_custom_call" | custom-call | tf_op jit(solution)/shard_map/exchange_6/pallas_call | solution.py:108
  410.1 74.0 %attention_backward.1.refs_0_ = bf16[8,3,2,64,512]{4,3,2,1,0:T(8,128)(2,1)} custom-call(bf16[8,3,2,64,512]{4,3,2,1,0:T(8,128)(2,1)} %get-tuple-element.26.qkv_ref, bf16[8,2,64,512]{3,2,1,0:T(8,128)(2,1)} %exchange_6.1.do_ref, f32[8,2,64,512]{3,2,1,0:T(8,128)} %get-tuple-element.32.keep_ref, f32[8,8,512]{2,1,0:T(8,128)} %get-tuple-element.33.lse_ref, ...), custom_call_target="tpu_custom_call" | custom-call | tf_op jit(solution)/shard_map/attention_backward/pallas_call | solution.py:257
  484.1 41.1 %exchange_7.1 = bf16[8,3,2,64,512]{4,3,2,1,0:T(8,128)(2,1)} custom-call(bf16[8,3,2,64,512]{4,3,2,1,0:T(8,128)(2,1)} %attention_backward.1.refs_0_), custom_call_target="tpu_custom_call" | custom-call | tf_op jit(solution)/shard_map/exchange_7/pallas_call | solution.py:108
  545.8 3.9 convolution_convert_fusion
  549.7 5.4 copy.188
  558.1 3.8 pad_maximum_fusion
  561.9 5.4 copy.193
  567.2 11.0 %reshape.499 = bf16[32,240,328]{1,0,2:T(8,128)(2,1)} reshape(bf16[8,960,328]{1,0,2:T(8,128)(2,1)} %copy.193) | data formatting | bytes 10076160 | tf_op jit(solution)/shard_map/reshape | solution.py:558
  578.2 7.9 copy.194
  587.7 156.6 %reduce-scatter.4.cloned.1.call-done = bf16[1,240,328]{1,2,0:T(8,128)(2,1)} async-done(((bf16[32,240,328]{1,2,0:T(8,128)(2,1)}), bf16[1,240,328]{1,2,0:T(8,128)(2,1)}) %reduce-scatter.4.cloned.1.call-update) | async-done | bytes 157456 | tf_op jit(solution)/shard_map/reduce_scatter | solution.py:557
  748.0 146.1 %reduce-scatter.6.cloned.1.call-done = bf16[1,240,640]{2,1,0:T(8,128)(2,1)} async-done(((bf16[16,240,640]{2,1,0:T(8,128)(2,1)}), bf16[1,240,640]{2,1,0:T(8,128)(2,1)}) %reduce-scatter.6.cloned.1.call-update) | async-done | bytes 307216 | tf_op jit(solution)/shard_map/reduce_scatter | solution.py:501
  894.2 4.2 fusion.5
  898.3 3.8 all-to-all-start.2
  905.2 21.9 %all-to-all-done.2 = bf16[32,16,960]{2,1,0:T(8,128)(2,1)S(1)} async-done(((bf16[32,16,960]{2,1,0:T(8,128)(2,1)}), bf16[32,16,960]{2,1,0:T(8,128)(2,1)S(1)}, u32[]{:S(2)}, u32[]{:S(2)}) %all-to-all-start.2) | async-done | bytes 983072 | tf_op jit(solution)/shard_map/all_to_all | solution.py:537
  935.1 18.9 %all-gather.15.cloned.1.call-done = bf16[8,240,328]{1,2,0:T(8,128)(2,1)} async-done(((bf16[1,240,328]{1,2,0:T(8,128)(2,1)}), bf16[8,240,328]{1,2,0:T(8,128)(2,1)}) %all-gather.15.cloned.1.call-update) | async-done | bytes 1259536 | tf_op jit(solution)/shard_map/all_gather | solution.py:560
  961.9 23.2 %all-gather.17.cloned.1.call-done = bf16[8,240,640]{2,1,0:T(8,128)(2,1)} async-done(((bf16[1,240,640]{2,1,0:T(8,128)(2,1)}), bf16[8,240,640]{2,1,0:T(8,128)(2,1)}) %all-gather.17.cloned.1.call-update) | async-done | bytes 2457616 | tf_op jit(solution)/shard_map/all_gather | solution.py:513
  (168 shorter events, 109.2 us)
Async XLA Ops:
  7.2 6.0 copy-start
  7.2 83.8 %all-gather.9.cloned.1.call-start = ((), (), s32[]{:S(2)}) async-start(), calls=%async_computation.6 | async-start | bytes 2027520 | tf_op jit(solution)/shard_map/all_gather | solution.py:410
  9.0 129.0 %all-gather.21.cloned.1.call-start = ((), (), s32[]{:S(2)}) async-start(), calls=%async_computation.15 | async-start | bytes 3514368 | tf_op jit(solution)/shard_map/all_gather | solution.py:402
  12.2 4.1 copy-start.12
  12.3 4.4 copy-start.14
  13.1 297.9 %all-gather.13.cloned.1.call-start = ((), (), s32[]{:S(2)}) async-start(), calls=%async_computation.8 | async-start | bytes 2785280 | tf_op jit(solution)/shard_map/all_gather | solution.py:423
  14.2 303.5 %all-gather.11.cloned.1.call-start = ((), (), s32[]{:S(2)}) async-start(), calls=%async_computation.7 | async-start | bytes 5222400 | tf_op jit(solution)/shard_map/all_gather | solution.py:419
  17.4 9.9 copy-start.16
  17.4 11.6 %copy-start.15 = (bf16[512,960]{0,1:T(8,128)(2,1)S(1)}, bf16[512,960]{0,1:T(8,128)(2,1)}, u32[]{:S(2)}) copy-start(bf16[512,960]{0,1:T(8,128)(2,1)} %param.15) | copy-start | bytes 2949124
  18.7 279.8 %all-to-all-start = ((bf16[32,16,960]{2,1,0:T(8,128)(2,1)}), bf16[32,16,960]{2,1,0:T(8,128)(2,1)}, u32[]{:S(2)}, u32[]{:S(2)}) async-start(bf16[32,16,960]{2,1,0:T(8,128)(2,1)} %bitcast.27), calls=%async_computation | async-start | bytes 2097152 | tf_op jit(solution)/shard_map/all_to_all | solution.py:444
  27.1 559.9 %reduce-scatter.8.cloned.1.call-start = ((), (), s32[]{:S(2)}) async-start(), calls=%async_computation.13 | async-start | bytes 2785280 | tf_op jit(solution)/shard_map/reduce_scatter | solution.py:507
  29.7 59.6 %copy-start.13 = (s32[512]{0:T(512)S(1)}, s32[512]{0:T(512)}, u32[]{:S(2)}) copy-start(s32[512]{0:T(512)} %param.19) | copy-start | bytes 6148
  153.6 4.4 copy-start.2
  160.2 5.9 copy-start.9
  167.4 1.7 slice-start
  368.7 375.6 %reduce-scatter.4.cloned.1.call-start = ((), (), s32[]{:S(2)}) async-start(), calls=%async_computation.9 | async-start | bytes 5541888 | tf_op jit(solution)/shard_map/reduce_scatter | solution.py:557
  373.0 4.7 copy-start.8
  377.8 1.4 copy-start.11
  528.3 3.7 copy-start.3
  540.3 1.9 copy-start.7
  542.2 3.6 copy-start.10
  555.2 2.9 copy-start.4
  586.1 308.0 %reduce-scatter.6.cloned.1.call-start = ((), (), s32[]{:S(2)}) async-start(), calls=%async_computation.11 | async-start | bytes 5222400 | tf_op jit(solution)/shard_map/reduce_scatter | solution.py:501
  586.9 341.9 %all-gather.19.cloned.1.call-start = ((), (), s32[]{:S(2)}) async-start(), calls=%async_computation.14 | async-start | bytes 1474560 | tf_op jit(solution)/shard_map/all_gather | solution.py:514
  587.6 366.4 %all-gather.15.cloned.1.call-start = ((), (), s32[]{:S(2)}) async-start(), calls=%async_computation.10 | async-start | bytes 1511424 | tf_op jit(solution)/shard_map/all_gather | solution.py:560
  744.3 154.0 %all-to-all-start.1 = ((bf16[32,16,960]{2,1,0:T(8,128)(2,1)}), bf16[32,16,960]{2,1,0:T(8,128)(2,1)}, u32[]{:S(2)}, u32[]{:S(2)}) async-start(bf16[32,16,960]{2,1,0:T(8,128)(2,1)} %bitcast.186), calls=%async_computation.1 | async-start | bytes 2097152 | tf_op jit(solution)/shard_map/all_to_all | solution.py:518
  748.0 237.1 %all-gather.17.cloned.1.call-start = ((), (), s32[]{:S(2)}) async-start(), calls=%async_computation.12 | async-start | bytes 2764800 | tf_op jit(solution)/shard_map/all_gather | solution.py:513
  898.3 28.7 %all-to-all-start.2 = ((bf16[32,16,960]{2,1,0:T(8,128)(2,1)}), bf16[32,16,960]{2,1,0:T(8,128)(2,1)S(1)}, u32[]{:S(2)}, u32[]{:S(2)}) async-start(bf16[32,16,960]{2,1,0:T(8,128)(2,1)} %bitcast.180), calls=%async_computation.2 | async-start | bytes 2097152 | tf_op jit(solution)/shard_map/all_to_all | solution.py:537
  954.0 2.5 copy-start.5
  956.6 1.2 copy-start.6
  1000.5 3.3 copy-start.1
Sparse Core Ops, SparseCore 0:
  11.4 63.8 all-gather.8
  78.7 59.1 all-gather.20
  141.2 79.6 all-gather.12
  224.1 93.5 all-gather.10
  368.8 87.5 reduce-scatter.7
  586.3 157.9 reduce-scatter.3
  749.5 144.5 reduce-scatter.5
  896.0 31.9 all-gather.18
  929.8 24.1 all-gather.14
  955.7 29.2 all-gather.16

commit v2 on v1

v2 whole, which is shorter than its diff:
```python
import functools

import jax
import jax.numpy as jnp
from jax import lax
from jax.experimental import pallas as pl
from jax.experimental.pallas import tpu as pltpu
from jax.sharding import Mesh
from jax.sharding import PartitionSpec as P

QUERY_HEADS = 15
KEY_VALUE_HEADS = 5
HEAD_DIM = 64
GROUP = QUERY_HEADS // KEY_VALUE_HEADS
EPSILON = 1e-05
NEGATIVE_HUGE = -1e30
ROPE_BASE = 10000.0
FF_CHUNK = 256
bf16 = jnp.bfloat16
f32 = jnp.float32
MESH = pl.DeviceIdType.MESH
REP = ("chip", "core")
ALL = ("chip", "core", "shard")
VMEM_SPEC = pl.BlockSpec(memory_space=pltpu.VMEM)
HBM_SPEC = pl.BlockSpec(memory_space=pl.ANY)


def dot(a, b, ca=1, cb=0):
    return lax.dot_general(a, b, (((ca,), (cb,)), ((), ())), preferred_element_type=f32)


def axes_size(sizes, axes):
    total = 1
    for name in axes:
        total *= sizes[name]
    return total


def peer_coords(index, axes, sizes):
    coords = {}
    for name in reversed(axes):
        coords[name] = lax.rem(index, sizes[name])
        index = index // sizes[name]
    return coords


def remote(src, dst, send_sem, recv_sem, coords):
    return pltpu.make_async_remote_copy(
        src_ref=src,
        dst_ref=dst,
        send_sem=send_sem,
        recv_sem=recv_sem,
        device_id=coords,
        device_id_type=MESH,
    )


def each(start, stop, body):
    def step(k, carry):
        body(k)
        return carry

    lax.fori_loop(start, stop, step, 0)


class Item:
    late = False
    aliased = False

    def start(self, ins, outs, scratch):
        pass

    def middle(self, ins, outs, scratch):
        pass

    def finish(self, ins, outs, scratch):
        pass


class AllToAll(Item):
    def __init__(self, sizes, array, axes, spread=False, late=False, source=None):
        self.sizes, self.axes, self.spread, self.late = sizes, axes, spread, late
        self.count = axes_size(sizes, axes)
        self.source = source
        self.inputs = [] if source is not None else [array]
        shape = (self.count,) + tuple(array.shape) if spread else tuple(array.shape)
        self.in_specs = [VMEM_SPEC] * len(self.inputs)
        self.out_shapes = [jax.ShapeDtypeStruct(shape, array.dtype)]
        self.out_specs = [VMEM_SPEC]
        self.scratch = [
            pltpu.SemaphoreType.DMA((self.count,)),
            pltpu.SemaphoreType.DMA((self.count,)),
        ]

    def copy(self, k, ins, outs, scratch):
        me = lax.axis_index(self.axes)
        peer = lax.rem(me + k, self.count)
        return remote(
            ins[0] if self.spread else ins[0].at[peer],
            outs[0].at[me],
            scratch[0].at[k],
            scratch[1].at[k],
            peer_coords(peer, self.axes, self.sizes),
        )

    def start(self, ins, outs, scratch):
        each(1, self.count, lambda k: self.copy(k, ins, outs, scratch).start())
        me = lax.axis_index(self.axes)
        outs[0][me] = ins[0][...] if self.spread else ins[0][me]

    def finish(self, ins, outs, scratch):
        each(1, self.count, lambda k: self.copy(k, ins, outs, scratch).wait())


class Scatter(Item):
    def __init__(self, sizes, array, axes, dim, half=False, late=False, source=None):
        self.sizes, self.axes, self.dim = sizes, axes, dim
        self.half, self.late, self.source = half, late, source
        self.count = axes_size(sizes, axes)
        self.slots = self.count // 2
        piece = tuple(array.shape[:dim]) + tuple(array.shape[dim + 1 :])
        self.inputs = [] if source is not None else [array]
        self.in_specs = [HBM_SPEC] * len(self.inputs)
        self.out_shapes = [jax.ShapeDtypeStruct((self.count - 1,) + piece, array.dtype)]
        self.out_specs = [HBM_SPEC]
        self.scratch = [
            pltpu.SemaphoreType.DMA((self.count,)),
            pltpu.SemaphoreType.DMA((self.count,)),
        ]

    def guarded(self, index, body):
        if self.half:
            pl.when(index // self.slots == lax.axis_index("core"))(body)
        else:
            body()

    def copy(self, k, ins, outs, scratch):
        me = lax.axis_index(self.axes)
        peer = lax.rem(me + k, self.count)
        index = lax.rem(peer, self.slots) if self.half else peer
        src = ins[0].at[index] if self.dim == 0 else ins[0].at[:, index]
        return peer, remote(
            src,
            outs[0].at[k - 1],
            scratch[0].at[k],
            scratch[1].at[k],
            peer_coords(peer, self.axes, self.sizes),
        )

    def start(self, ins, outs, scratch):
        def send(k):
            peer, copy = self.copy(k, ins, outs, scratch)
            self.guarded(peer, copy.start)

        each(1, self.count, send)

    def finish(self, ins, outs, scratch):
        def receive(k):
            self.copy(k, ins, outs, scratch)[1].wait_recv()

        def sent(k):
            peer, copy = self.copy(k, ins, outs, scratch)
            self.guarded(peer, copy.wait_send)

        me = lax.axis_index(self.axes)
        self.guarded(me, lambda: each(1, self.count, receive))
        each(1, self.count, sent)


class SpreadHalf(Item):
    def __init__(self, sizes, array):
        self.sizes, self.count = sizes, axes_size(sizes, REP)
        self.slots = sizes["shard"] // 2
        self.inputs, self.in_specs = [array], [VMEM_SPEC]
        shape = (sizes["chip"],) + tuple(array.shape)
        self.out_shapes = [jax.ShapeDtypeStruct(shape, array.dtype)]
        self.out_specs = [VMEM_SPEC]
        self.scratch = [
            pltpu.SemaphoreType.DMA((self.count,)),
            pltpu.SemaphoreType.DMA((self.count,)),
        ]

    def owner(self):
        return lax.axis_index("shard") // self.slots

    def copy(self, k, ins, outs, scratch, sending):
        me = lax.axis_index(REP)
        peer = lax.rem(me + k, self.count) if sending else lax.rem(me + self.count - k, self.count)
        chip = lax.axis_index("chip") if sending else peer // 2
        return peer, remote(
            ins[0],
            outs[0].at[chip],
            scratch[0].at[k],
            scratch[1].at[k],
            peer_coords(peer, REP, self.sizes),
        )

    def start(self, ins, outs, scratch):
        @pl.when(lax.axis_index("core") == self.owner())
        def _():
            each(1, self.count, lambda k: self.copy(k, ins, outs, scratch, True)[1].start())
            outs[0][lax.axis_index("chip")] = ins[0][...]

    def finish(self, ins, outs, scratch):
        def receive(k):
            peer, copy = self.copy(k, ins, outs, scratch, False)
            pl.when(lax.rem(peer, 2) == self.owner())(copy.wait_recv)

        each(1, self.count, receive)

        @pl.when(lax.axis_index("core") == self.owner())
        def _():
            each(1, self.count, lambda k: self.copy(k, ins, outs, scratch, True)[1].wait_send())


class Gather(Item):
    def __init__(self, sizes, array, split_axes, stages, half=False):
        self.sizes, self.split_axes, self.stages, self.half = sizes, split_axes, stages, half
        self.shards = sizes["shard"]
        self.slots = self.shards // 2 if half else self.shards
        self.split = axes_size(sizes, split_axes)
        both = stages == "both"
        self.inputs = [array]
        self.in_specs = [VMEM_SPEC if both else HBM_SPEC]
        if stages == "plane":
            shape, self.aliased = tuple(array.shape), True
        else:
            shape = (self.slots,) + tuple(array.shape)
        self.out_shapes = [jax.ShapeDtypeStruct(shape, array.dtype)]
        self.out_specs = [VMEM_SPEC if both else HBM_SPEC]
        dma = pltpu.SemaphoreType.DMA
        self.scratch = []
        if stages != "plane":
            self.scratch += [dma((self.shards,)), dma((self.shards,))]
        if stages == "z":
            self.scratch += [pltpu.VMEM(array.shape, array.dtype), dma((2,))]
        if stages != "z":
            self.scratch += [dma((self.split, self.shards)), dma((self.split, self.shards))]

    def valid(self, z):
        if not self.half:
            return None
        return z // self.slots == lax.axis_index("core")

    def guarded(self, z, body):
        ok = self.valid(z)
        if ok is None:
            body()
        else:
            pl.when(ok)(body)

    def slot(self, z):
        return lax.rem(z, self.slots) if self.half else z

    def z_copy(self, k, src, full, scratch, sending):
        me = lax.axis_index("shard")
        mine = lax.axis_index(self.split_axes)
        peer = lax.rem(me + k, self.shards) if sending else lax.rem(me + self.shards - k, self.shards)
        source = me if sending else peer
        dst = full.at[self.slot(source), mine]
        return remote(
            src.at[mine] if sending else dst,
            dst,
            scratch[0].at[k],
            scratch[1].at[k],
            {"shard": peer},
        )

    def start(self, ins, outs, scratch):
        me = lax.axis_index("shard")
        if self.stages == "plane":
            self.plane_start(outs[0], scratch)
            return
        src, full = ins[0], outs[0]

        def send():
            each(1, self.shards, lambda k: self.z_copy(k, src, full, scratch, True).start())

        self.guarded(me, send)
        if self.stages == "both":
            full[me] = src[...]
        else:

            def load():
                pltpu.make_async_copy(src, scratch[2], scratch[3].at[0]).start()

            self.guarded(me, load)

    def z_finish(self, src, full, scratch):
        me = lax.axis_index("shard")

        def receive(k):
            peer = lax.rem(me + self.shards - k, self.shards)
            self.guarded(
                peer, lambda: self.z_copy(k, src, full, scratch, False).wait_recv()
            )

        each(1, self.shards, receive)

        def sent():
            each(1, self.shards, lambda k: self.z_copy(k, src, full, scratch, True).wait_send())

        self.guarded(me, sent)

    def plane_copy(self, k, d, full, scratch, sending):
        me, mine = lax.axis_index("shard"), lax.axis_index(self.split_axes)
        z = lax.rem(me + d, self.shards)
        if sending:
            peer, owner = lax.rem(mine + k, self.split), mine
        else:
            peer = owner = lax.rem(mine + self.split - k, self.split)
        region = full.at[self.slot(z), owner]
        return z, remote(
            region,
            region,
            scratch[-2].at[k, d],
            scratch[-1].at[k, d],
            peer_coords(peer, self.split_axes, self.sizes),
        )

    def plane_each(self, full, scratch, sending, act):
        def peers(k):
            def shards(d):
                z, copy = self.plane_copy(k, d, full, scratch, sending)
                self.guarded(z, lambda: act(copy))

            each(1, self.shards, shards)

        each(1, self.split, peers)

    def plane_start(self, full, scratch):
        self.plane_each(full, scratch, True, lambda copy: copy.start())

    def middle(self, ins, outs, scratch):
        if self.stages == "both":
            self.z_finish(ins[0], outs[0], scratch)
            self.plane_start(outs[0], scratch)
        elif self.stages == "z":
            me = lax.axis_index("shard")

            def store():
                pltpu.make_async_copy(ins[0], scratch[2], scratch[3].at[0]).wait()
                pltpu.make_async_copy(
                    scratch[2], outs[0].at[self.slot(me)], scratch[3].at[1]
                ).start()

            self.guarded(me, store)

    def finish(self, ins, outs, scratch):
        if self.stages == "z":
            me = lax.axis_index("shard")

            def stored():
                pltpu.make_async_copy(
                    scratch[2], outs[0].at[self.slot(me)], scratch[3].at[1]
                ).wait()

            self.guarded(me, stored)
            self.z_finish(ins[0], outs[0], scratch)
        else:
            self.plane_each(outs[0], scratch, False, lambda copy: copy.wait_recv())
            self.plane_each(outs[0], scratch, True, lambda copy: copy.wait_send())


class Compute:
    def __init__(self, body, inputs, out_shapes, scratch=()):
        self.body, self.inputs, self.out_shapes = body, list(inputs), list(out_shapes)
        self.scratch = list(scratch)


def greet_all(sizes, wide):
    barrier = pltpu.get_barrier_semaphore()
    groups = [ALL] if wide else [REP, ("shard",)]
    total = 0
    for axes in groups:
        count, me = axes_size(sizes, axes), lax.axis_index(axes)
        total += count - 1

        def greet(k):
            peer = peer_coords(lax.rem(me + k, count), axes, sizes)
            pl.semaphore_signal(barrier, inc=1, device_id=peer, device_id_type=MESH)

        each(1, count, greet)
    pl.semaphore_wait(barrier, total)


def run(collective_id, name, sizes, items, compute=None):
    wide = any(getattr(item, "axes", ()) == ALL for item in items)
    compute = compute or Compute(None, [], [])
    inputs, in_specs, out_shapes, out_specs, scratch, aliases = [], [], [], [], [], {}
    spans = []
    for item in items:
        if item.aliased:
            aliases[len(inputs)] = len(out_shapes)
        spans.append((len(inputs), len(out_shapes), len(scratch)))
        inputs += item.inputs
        in_specs += item.in_specs
        out_shapes += item.out_shapes
        out_specs += item.out_specs
        scratch += item.scratch
    own = (len(inputs), len(out_shapes), len(scratch))
    inputs += compute.inputs
    in_specs += [VMEM_SPEC] * len(compute.inputs)
    out_shapes += compute.out_shapes
    out_specs += [VMEM_SPEC] * len(compute.out_shapes)
    scratch += compute.scratch
    n_in, n_out = len(inputs), len(out_shapes)

    def kernel(*refs):
        ins, outs, tmp = refs[:n_in], refs[n_in : n_in + n_out], refs[n_in + n_out :]

        def parts(index):
            item, (a, b, c) = items[index], spans[index]
            item_ins = ins[a : a + len(item.inputs)]
            if getattr(item, "source", None) is not None:
                item_ins = [outs[own[1] + item.source]]
            return (
                item_ins,
                outs[b : b + len(item.out_shapes)],
                tmp[c : c + len(item.scratch)],
            )

        greet_all(sizes, wide)
        for index, item in enumerate(items):
            if not item.late:
                item.start(*parts(index))
        for index, item in enumerate(items):
            item.middle(*parts(index))
        if compute.body is not None:
            compute.body(ins[own[0] :], outs[own[1] :], tmp[own[2] :])
        for index, item in enumerate(items):
            if item.late:
                item.start(*parts(index))
        for index, item in enumerate(items):
            item.finish(*parts(index))

    return pl.pallas_call(
        kernel,
        out_shape=out_shapes,
        in_specs=in_specs,
        out_specs=out_specs,
        scratch_shapes=scratch,
        input_output_aliases=aliases,
        compiler_params=pltpu.CompilerParams(collective_id=collective_id, has_side_effects=True),
        name=name,
    )(*inputs)


def mask_rows(code_row):
    index = lax.broadcasted_iota(jnp.int32, (16, code_row.shape[1]), 0)
    return jnp.where(index == code_row, 0.0, NEGATIVE_HUGE).astype(bf16)


def segment_rows(segment_row):
    index = lax.broadcasted_iota(jnp.int32, (16, segment_row.shape[1]), 0)
    return jnp.where(index == segment_row, 1.0, 0.0).astype(bf16)


def as_column(row):
    return jnp.transpose(jnp.broadcast_to(row, (128, row.shape[1])))[:, :1]


def diagonal_bias(info):
    code, place = as_column(info[0:1]), as_column(info[2:3])
    allowed = (place == info[2:3]) | ((code == info[1:2]) & (place <= info[2:3]))
    return jnp.where(allowed, 0.0, NEGATIVE_HUGE)


def forward_body(ins, outs, tmp):
    qkv_ref, info_ref = ins
    out_ref, keep_ref, lse_ref = outs
    bias, acc, stat = tmp
    blocks, _, slots = qkv_ref.shape[:3]

    @pl.loop(0, blocks)
    def _(i):
        bias[...] = diagonal_bias(info_ref[i])
        seg = segment_rows(info_ref[i, 1:2])
        qa = [jnp.concatenate([qkv_ref[i, 0, m], seg], axis=0) for m in range(slots)]
        for m in range(slots):
            s = dot(jnp.transpose(qkv_ref[i, 1, m]), qkv_ref[i, 0, m]) + bias[...]
            top = jnp.max(s, axis=0, keepdims=True)
            p = jnp.exp(s - top)
            stat[2 * m : 2 * m + 1] = top
            stat[2 * m + 1 : 2 * m + 2] = jnp.sum(p, axis=0, keepdims=True)
            acc[m] = dot(qkv_ref[i, 2, m], p.astype(bf16))

        @pl.loop(0, i)
        def _(j):
            mask = mask_rows(info_ref[j, 0:1])
            for m in range(slots):
                ka = jnp.transpose(jnp.concatenate([qkv_ref[j, 1, m], mask], axis=0))
                s = dot(ka, qa[m])
                old = stat[2 * m : 2 * m + 1]
                top = jnp.maximum(old, jnp.max(s, axis=0, keepdims=True))
                p = jnp.exp(s - top)
                factor = jnp.exp(old - top)
                stat[2 * m : 2 * m + 1] = top
                stat[2 * m + 1 : 2 * m + 2] = stat[2 * m + 1 : 2 * m + 2] * factor + jnp.sum(
                    p, axis=0, keepdims=True
                )
                acc[m] = acc[m] * factor + dot(qkv_ref[j, 2, m], p.astype(bf16))

        for m in range(slots):
            total = stat[2 * m + 1 : 2 * m + 2]
            result = acc[m] / total
            out_ref[i, m] = result.astype(bf16)
            keep_ref[i, m] = result
            lse_ref[i, m : m + 1] = stat[2 * m : 2 * m + 1] + jnp.log(total)


def backward_body(ins, outs, tmp):
    qkv_ref, do_ref, keep_ref, lse_ref, info_ref = ins
    (out_ref,) = outs
    bias, dq, qn, don, delta = tmp
    blocks, _, slots = qkv_ref.shape[:3]

    @pl.loop(0, blocks)
    def _(i):
        for m in range(slots):
            qn[i, m] = jnp.transpose(qkv_ref[i, 0, m])
            don[i, m] = jnp.transpose(do_ref[i, m])
            delta[i, m : m + 1] = jnp.sum(
                do_ref[i, m].astype(f32) * keep_ref[i, m], axis=0, keepdims=True
            )
            dq[i, m] = jnp.zeros_like(dq[i, m])

    @pl.loop(0, blocks)
    def _(j):
        bias[...] = diagonal_bias(info_ref[j])
        mask = mask_rows(info_ref[j, 0:1])
        kn = [jnp.transpose(qkv_ref[j, 1, m]) for m in range(slots)]
        ka = [
            jnp.transpose(jnp.concatenate([qkv_ref[j, 1, m], mask], axis=0)) for m in range(slots)
        ]
        vn = [jnp.transpose(qkv_ref[j, 2, m]) for m in range(slots)]

        def tile(i, m, s):
            p = jnp.exp(s - lse_ref[i, m : m + 1])
            dp = dot(vn[m], do_ref[i, m])
            ds = (p * (dp - delta[i, m : m + 1])).astype(bf16)
            dq[i, m] += dot(qkv_ref[j, 1, m], ds)
            return dot(ds, qn[i, m]), dot(p.astype(bf16), don[i, m])

        start = []
        for m in range(slots):
            start += list(tile(j, m, dot(kn[m], qkv_ref[j, 0, m]) + bias[...]))

        def later(i, carry):
            seg = segment_rows(info_ref[i, 1:2])
            new = []
            for m in range(slots):
                qa = jnp.concatenate([qkv_ref[i, 0, m], seg], axis=0)
                a, b = tile(i, m, dot(ka[m], qa))
                new += [carry[2 * m] + a, carry[2 * m + 1] + b]
            return tuple(new)

        done = lax.fori_loop(j + 1, blocks, later, tuple(start))
        for m in range(slots):
            out_ref[j, 1, m] = jnp.transpose(done[2 * m]).astype(bf16)
            out_ref[j, 2, m] = jnp.transpose(done[2 * m + 1]).astype(bf16)


    @pl.loop(0, blocks)
    def _(i):
        for m in range(slots):
            out_ref[i, 0, m] = (dq[i, m] * HEAD_DIM ** (-0.5)).astype(bf16)


def ffn_kernel(x_ref, gf_ref, gu_ref, down_ref, part_ref, gu_grad_ref, down_grad_ref, ffn, dx):
    k = pl.program_id(0)
    half = gu_ref.shape[1] // 2
    x, gf = x_ref[...], gf_ref[...]
    both = dot(x, gu_ref[...])
    gate, up = both[:, :half], both[:, half:]
    sig = 1.0 / (1.0 + jnp.exp(-gate))
    act = gate * sig
    hidden = (act * up).astype(bf16)
    grad_hidden = dot(gf, down_ref[...], 1, 1)
    grad_gate = (grad_hidden * up * (sig * (1.0 + gate * (1.0 - sig)))).astype(bf16)
    grad_up = (grad_hidden * act).astype(bf16)
    grads = jnp.concatenate([grad_gate, grad_up], axis=1)
    ffn_now = dot(hidden, down_ref[...])
    dx_now = dot(grads, gu_ref[...], 1, 1)

    @pl.when(k == 0)
    def _():
        ffn[...] = ffn_now
        dx[...] = dx_now

    @pl.when(k > 0)
    def _():
        ffn[...] += ffn_now
        dx[...] += dx_now

    gu_grad = dot(x, grads, 0, 0)
    shards, padded = gu_grad_ref.shape[:2]
    filled = x.shape[1] // shards
    for z in range(shards):
        gu_grad_ref[z, :filled] = gu_grad[z * filled : (z + 1) * filled].astype(bf16)
        if padded > filled:
            gu_grad_ref[z, filled:] = jnp.zeros((padded - filled, gu_grad.shape[1]), bf16)
    down_grad_ref[...] = dot(hidden, gf, 0, 0).astype(bf16)

    @pl.when(k == pl.num_programs(0) - 1)
    def _():
        rows = part_ref.shape[2]
        for c in range(2):
            part_ref[c, 0] = dx[c * rows : (c + 1) * rows].astype(bf16)
            part_ref[c, 1] = ffn[c * rows : (c + 1) * rows].astype(bf16)


def feed_forward(x, gf, gate_up, down, shards, padded):
    tokens, width = x.shape
    hidden, columns = FF_CHUNK, 2 * FF_CHUNK
    chunks = gate_up.shape[1] // columns
    return pl.pallas_call(
        ffn_kernel,
        grid=(chunks,),
        in_specs=[
            pl.BlockSpec((tokens, width), lambda k: (0, 0)),
            pl.BlockSpec((tokens, width), lambda k: (0, 0)),
            pl.BlockSpec((width, columns), lambda k: (0, k)),
            pl.BlockSpec((hidden, width), lambda k: (k, 0)),
        ],
        out_specs=[
            pl.BlockSpec((2, 2, tokens // 2, width), lambda k: (0, 0, 0, 0)),
            pl.BlockSpec((shards, padded, columns), lambda k: (0, 0, k)),
            pl.BlockSpec((hidden, width), lambda k: (k, 0)),
        ],
        out_shape=[
            jax.ShapeDtypeStruct((2, 2, tokens // 2, width), bf16),
            jax.ShapeDtypeStruct((shards, padded, chunks * columns), bf16),
            jax.ShapeDtypeStruct(down.shape, bf16),
        ],
        scratch_shapes=[pltpu.VMEM((tokens, width), f32), pltpu.VMEM((tokens, width), f32)],
        name="feed_forward",
    )(x, gf, gate_up, down)


def rms_scale(rows, gain):
    return rows * lax.rsqrt(jnp.mean(rows * rows, axis=-1, keepdims=True) + EPSILON) * gain


def norm_back(rows, gain, grad):
    r = lax.rsqrt(jnp.mean(rows * rows, axis=-1, keepdims=True) + EPSILON)
    scaled = gain * grad
    back = r * scaled - rows * (r * r * r) * jnp.mean(scaled * rows, axis=-1, keepdims=True)
    return back, jnp.sum(grad * rows * r, axis=0)


def line_layout(lengths_row, positions):
    seq_ends = jnp.cumsum(lengths_row, dtype=jnp.int32)
    reached = seq_ends[None, :] <= positions[:, None]
    segment = jnp.sum(reached.astype(jnp.int32), axis=1)
    starts = jnp.max(jnp.where(reached, seq_ends[None, :], 0), axis=1)
    return segment, positions - starts, positions < seq_ends[-1]


def project_body(ins, outs, tmp):
    hidden_ref, weight_ref, gain_ref, cos_ref, sin_ref = ins
    sent_ref, normed_ref = outs
    reps, _, slots, _, rows = sent_ref.shape
    hidden = hidden_ref[...].astype(f32)
    normed = rms_scale(hidden, gain_ref[...]).astype(bf16)
    normed_ref[...] = normed
    cosines, sines = cos_ref[...], sin_ref[...]
    half, columns = HEAD_DIM // 2, weight_ref.shape[1]

    def put(kind, head, value):
        sent_ref[head // slots, kind, head % slots] = value

    for start in range(0, columns, 256):
        stop = min(start + 256, columns)
        block = jnp.transpose(dot(normed, weight_ref[:, start:stop]))
        for head in range(start // HEAD_DIM, stop // HEAD_DIM):
            at = head * HEAD_DIM - start
            a, b = block[at : at + half], block[at + half : at + HEAD_DIM]
            if head < QUERY_HEADS:
                scale = HEAD_DIM ** (-0.5)
                put(
                    0,
                    head,
                    (
                        jnp.concatenate(
                            [a * cosines - b * sines, b * cosines + a * sines], axis=0
                        )
                        * scale
                    ).astype(bf16),
                )
            elif head < QUERY_HEADS + KEY_VALUE_HEADS:
                value = jnp.concatenate(
                    [a * cosines - b * sines, b * cosines + a * sines], axis=0
                ).astype(bf16)
                for m in range(GROUP):
                    put(1, (head - QUERY_HEADS) * GROUP + m, value)
            else:
                value = block[at : at + HEAD_DIM].astype(bf16)
                for m in range(GROUP):
                    put(2, (head - QUERY_HEADS - KEY_VALUE_HEADS) * GROUP + m, value)
    for head in range(QUERY_HEADS, reps * slots):
        for kind in range(3):
            put(kind, head, jnp.zeros((HEAD_DIM, rows), bf16))


def project_back_body(ins, outs, tmp):
    grads_ref, cos_ref, sin_ref, weight_ref, hidden_ref, normed_ref, gain_ref, base_ref = ins
    sent_ref, weight_grad_ref, gain_grad_ref = outs
    (dt,) = tmp
    slots, half = grads_ref.shape[2], HEAD_DIM // 2
    cosines, sines = cos_ref[...], sin_ref[...]

    def get(kind, head):
        return grads_ref[head // slots, kind, head % slots].astype(f32)

    def back(value):
        a, b = value[:half], value[half:]
        return jnp.concatenate([a * cosines + b * sines, b * cosines - a * sines], axis=0)

    for head in range(QUERY_HEADS):
        dt[head * HEAD_DIM : (head + 1) * HEAD_DIM] = back(get(0, head)).astype(bf16)
    for group in range(KEY_VALUE_HEADS):
        for kind in (1, 2):
            value = get(kind, group * GROUP)
            for m in range(1, GROUP):
                value = value + get(kind, group * GROUP + m)
            if kind == 1:
                value = back(value)
            at = (QUERY_HEADS + (kind - 1) * KEY_VALUE_HEADS + group) * HEAD_DIM
            dt[at : at + HEAD_DIM] = value.astype(bf16)
    grad = dot(dt[...], weight_ref[...], 0, 1)
    norm_grad, gain_grad = norm_back(hidden_ref[...].astype(f32), gain_ref[...], grad)
    gain_grad_ref[...] = jnp.broadcast_to(gain_grad[None], gain_grad_ref.shape)
    total = (base_ref[...] + norm_grad).astype(bf16)
    devices, per_pair = sent_ref.shape[:2]
    sent_ref[...] = total.reshape(sent_ref.shape)
    shards, reps, unit, columns = weight_grad_ref.shape
    filled = normed_ref.shape[1] // shards
    for start in range(0, columns, 256):
        stop = min(start + 256, columns)
        block = dot(normed_ref[...], dt[start:stop], 0, 1)
        for z in range(shards):
            for r in range(reps):
                size = max(0, min(unit, filled - r * unit))
                at = z * filled + r * unit
                if size:
                    weight_grad_ref[z, r, :size, start:stop] = block[at : at + size].astype(bf16)
                if size < unit:
                    weight_grad_ref[z, r, size:, start:stop] = jnp.zeros(
                        (unit - size, stop - start), bf16
                    )


def rounded_up(value, unit):
    return -(-value // unit) * unit


def local(
    sizes,
    hidden_in,
    cotangent,
    destination,
    seq_lengths,
    gate_mask,
    query_weight,
    key_matrix,
    value_matrix,
    out_weight,
    gate_weight,
    up_weight,
    down_weight,
    attn_gain,
    ffn_gain,
    router_weight,
):
    rows, width = hidden_in.shape
    chips, shards = sizes["chip"], sizes["shard"]
    reps = 2 * chips
    devices = reps * shards
    per_pair = rows // devices
    slots = -(-QUERY_HEADS // reps)
    padded_heads = slots * reps
    chip, core, shard = lax.axis_index("chip"), lax.axis_index("core"), lax.axis_index("shard")
    rep = lax.axis_index(REP)
    shard_rows = query_weight.shape[0]
    rep_unit = rounded_up(-(-shard_rows // reps), 8)
    padded = rep_unit * reps
    chip_unit = padded // chips
    ff_half = gate_weight.shape[1] // 2
    chunks = ff_half // FF_CHUNK

    def padded_rows(array):
        return jnp.pad(array, ((0, padded - shard_rows), (0, 0)))

    qkv_shard = padded_rows(jnp.concatenate([query_weight, key_matrix, value_matrix], axis=1))
    qkv_shard = qkv_shard.reshape(reps, rep_unit, -1)
    out_shard = padded_rows(out_weight).reshape(reps, rep_unit, width)
    halves = [
        lax.dynamic_slice_in_dim(w, core * ff_half, ff_half, 1).reshape(
            shard_rows, chunks, 1, FF_CHUNK
        )
        for w in (gate_weight, up_weight)
    ]
    gate_up_shard = jnp.concatenate(halves, axis=2).reshape(shard_rows, 2 * ff_half)
    gate_up_shard = padded_rows(gate_up_shard).reshape(chips, chip_unit, 2 * ff_half)
    down_unit = down_weight.shape[0] // chips
    down_shard = down_weight.reshape(chips, down_unit, width)
    vectors = jnp.stack([attn_gain, ffn_gain, router_weight]).astype(f32)
    vectors = jnp.pad(vectors, ((0, 5), (0, 0)))

    def full_rows(full):
        full = full.reshape(shards, padded, full.shape[-1])
        return full[:, :shard_rows].reshape(width, full.shape[-1])

    row_index = jnp.arange(rows, dtype=jnp.int32)
    target = destination // rows
    earlier = (target[None, :] == target[:, None]) & (row_index[None, :] < row_index[:, None])
    slot_of_row = target * per_pair + jnp.sum(earlier.astype(jnp.int32), axis=1)
    to_slot = slot_of_row[None, :] == row_index[:, None]
    to_slot_b = to_slot.astype(bf16)
    place_sent = jnp.sum(jnp.where(to_slot, (destination % rows)[None, :], 0), axis=1)
    place_sent = place_sent.reshape(devices, 1, per_pair)
    place_sent = jnp.pad(place_sent, ((0, 0), (0, 0), (0, 128 - per_pair)))

    def by_slot(tokens):
        tokens = jnp.dot(to_slot_b, tokens, preferred_element_type=f32).astype(bf16)
        return tokens.reshape(devices, per_pair, width)

    got_hidden, got_place, vectors_got, qkv_full = run(
        1,
        "first",
        sizes,
        [
            AllToAll(sizes, by_slot(hidden_in), ALL),
            AllToAll(sizes, place_sent, ALL),
            AllToAll(sizes, vectors, ("shard",), spread=True),
            Gather(sizes, qkv_shard, REP, "both"),
        ],
    )
    hidden = got_hidden.reshape(rows, width)
    place = got_place[:, 0, :per_pair].reshape(rows)
    qkv_full = full_rows(qkv_full)
    vectors_full = jnp.transpose(vectors_got[:, :3], (1, 0, 2)).reshape(3, width)
    gain_one, gain_two, full_router = vectors_full[0], vectors_full[1], vectors_full[2]

    positions = rep * rows + place
    segment, within, is_valid = line_layout(seq_lengths[0], positions)
    here = place[:, None] == row_index[None, :]
    gate_here = jnp.sum(jnp.where(here, gate_mask[None, :], 0), axis=1)
    active = is_valid & (gate_here == 1)
    key_code = jnp.where(active, segment, -1)
    active_f = active.astype(f32)
    info = jnp.pad(jnp.stack([key_code, segment, place]), ((0, 5), (0, 0)))
    steps = jnp.arange(HEAD_DIM // 2).astype(f32)
    frequency = jnp.power(ROPE_BASE, -2.0 * steps / HEAD_DIM)
    angles = frequency[:, None] * within.astype(f32)[None, :]
    cosines, sines = jnp.cos(angles), jnp.sin(angles)

    heads_shape = (reps, 3, slots, HEAD_DIM, rows)
    heads_type = jax.ShapeDtypeStruct(heads_shape, bf16)
    gate_up_z, down_z, out_z, info_got, qkv_got, _, first_normalized = run(
        2,
        "project",
        sizes,
        [
            Gather(sizes, gate_up_shard, ("chip",), "z"),
            Gather(sizes, down_shard, ("chip",), "z", half=True),
            Gather(sizes, out_shard, REP, "z"),
            AllToAll(sizes, info, REP, spread=True),
            AllToAll(sizes, heads_type, REP, late=True, source=0),
        ],
        Compute(
            project_body,
            [hidden, qkv_full, gain_one[None], cosines, sines],
            [heads_type, jax.ShapeDtypeStruct((rows, width), bf16)],
        ),
    )
    slot_type = jax.ShapeDtypeStruct((reps, slots, HEAD_DIM, rows), bf16)
    gate_up_full, down_full, out_full, got_grad, att_home, _, att_keep, lse = run(
        3,
        "attend",
        sizes,
        [
            Gather(sizes, gate_up_z, ("chip",), "plane"),
            Gather(sizes, down_z, ("chip",), "plane", half=True),
            Gather(sizes, out_z, REP, "plane"),
            AllToAll(sizes, by_slot(cotangent), ALL),
            AllToAll(sizes, slot_type, REP, late=True, source=0),
        ],
        Compute(
            forward_body,
            [qkv_got, info_got],
            [
                slot_type,
                jax.ShapeDtypeStruct(slot_type.shape, f32),
                jax.ShapeDtypeStruct((reps, 8, rows), f32),
            ],
            [
                pltpu.VMEM((rows, rows), f32),
                pltpu.VMEM((slots, HEAD_DIM, rows), f32),
                pltpu.VMEM((8, rows), f32),
            ],
        ),
    )
    attn_out_t = att_home.reshape(padded_heads * HEAD_DIM, rows)[:width]
    full_out = full_rows(out_full)
    gate_up = full_rows(gate_up_full)
    down = down_full.reshape(ff_half, width)

    hidden_f = hidden.astype(f32)
    router_logit = jnp.sum(hidden_f * full_router, axis=1)
    gate_value = jax.nn.sigmoid(router_logit)
    branch_scale = active_f * gate_value
    attn_branch = jnp.einsum("dt,de->te", attn_out_t, full_out, preferred_element_type=f32)
    middle = hidden_f + attn_branch
    normed_two = rms_scale(middle, gain_two).astype(bf16)
    grad_out = got_grad.reshape(rows, width).astype(f32)
    grad_branch = branch_scale[:, None] * grad_out
    grad_ffn = grad_branch.astype(bf16)
    x_pair, gf_pair = run(
        4,
        "pair",
        sizes,
        [
            AllToAll(sizes, normed_two, ("core",), spread=True),
            AllToAll(sizes, grad_ffn, ("core",), spread=True),
        ],
    )
    parts, gate_up_grad, down_grad = feed_forward(
        x_pair.reshape(2 * rows, width),
        gf_pair.reshape(2 * rows, width),
        gate_up,
        down,
        shards,
        padded,
    )
    (parts_got,) = run(5, "parts", sizes, [AllToAll(sizes, parts, ("core",))])
    grad_normed_two = parts_got[0, 0].astype(f32) + parts_got[1, 0].astype(f32)
    ffn_branch = parts_got[0, 1].astype(f32) + parts_got[1, 1].astype(f32)
    branch_sum = attn_branch + ffn_branch
    result = (hidden_f + branch_scale[:, None] * branch_sum).astype(bf16)
    grad_logit = active_f * jnp.sum(grad_out * branch_sum, axis=1) * gate_value * (1.0 - gate_value)
    grad_middle, grad_gain_ffn = norm_back(middle, gain_two, grad_normed_two)
    grad_attn = (grad_branch + grad_middle).astype(bf16)
    grad_attention_t = jnp.einsum("te,de->dt", grad_attn, full_out, preferred_element_type=f32)
    grad_attention_t = jnp.pad(
        grad_attention_t.astype(bf16), ((0, padded_heads * HEAD_DIM - width), (0, 0))
    ).reshape(slot_type.shape)
    (grad_got,) = run(6, "grads", sizes, [AllToAll(sizes, grad_attention_t, REP)])

    out_grad = jnp.einsum("dt,te->de", attn_out_t, grad_attn, preferred_element_type=f32)
    out_grad = jnp.pad(
        out_grad.astype(bf16).reshape(shards, shard_rows, width),
        ((0, 0), (0, padded - shard_rows), (0, 0)),
    ).reshape(shards, reps, rep_unit, width)
    gate_up_grad = gate_up_grad.reshape(shards, chips, chip_unit, 2 * ff_half)
    down_grad = down_grad.reshape(shards // 2, chips, down_unit, width)
    gate_up_recv, down_recv, out_recv, home_out, heads_home, _ = run(
        7,
        "attend_back",
        sizes,
        [
            Scatter(sizes, gate_up_grad, ("chip",), 1),
            Scatter(sizes, down_grad, ("chip",), 1),
            Scatter(sizes, out_grad, REP, 1),
            AllToAll(sizes, result.reshape(devices, per_pair, width), ALL),
            AllToAll(sizes, heads_type, REP, late=True, source=0),
        ],
        Compute(
            backward_body,
            [qkv_got, grad_got, att_keep, lse, info_got],
            [heads_type],
            [
                pltpu.VMEM((rows, rows), f32),
                pltpu.VMEM((reps, slots, HEAD_DIM, rows), f32),
                pltpu.VMEM((reps, slots, rows, HEAD_DIM), bf16),
                pltpu.VMEM((reps, slots, rows, HEAD_DIM), bf16),
                pltpu.VMEM((reps, 8, rows), f32),
            ],
        ),
    )

    def summed(own, got):
        total = own.astype(f32)
        for index in range(got.shape[0]):
            total = total + got[index].astype(f32)
        return total.astype(bf16)

    def taken(array, index, dim):
        return lax.dynamic_index_in_dim(array, index, dim, keepdims=False)

    gate_up_sum = summed(taken(gate_up_grad, chip, 1), gate_up_recv)
    down_sum = summed(taken(down_grad, chip, 1), down_recv)
    out_sum = summed(taken(out_grad, rep, 1), out_recv)

    base = grad_out + grad_middle + grad_logit[:, None] * full_router
    tokens_type = jax.ShapeDtypeStruct((devices, per_pair, width), bf16)
    qkv_grad_type = jax.ShapeDtypeStruct((shards, reps, rep_unit, qkv_full.shape[1]), bf16)
    gate_up_recv, down_recv, out_recv, home_grad, qkv_recv, _, qkv_grad, gain_grad = run(
        8,
        "project_back",
        sizes,
        [
            Scatter(sizes, gate_up_sum, ("shard",), 0),
            Scatter(sizes, down_sum, ("shard",), 0, half=True),
            Scatter(sizes, out_sum, ("shard",), 0),
            AllToAll(sizes, tokens_type, ALL, late=True, source=0),
            Scatter(sizes, qkv_grad_type, REP, 1, late=True, source=1),
        ],
        Compute(
            project_back_body,
            [
                heads_home,
                cosines,
                sines,
                qkv_full,
                hidden,
                first_normalized,
                gain_one[None],
                base,
            ],
            [tokens_type, qkv_grad_type, jax.ShapeDtypeStruct((8, width), f32)],
            [pltpu.VMEM((qkv_full.shape[1], rows), bf16)],
        ),
    )
    gate_up_sum = summed(taken(gate_up_sum, shard, 0), gate_up_recv)
    down_sum = summed(taken(down_sum, lax.rem(shard, shards // 2), 0), down_recv)
    out_sum = summed(taken(out_sum, shard, 0), out_recv)
    qkv_sum = summed(taken(qkv_grad, rep, 1), qkv_recv)
    router_grad = jnp.sum(grad_logit[:, None] * hidden_f, axis=0)
    vector_grads = jnp.stack([gain_grad[0], grad_gain_ffn, router_grad])
    vector_grads = jnp.pad(vector_grads, ((0, 5), (0, 0))).reshape(8, shards, shard_rows)
    vector_grads = jnp.broadcast_to(
        jnp.transpose(vector_grads, (1, 0, 2))[None], (reps, shards, 8, shard_rows)
    ).reshape(devices, 8, shard_rows)
    gate_up_home, down_home, out_home, vectors_home, qkv_recv = run(
        9,
        "totals",
        sizes,
        [
            AllToAll(sizes, gate_up_sum, REP, spread=True),
            SpreadHalf(sizes, down_sum),
            AllToAll(sizes, out_sum, REP, spread=True),
            AllToAll(sizes, vector_grads, ALL),
            Scatter(sizes, qkv_sum, ("shard",), 0),
        ],
    )
    qkv_sum = summed(taken(qkv_sum, shard, 0), qkv_recv)
    (qkv_home,) = run(10, "last", sizes, [AllToAll(sizes, qkv_sum, REP, spread=True)])

    qkv_total = qkv_home.reshape(padded, -1)[:shard_rows].astype(f32)
    out_total = out_home.reshape(padded, width)[:shard_rows].astype(f32)
    gate_up_total = gate_up_home.reshape(chips, 2, chip_unit, chunks, 2, FF_CHUNK)

    def half_total(which):
        total = jnp.transpose(gate_up_total[:, :, :, :, which], (0, 2, 1, 3, 4))
        return total.reshape(padded, 2 * ff_half)[:shard_rows].astype(f32)

    vector_total = jnp.sum(vectors_home, axis=0)
    q_end, k_end = query_weight.shape[1], query_weight.shape[1] + key_matrix.shape[1]

    def home_rows(home):
        home = home.reshape(rows, width)
        return jnp.einsum("sr,sw->rw", to_slot_b, home, preferred_element_type=f32).astype(bf16)

    return (
        home_rows(home_out),
        home_rows(home_grad),
        qkv_total[:, :q_end],
        qkv_total[:, q_end:k_end],
        qkv_total[:, k_end:],
        out_total,
        half_total(0),
        half_total(1),
        down_home.reshape(-1, width).astype(f32),
        vector_total[0],
        vector_total[1],
        vector_total[2],
    )


def solution(mesh):
    reps, shards = mesh.shape["rep"], mesh.shape["shard"]
    sizes = {"chip": reps // 2, "core": 2, "shard": shards}
    split_mesh = Mesh(mesh.devices.reshape(reps // 2, 2, shards), ALL)
    tokens, tokens_1d = P(ALL, None), P(ALL)
    weight, vector = P("shard", None), P("shard")
    return jax.shard_map(
        functools.partial(local, sizes),
        mesh=split_mesh,
        in_specs=(tokens, tokens, tokens_1d, weight, tokens_1d) + (weight,) * 7 + (vector,) * 3,
        out_specs=(tokens, tokens) + (weight,) * 7 + (vector,) * 3,
        check_vma=False,
    )
```

time: 1020 us -> 774 us (0.76)
  waiting for transfers between devices: 418 us -> 0 us
  Pallas kernels: 385 us -> 642 us
  local copies, waits for them, and re-layouts: 108 us -> 60.4 us
  starting transfers between devices: 16.4 us -> 0 us
  matrix products: 27.1 us -> 11.2 us
  between operations: 15.1 us -> 1.72 us
    reduce_scatter x3 -> x0, waiting for transfers between devices: 303 us -> none  [the longest x1 157 us: local(): lax.psum_scatter(proj_grad.reshape(devices, shard_rows, -1), ALL, scatter...]
    pallas_call x9 -> x10, Pallas kernels: 342 us -> 606 us  [run(): pl.pallas_call(kernel, out_shape=out_shapes, in_specs=in_specs, out_specs...]
    all_gather x7 -> x0, waiting for transfers between devices: 91.8 us -> none  [the longest x1 43.1 us: local(): qkv_all = lax.all_gather(qkv_piece, ALL, axis=0, tiled=True)]
    all_to_all x3 -> x0, waiting for transfers between devices: 21.9 us -> none  [the longest x1 21.9 us: local(): lax.all_to_all(grad_hidden.astype(bf16).reshape(devices, per_pair, width)...]
    transpose x8 -> x4, local copies, waits for them, and re-layouts: 22.1 us -> 1.94 us  [the longest x2 1.17 us: half_total(): total = jnp.transpose(gate_up_total[:, :, :, :, which], (0, 2, 1, 3, 4))]
    all_to_all x3 -> x0, starting transfers between devices: 15.8 us -> none  [the longest x1 8.34 us: local(): lax.all_to_all(sent_grad.reshape(devices, per_pair, width), ALL, split_ax...]
    reshape x4 -> x6, local copies, waits for them, and re-layouts: 27.5 us -> 12.2 us  [the longest x1 6.6 us: local(): gate_up_home.reshape(chips, 2, chip_unit, chunks, 2, FF_CHUNK)]
    dot_general x7 -> x4, matrix products: 19.5 us -> 6.18 us  [the longest x2 4.71 us: home_rows(): jnp.einsum('sr,sw->rw', to_slot_b, home, preferred_element_type=f32)]
  transfers between devices with their start and end apart: 13 -> 0, of which waited for: 7 -> 0; matrix products, arithmetic and copies ran while one was open for 15% -> 0% of each run, Pallas kernels for 33% -> 0%
where the time goes in v2:
time: 774 us; the launch traced here: 766 us
  Pallas kernels  642 us (83%)
  local copies, waits for them, and re-layouts  60.4 us (8%)
  other arithmetic  50.1 us (6%)
  matrix products  11.2 us (1%)
    pallas_call x10, Pallas kernels, run(): pl.pallas_call(kernel, out_shape=out_shapes, in_specs=in_specs, out_specs...  606 us
    pallas_call x1, Pallas kernels, feed_forward(): pl.pallas_call(ffn_kernel, grid=(chunks,), in_specs=[pl.BlockSpec((tokens...  36 us

profile of v2, /device:TPU:0, one launch (start us, length us, event | category | flops | bytes accessed | tf_op | source)
XLA Modules:
  0.0 765.8 jit_solution(8252183172809178492)
XLA Ops:
  7.1 72.2 %first.1 = (bf16[32,16,960]{2,1,0:T(8,128)(2,1)}, s32[32,1,128]{2,1,0:T(1,128)}, f32[4,8,240]{2,1,0:T(8,128)}, bf16[4,8,32,1600]{3,2,1,0:T(8,128)(2,1)}) custom-call(bf16[32,16,960]{2,1,0:T(8,128)(2,1)} %bitcast.218, s32[32,1,128]{2,1,0:T(1,128)} %pad.38.refs_1_, f32[8,240]{1,0:T(8,128)} %fusion.33.refs_2_, bf16[8,32,1600]{2,1,0:T(8,128)(2,1)} %bitcast.223), custom_call_target="tpu_custom_call" | custom-call | tf_op jit(solution)/shard_map/first/pallas_call | solution.py:437
  93.2 3.9 slice.243
  97.1 1.9 copy.159
  99.8 51.8 %project.1 = (bf16[4,4,64,2560]{3,2,1,0:T(8,128)(2,1)}, bf16[2,4,160,960]{3,2,1,0:T(8,128)(2,1)}, bf16[4,8,32,960]{3,2,1,0:T(8,128)(2,1)}, s32[8,8,512]{2,1,0:T(...) custom-call(bf16[4,64,2560]{2,1,0:T(8,128)(2,1)} %bitcast.216, ...), custom_call_target="tpu_custom_call" | custom-call | tf_op jit(solution)/shard_map/project/pallas_call | solution.py:437
  153.7 124.2 %attend.1 = (bf16[4,4,64,2560]{3,2,1,0:T(8,128)(2,1)}, bf16[2,4,160,960]{3,2,1,0:T(8,128)(2,1)}, bf16[4,8,32,960]{3,2,1,0:T(8,128)(2,1)}, bf16[32,16,960]{2,1,0:...) custom-call(bf16[4,4,64,2560]{3,2,1,0:T(8,128)(2,1)} %get-tuple-elem, ...), custom_call_target="tpu_custom_call", output_to_operand_aliasing={{0}: (0, {}), {1}: (1, {}), {2}: (2, {})} | custom-call | tf_op jit(solution)/shard_map/attend/pallas_call | solution.py:437
  277.9 2.6 fusion.2.refs_1_
  282.8 2.6 multiply_reduce_fusion.1
  285.5 2.9 multiply_convert_fusion.refs_0_
  288.4 9.3 %pair.1 = (bf16[2,512,960]{2,1,0:T(8,128)(2,1)}, bf16[2,512,960]{2,1,0:T(8,128)(2,1)}) custom-call(bf16[512,960]{1,0:T(8,128)(2,1)} %multiply_convert_fusion.refs_0_, bf16[512,960]{1,0:T(8,128)(2,1)} %fusion.2.refs_1_), custom_call_target="tpu_custom_call" | custom-call | tf_op jit(solution)/shard_map/pair/pallas_call | solution.py:437
  297.7 5.0 slice.249
  302.7 36.0 %feed_forward.1 = (bf16[2,2,512,960]{3,2,1,0:T(8,128)(2,1)}, bf16[4,256,2560]{2,1,0:T(8,128)(2,1)}, bf16[1280,960]{1,0:T(8,128)(2,1)}) custom-call(bf16[1024,960]{1,0:T(8,128)(2,1)} %bitcast.229, bf16[1024,960]{1,0:T(8,128)(2,1)} %bitcast.230, bf16[960,2560]{1,0:T(8,128)(2,1)} %bitcast.206, bf16[1280,960]{1,0:T(8,128)(2,1)} %bitcast.207), custom_call_target="tpu_custom_call" | custom-call | tf_op jit(solution)/shard_map/feed_forward/pallas_call | solution.py:617
  338.7 10.9 %parts.1 = bf16[2,2,512,960]{3,2,1,0:T(8,128)(2,1)} custom-call(bf16[2,2,512,960]{3,2,1,0:T(8,128)(2,1)} %get-tuple-element.69.refs_0_), custom_call_target="tpu_custom_call" | custom-call | tf_op jit(solution)/shard_map/parts/pallas_call | solution.py:437
  349.7 4.4 fusion.10
  354.4 3.4 fusion.7
  360.0 15.2 %grads.1.refs_5_ = bf16[8,2,64,512]{3,2,1,0:T(8,128)(2,1)} custom-call(bf16[8,2,64,512]{3,2,1,0:T(8,128)(2,1)} %bitcast.219), custom_call_target="tpu_custom_call" | custom-call | tf_op jit(solution)/shard_map/grads/pallas_call | solution.py:437
  378.0 164.5 %attend_back.1 = (bf16[3,4,64,2560]{3,2,1,0:T(8,128)(2,1)}, bf16[3,2,160,960]{3,2,1,0:T(8,128)(2,1)}, bf16[7,4,32,960]{3,2,1,0:T(8,128)(2,1)}, bf16[32,16,960]{2...) custom-call(bf16[4,4,64,2560]{3,2,1,0:T(8,128)(2,1)} %bitcast.212, ...), custom_call_target="tpu_custom_call" | custom-call | tf_op jit(solution)/shard_map/attend_back/pallas_call | solution.py:437
  542.6 2.7 fusion.17.refs_2_
  545.2 2.4 fusion.11.refs_1_
  547.6 4.2 fusion.refs_0_
  551.8 84.0 %project_back.1 = (bf16[3,64,2560]{2,1,0:T(8,128)(2,1)}, bf16[3,160,960]{2,1,0:T(8,128)(2,1)}, bf16[3,32,960]{2,1,0:T(8,128)(2,1)}, bf16[32,16,960]{2,1,0:T(8,12...) custom-call(bf16[4,64,2560]{2,1,0:T(8,128)(2,1)} %fusion.refs_0_, ...), custom_call_target="tpu_custom_call" | custom-call | tf_op jit(solution)/shard_map/project_back/pallas_call | solution.py:437
  635.9 3.2 fusion.16.refs_4_
  643.5 2.1 fusion.23.refs_1_
  647.5 61.0 %totals.1 = (bf16[8,64,2560]{2,1,0:T(8,128)(2,1)}, bf16[4,160,960]{2,1,0:T(8,128)(2,1)}, bf16[8,32,960]{2,1,0:T(8,128)(2,1)}, f32[32,8,240]{2,1,0:T(8,128)}, bf16[3,32,1600]{2,1,0:T(8,128)(2,1)}) custom-call(bf16[64,2560]{1,0:T(8,128)(2,1)} %fusion.22.refs_0_, bf16[160,960]{1,0:T(8,128)(2,1)} %fusion.23.refs_1_, bf16[32,960]{1,0:T(8,128)(2,1)} %fusion.25.refs_2_, ...), custom_call_target="tpu_custom_call" | custom-call | tf_op jit(solution)/shard_map/totals/pallas_call | solution.py:437
  708.5 6.6 reshape.407
  715.1 7.7 %fusion.35 = (bf16[4,2,64,5,1,256]{5,4,3,2,1,0:T(2,128)(2,1)S(1)}, bf16[4,2,64,5,1,256]{5,4,3,2,1,0:T(2,128)(2,1)}) fusion(bf16[4,2,64,5,2,256]{5,4,3,2,1,0:T(2,128)(2,1)} %reshape.407), kind=kLoop, calls=%fused_computation.132 | loop fusion | bytes 5242880 | tf_op jit(solution)/shard_map/slice | solution.py:1056
  723.3 2.3 reshape.409
  725.6 3.2 slice_convert_fusion
  729.4 2.3 reshape.408
  731.7 3.1 slice_convert_fusion.1
  736.7 3.2 copy.177
  741.5 13.2 %last.1 = bf16[8,32,1600]{2,1,0:T(8,128)(2,1)} custom-call(bf16[32,1600]{1,0:T(8,128)(2,1)} %fusion.24.refs_0_), custom_call_target="tpu_custom_call" | custom-call | tf_op jit(solution)/shard_map/last/pallas_call | solution.py:437
  760.6 3.0 convolution_convert_fusion.1
  (165 shorter events, 49.1 us)
Async XLA Ops:
  1.7 3.0 copy-start.28
  2.6 2.2 copy-start.26
  2.6 2.4 copy-start.19
  5.4 77.2 %copy-start.32 = (s32[512]{0:T(512)S(1)}, s32[512]{0:T(512)}, u32[]{:S(2)}) copy-start(s32[512]{0:T(512)} %param.19) | copy-start | bytes 6148
  5.4 77.4 %copy-start.41 = (s32[1,8]{1,0:T(1,128)S(1)}, s32[1,8]{1,0:T(1,128)}, u32[]{:S(2)}) copy-start(s32[1,8]{1,0:T(1,128)} %param.18) | copy-start | bytes 100
  6.4 80.8 %copy-start.22 = (bf16[240,2560]{1,0:T(8,128)(2,1)S(1)}, bf16[240,2560]{1,0:T(8,128)(2,1)}, u32[]{:S(2)}) copy-start(bf16[240,2560]{1,0:T(8,128)(2,1)} %param.25) | copy-start | bytes 3686404
  84.8 4.1 copy-start.30
  93.2 3.9 copy-start.14
  99.8 51.8 %copy-start.29 = (s32[512]{0:T(512)S(1)}, s32[512]{0:T(512)}, u32[]{:S(2)}) copy-start(s32[512]{0:T(512)} %copy-done.28) | copy-start | bytes 6148
  99.8 51.8 %copy-start.37 = (bf16[512,960]{0,1:T(8,128)(2,1)S(1)}, bf16[512,960]{0,1:T(8,128)(2,1)}, u32[]{:S(2)}) copy-start(bf16[512,960]{0,1:T(8,128)(2,1)} %param.16) | copy-start | bytes 2949124
  277.9 2.6 copy-start.8
  280.7 4.7 copy-start.10
  338.7 11.0 %copy-start.7 = (bf16[32,16,960]{2,1,0:T(8,128)(2,1)S(1)}, bf16[32,16,960]{2,1,0:T(8,128)(2,1)}, u32[]{:S(2)}) copy-start(bf16[32,16,960]{2,1,0:T(8,128)(2,1)} %get-tuple-element.62) | copy-start | bytes 2949124
  349.6 4.4 copy-start.33
  349.6 4.4 copy-start.4
  349.6 4.7 copy-start.5
  354.4 3.4 copy-start.11
  359.0 16.3 %copy-start.36 = (bf16[8,2,64,512]{3,2,1,0:T(8,128)(2,1)S(1)}, bf16[8,2,64,512]{3,2,1,0:T(8,128)(2,1)}, u32[]{:S(2)}) copy-start(bf16[8,2,64,512]{3,2,1,0:T(8,128)(2,1)} %get-tuple-element.60) | copy-start | bytes 3145732
  360.0 15.2 %copy-start.16 = (bf16[512,960]{1,0:T(8,128)(2,1)S(1)}, bf16[512,960]{1,0:T(8,128)(2,1)}, u32[]{:S(2)}) copy-start(bf16[512,960]{1,0:T(8,128)(2,1)} %copy-done.15) | copy-start | bytes 2949124
  542.5 2.7 copy-start.12
  635.8 3.4 copy-start.31
  635.8 3.4 copy-start.27
  635.8 4.2 copy-start.3
  635.8 6.2 copy-start.24
  635.8 7.7 copy-start.9
  639.1 6.5 copy-start.17
  725.6 3.2 copy-start.6
  731.7 3.1 copy-start.13
  736.7 3.2 copy-start.21
  756.8 3.2 copy-start.23
  760.0 3.6 copy-start.34
  760.6 4.7 copy-start.1
  (10 other events, 18.4 us)

commit v3 on v2

--- a/solution.py
+++ b/solution.py
@@ -65,152 +65,209 @@
 
 class Item:
     late = False
+    final = False
     aliased = False
-
-    def start(self, ins, outs, scratch):
-        pass
-
-    def middle(self, ins, outs, scratch):
-        pass
-
-    def finish(self, ins, outs, scratch):
-        pass
+    pre = 0
+
+    def steps(self, ins, outs, scratch):
+        yield
 
 
 class AllToAll(Item):
-    def __init__(self, sizes, array, axes, spread=False, late=False, source=None):
+    final = True
+
+    def __init__(self, sizes, array, axes, spread=False, by_shard=False, late=False, source=None):
         self.sizes, self.axes, self.spread, self.late = sizes, axes, spread, late
+        self.by_shard = by_shard
         self.count = axes_size(sizes, axes)
         self.source = source
         self.inputs = [] if source is not None else [array]
-        shape = (self.count,) + tuple(array.shape) if spread else tuple(array.shape)
+        piece = tuple(array.shape) if spread else tuple(array.shape[1:])
         self.in_specs = [VMEM_SPEC] * len(self.inputs)
-        self.out_shapes = [jax.ShapeDtypeStruct(shape, array.dtype)]
+        self.out_shapes = [jax.ShapeDtypeStruct((self.count,) + piece, array.dtype)]
         self.out_specs = [VMEM_SPEC]
         self.scratch = [
             pltpu.SemaphoreType.DMA((self.count,)),
             pltpu.SemaphoreType.DMA((self.count,)),
         ]
 
+    def index(self, peer):
+        return lax.rem(peer, self.sizes["shard"]) if self.by_shard else peer
+
     def copy(self, k, ins, outs, scratch):
         me = lax.axis_index(self.axes)
         peer = lax.rem(me + k, self.count)
         return remote(
-            ins[0] if self.spread else ins[0].at[peer],
+            ins[0] if self.spread else ins[0].at[self.index(peer)],
             outs[0].at[me],
             scratch[0].at[k],
             scratch[1].at[k],
             peer_coords(peer, self.axes, self.sizes),
         )
 
-    def start(self, ins, outs, scratch):
+    def steps(self, ins, outs, scratch):
         each(1, self.count, lambda k: self.copy(k, ins, outs, scratch).start())
         me = lax.axis_index(self.axes)
-        outs[0][me] = ins[0][...] if self.spread else ins[0][me]
-
-    def finish(self, ins, outs, scratch):
+        outs[0][me] = ins[0][...] if self.spread else ins[0][self.index(me)]
+        yield
         each(1, self.count, lambda k: self.copy(k, ins, outs, scratch).wait())
 
 
-class Scatter(Item):
-    def __init__(self, sizes, array, axes, dim, half=False, late=False, source=None):
-        self.sizes, self.axes, self.dim = sizes, axes, dim
-        self.half, self.late, self.source = half, late, source
-        self.count = axes_size(sizes, axes)
-        self.slots = self.count // 2
-        piece = tuple(array.shape[:dim]) + tuple(array.shape[dim + 1 :])
-        self.inputs = [] if source is not None else [array]
-        self.in_specs = [HBM_SPEC] * len(self.inputs)
-        self.out_shapes = [jax.ShapeDtypeStruct((self.count - 1,) + piece, array.dtype)]
-        self.out_specs = [HBM_SPEC]
-        self.scratch = [
-            pltpu.SemaphoreType.DMA((self.count,)),
-            pltpu.SemaphoreType.DMA((self.count,)),
-        ]
-
-    def guarded(self, index, body):
-        if self.half:
-            pl.when(index // self.slots == lax.axis_index("core"))(body)
-        else:
-            body()
-
-    def copy(self, k, ins, outs, scratch):
-        me = lax.axis_index(self.axes)
-        peer = lax.rem(me + k, self.count)
-        index = lax.rem(peer, self.slots) if self.half else peer
-        src = ins[0].at[index] if self.dim == 0 else ins[0].at[:, index]
+class Heads(Item):
+    final = True
+    late = True
+
+    def __init__(self, sizes, array, to, source):
+        self.sizes, self.to, self.source = sizes, to, source
+        self.count = axes_size(sizes, REP)
+        self.slots = array.shape[1] // 3
+        self.main = array.shape[1] if self.slots != 2 else 4
+        self.units = array.shape[1]
+        self.inputs, self.in_specs = [], []
+        self.out_shapes = [jax.ShapeDtypeStruct(array.shape, array.dtype)]
+        self.out_specs = [VMEM_SPEC]
+        dma = pltpu.SemaphoreType.DMA
+        self.scratch = [dma((2, self.count)), dma((2, self.count))]
+
+    def copy(self, k, ins, outs, scratch, extra, sending):
+        me = lax.axis_index(REP)
+        peer = lax.rem(me + (k if sending else self.count - k), self.count)
+        units = pl.ds(self.main, self.units - self.main) if extra else pl.ds(0, self.main)
         return peer, remote(
-            src,
-            outs[0].at[k - 1],
-            scratch[0].at[k],
-            scratch[1].at[k],
-            peer_coords(peer, self.axes, self.sizes),
-        )
-
-    def start(self, ins, outs, scratch):
-        def send(k):
-            peer, copy = self.copy(k, ins, outs, scratch)
-            self.guarded(peer, copy.start)
-
-        each(1, self.count, send)
-
-    def finish(self, ins, outs, scratch):
-        def receive(k):
-            self.copy(k, ins, outs, scratch)[1].wait_recv()
-
-        def sent(k):
-            peer, copy = self.copy(k, ins, outs, scratch)
-            self.guarded(peer, copy.wait_send)
-
-        me = lax.axis_index(self.axes)
-        self.guarded(me, lambda: each(1, self.count, receive))
-        each(1, self.count, sent)
-
-
-class SpreadHalf(Item):
-    def __init__(self, sizes, array):
-        self.sizes, self.count = sizes, axes_size(sizes, REP)
-        self.slots = sizes["shard"] // 2
-        self.inputs, self.in_specs = [array], [VMEM_SPEC]
-        shape = (sizes["chip"],) + tuple(array.shape)
-        self.out_shapes = [jax.ShapeDtypeStruct(shape, array.dtype)]
-        self.out_specs = [VMEM_SPEC]
-        self.scratch = [
-            pltpu.SemaphoreType.DMA((self.count,)),
-            pltpu.SemaphoreType.DMA((self.count,)),
-        ]
-
-    def owner(self):
-        return lax.axis_index("shard") // self.slots
-
-    def copy(self, k, ins, outs, scratch, sending):
-        me = lax.axis_index(REP)
-        peer = lax.rem(me + k, self.count) if sending else lax.rem(me + self.count - k, self.count)
-        chip = lax.axis_index("chip") if sending else peer // 2
-        return peer, remote(
-            ins[0],
-            outs[0].at[chip],
-            scratch[0].at[k],
-            scratch[1].at[k],
+            ins[0].at[peer, units],
+            outs[0].at[me if sending else peer, units],
+            scratch[0].at[int(extra), k],
+            scratch[1].at[int(extra), k],
             peer_coords(peer, REP, self.sizes),
         )
 
-    def start(self, ins, outs, scratch):
-        @pl.when(lax.axis_index("core") == self.owner())
-        def _():
-            each(1, self.count, lambda k: self.copy(k, ins, outs, scratch, True)[1].start())
-            outs[0][lax.axis_index("chip")] = ins[0][...]
-
-    def finish(self, ins, outs, scratch):
-        def receive(k):
-            peer, copy = self.copy(k, ins, outs, scratch, False)
-            pl.when(lax.rem(peer, 2) == self.owner())(copy.wait_recv)
-
-        each(1, self.count, receive)
-
-        @pl.when(lax.axis_index("core") == self.owner())
-        def _():
-            each(1, self.count, lambda k: self.copy(k, ins, outs, scratch, True)[1].wait_send())
+    def every(self, ins, outs, scratch, sending, act):
+        def main(k):
+            act(self.copy(k, ins, outs, scratch, False, sending)[1])
+
+        def extra(k):
+            peer, copy = self.copy(k, ins, outs, scratch, True, sending)
+            owner = peer if sending == self.to else lax.axis_index(REP)
+            pl.when(apart(owner) == 1)(lambda: act(copy))
+
+        each(1, self.count, main)
+        if self.units > self.main:
+            each(1, self.count, extra)
+
+    def steps(self, ins, outs, scratch):
+        self.every(ins, outs, scratch, True, lambda copy: copy.start())
+        me = lax.axis_index(REP)
+        outs[0][me] = ins[0][me]
+        yield
+        self.every(ins, outs, scratch, False, lambda copy: copy.wait_recv())
+        self.every(ins, outs, scratch, True, lambda copy: copy.wait_send())
+
+
+def apart(rep):
+    last = KEY_VALUE_HEADS - 1
+    return jnp.minimum((2 * rep + 1) // GROUP, last) - jnp.minimum((2 * rep) // GROUP, last)
+
+
+def key_slots(slots):
+    return [0, apart(lax.axis_index(REP))] if slots == 2 else list(range(slots))
+
+
+def key_unit(slots, slot):
+    return slots + 2 * slot
+
+
+def value_unit(slots, slot):
+    return slots + 2 * slot + 1
+
+
+def flipped(chip, k):
+    x, y = lax.rem(chip, 2), chip // 2
+    x = 1 - x if k in (1, 3) else x
+    y = 1 - y if k in (2, 3) else y
+    return 2 * y + x
+
+
+class Plane:
+    def __init__(self, sizes, pair, lo, hi):
+        self.pair, self.lo, self.hi, self.chips = pair, lo, hi, sizes["chip"]
+        self.relay = self.chips == 4
+        self.near = (1, 2) if self.relay else tuple(range(1, self.chips))
+        self.scratch = [pltpu.SemaphoreType.DMA((self.chips, hi))] * (4 if pair else 2)
+
+    def bind(self, region, path, guard, other, sems):
+        self.region, self.path, self.guard, self.other, self.sems = region, path, guard, other, sems
+        self.chip, self.core = lax.axis_index("chip"), lax.axis_index("core")
+
+    def peer(self, k):
+        return flipped(self.chip, k) if self.relay else lax.rem(self.chip + k, self.chips)
+
+    def owner(self, k):
+        if self.relay:
+            return flipped(self.chip, k)
+        return lax.rem(self.chip + self.chips - k, self.chips)
+
+    def copy(self, t, k, owner, to):
+        ref = self.region(t, owner, self.core)
+        return remote(ref, ref, self.sems[0].at[k, t], self.sems[1].at[k, t], {"chip": to})
+
+    def relayed(self, t, k):
+        return self.copy(t, 3, self.owner(k), self.peer(3 - k))
+
+    def pass_on(self, t, owner, core=None):
+        ref = self.region(t, owner, self.core if core is None else core)
+        return remote(
+            ref, ref, self.sems[2].at[owner, t], self.sems[3].at[owner, t], {"core": 1 - self.core}
+        )
+
+    def parts(self, body, guard=None):
+        each(self.lo, self.hi, lambda t: (guard or self.guard)(t, lambda: body(t)))
+
+    def start(self):
+        def part(t):
+            for k in self.near:
+                self.copy(t, k, self.chip, self.peer(k)).start()
+            if self.pair:
+                self.pass_on(t, self.chip).start()
+
+        self.parts(part)
+
+    def forward(self):
+        def arrived(t, k):
+            self.copy(t, k, self.owner(k), self.chip).wait_recv()
+            if self.pair:
+                self.pass_on(t, self.owner(k)).start()
+
+        def part(t):
+            for k in self.near:
+                arrived(t, k)
+                if self.relay:
+                    pl.when(self.path(t) == k - 1)(lambda: self.relayed(t, k).start())
+
+        self.parts(part)
+        if self.relay:
+            self.parts(lambda t: arrived(t, 3))
+
+    def finish(self):
+        def sent(t):
+            for k in self.near:
+                self.copy(t, k, self.chip, self.peer(k)).wait_send()
+                if self.relay:
+                    pl.when(self.path(t) == k - 1)(lambda: self.relayed(t, k).wait_send())
+            if self.pair:
+                each(0, self.chips, lambda c: self.pass_on(t, c).wait_send())
+
+        self.parts(sent)
+        if self.pair:
+            self.parts(
+                lambda t: each(
+                    0, self.chips, lambda c: self.pass_on(t, c, 1 - self.core).wait_recv()
+                ),
+                self.other,
+            )
+
+
+def always(t, body):
+    body()
 
 
 class Gather(Item):
@@ -218,8 +275,9 @@
         self.sizes, self.split_axes, self.stages, self.half = sizes, split_axes, stages, half
         self.shards = sizes["shard"]
         self.slots = self.shards // 2 if half else self.shards
-        self.split = axes_size(sizes, split_axes)
+        self.pair = len(split_axes) == 2
         both = stages == "both"
+        self.pre = 0 if stages == "plane" else 1
         self.inputs = [array]
         self.in_specs = [VMEM_SPEC if both else HBM_SPEC]
         if stages == "plane":
@@ -234,20 +292,15 @@
             self.scratch += [dma((self.shards,)), dma((self.shards,))]
         if stages == "z":
             self.scratch += [pltpu.VMEM(array.shape, array.dtype), dma((2,))]
-        if stages != "z":
-            self.scratch += [dma((self.split, self.shards)), dma((self.split, self.shards))]
-
-    def valid(self, z):
-        if not self.half:
-            return None
-        return z // self.slots == lax.axis_index("core")
+        else:
+            self.plane = Plane(sizes, self.pair, 1, self.shards)
+            self.scratch += self.plane.scratch
 
     def guarded(self, z, body):
-        ok = self.valid(z)
-        if ok is None:
+        if self.half:
+            pl.when(z // self.slots == lax.axis_index("core"))(body)
+        else:
             body()
-        else:
-            pl.when(ok)(body)
 
     def slot(self, z):
         return lax.rem(z, self.slots) if self.half else z
@@ -266,25 +319,11 @@
             {"shard": peer},
         )
 
-    def start(self, ins, outs, scratch):
-        me = lax.axis_index("shard")
-        if self.stages == "plane":
-            self.plane_start(outs[0], scratch)
-            return
-        src, full = ins[0], outs[0]
-
-        def send():
-            each(1, self.shards, lambda k: self.z_copy(k, src, full, scratch, True).start())
-
-        self.guarded(me, send)
-        if self.stages == "both":
-            full[me] = src[...]
-        else:
-
-            def load():
-                pltpu.make_async_copy(src, scratch[2], scratch[3].at[0]).start()
-
-            self.guarded(me, load)
+    def z_start(self, src, full, scratch):
+        self.guarded(
+            lax.axis_index("shard"),
+            lambda: each(1, self.shards, lambda k: self.z_copy(k, src, full, scratch, True).start()),
+        )
 
     def z_finish(self, src, full, scratch):
         me = lax.axis_index("shard")
@@ -302,64 +341,226 @@
 
         self.guarded(me, sent)
 
-    def plane_copy(self, k, d, full, scratch, sending):
-        me, mine = lax.axis_index("shard"), lax.axis_index(self.split_axes)
-        z = lax.rem(me + d, self.shards)
-        if sending:
-            peer, owner = lax.rem(mine + k, self.split), mine
-        else:
-            peer = owner = lax.rem(mine + self.split - k, self.split)
-        region = full.at[self.slot(z), owner]
-        return z, remote(
-            region,
-            region,
-            scratch[-2].at[k, d],
-            scratch[-1].at[k, d],
-            peer_coords(peer, self.split_axes, self.sizes),
+    def steps(self, ins, outs, scratch):
+        me = lax.axis_index("shard")
+        src, full = ins[0], outs[0]
+        if self.stages == "z":
+            self.z_start(src, full, scratch)
+            load = pltpu.make_async_copy(src, scratch[2], scratch[3].at[0])
+            store = pltpu.make_async_copy(scratch[2], full.at[self.slot(me)], scratch[3].at[1])
+            self.guarded(me, load.start)
+            yield
+
+            def both():
+                load.wait()
+                store.start()
+
+            self.guarded(me, both)
+            yield
+            self.guarded(me, store.wait)
+            self.z_finish(src, full, scratch)
+            return
+
+        def shard_of(t):
+            return lax.rem(me + t, self.shards)
+
+        def region(t, chip, core):
+            return full.at[self.slot(shard_of(t)), 2 * chip + core if self.pair else chip]
+
+        guard = (lambda t, body: self.guarded(shard_of(t), body)) if self.half else always
+        if self.stages == "both":
+            self.z_start(src, full, scratch)
+            full[me] = src[...]
+            yield
+            self.z_finish(src, full, scratch)
+        self.plane.bind(
+            region, lambda t: lax.rem(shard_of(t), 2), guard, always, scratch[-len(self.plane.scratch) :]
         )
-
-    def plane_each(self, full, scratch, sending, act):
-        def peers(k):
-            def shards(d):
-                z, copy = self.plane_copy(k, d, full, scratch, sending)
-                self.guarded(z, lambda: act(copy))
-
-            each(1, self.shards, shards)
-
-        each(1, self.split, peers)
-
-    def plane_start(self, full, scratch):
-        self.plane_each(full, scratch, True, lambda copy: copy.start())
-
-    def middle(self, ins, outs, scratch):
-        if self.stages == "both":
-            self.z_finish(ins[0], outs[0], scratch)
-            self.plane_start(outs[0], scratch)
-        elif self.stages == "z":
-            me = lax.axis_index("shard")
-
-            def store():
-                pltpu.make_async_copy(ins[0], scratch[2], scratch[3].at[0]).wait()
-                pltpu.make_async_copy(
-                    scratch[2], outs[0].at[self.slot(me)], scratch[3].at[1]
-                ).start()
-
-            self.guarded(me, store)
-
-    def finish(self, ins, outs, scratch):
-        if self.stages == "z":
-            me = lax.axis_index("shard")
-
-            def stored():
-                pltpu.make_async_copy(
-                    scratch[2], outs[0].at[self.slot(me)], scratch[3].at[1]
-                ).wait()
-
-            self.guarded(me, stored)
-            self.z_finish(ins[0], outs[0], scratch)
-        else:
-            self.plane_each(outs[0], scratch, False, lambda copy: copy.wait_recv())
-            self.plane_each(outs[0], scratch, True, lambda copy: copy.wait_send())
+        self.plane.start()
+        yield
+        self.plane.forward()
+        yield
+        self.plane.finish()
+
+
+class Reduce(Item):
+    def __init__(self, sizes, array, stages, half=False, late=False, source=None):
+        self.stages, self.half, self.late, self.source = stages, half, late, source
+        self.pre = int(stages[0] == "pair" and not late)
+        self.chips, self.shards = sizes["chip"], sizes["shard"]
+        self.slots = self.shards // 2
+        lead = {"pair": 3, "plane": 2, "shard": 1, "spread": 0}[stages[0]]
+        unit = tuple(array.shape[lead:])
+        self.zs = array.shape[0]
+        zs, chips, dtype = self.zs, self.chips, array.dtype
+        self.inputs = [] if source is not None else [array]
+        self.from_hbm = source is None and stages[0] == "plane"
+        self.in_specs = [HBM_SPEC if self.from_hbm else VMEM_SPEC] * len(self.inputs)
+        self.names, self.scratch = [], []
+
+        def add(name, buffer):
+            self.names.append(name)
+            self.scratch.append(buffer)
+
+        dma = pltpu.SemaphoreType.DMA
+        if "pair" in stages:
+            add("pair_got", pltpu.VMEM((zs, chips) + unit, dtype))
+            add("pair_sum", pltpu.VMEM((zs, chips) + unit, dtype))
+            add("pair_sems", dma((2,)))
+        if "plane" in stages:
+            add("plane_got", pltpu.VMEM((chips - 1, zs) + unit, dtype))
+            add("plane_sent", dma((chips,)))
+            add("plane_arrived", dma((chips,)))
+            if self.from_hbm:
+                add("plane_own", pltpu.VMEM((zs,) + unit, dtype))
+                add("own_sems", dma((1,)))
+            if stages[-1] != "plane":
+                add("plane_sum", pltpu.VMEM((zs,) + unit, dtype))
+        if "shard" in stages:
+            add("shard_got", pltpu.VMEM((self.shards - 1,) + unit, dtype))
+            add("shard_sent", dma((self.shards,)))
+            add("shard_arrived", dma((self.shards,)))
+        shape = (zs,) + unit if stages[-1] == "plane" else unit
+        if stages[-1] == "spread":
+            shape = (chips,) + (() if half else (2,)) + unit
+            self.plane = Plane(sizes, True, 0, unit[0])
+            for index, buffer in enumerate(self.plane.scratch):
+                add("spread%d" % index, buffer)
+        self.out_shapes = [jax.ShapeDtypeStruct(shape, dtype)]
+        self.out_specs = [VMEM_SPEC]
+
+    def steps(self, ins, outs, scratch):
+        buf = dict(zip(self.names, scratch))
+        chip, core, shard = (lax.axis_index(name) for name in ALL)
+        now, out, last, sent = ins[0], outs[0], self.stages[-1], []
+        mine = out.at[chip] if self.half else out.at[chip, core]
+
+        def carrying(index):
+            return index // self.slots == core
+
+        def guard(t, body):
+            if self.half:
+                pl.when(carrying(shard))(body)
+            else:
+                body()
+
+        def other(t, body):
+            if self.half:
+                pl.when(jnp.logical_not(carrying(shard)))(body)
+            else:
+                body()
+
+        if "pair" in self.stages:
+            pair = remote(
+                now.at[:, :, 1 - core],
+                buf["pair_got"],
+                buf["pair_sems"].at[0],
+                buf["pair_sems"].at[1],
+                {"core": 1 - core},
+            )
+            pair.start()
+            yield
+            pair.wait()
+            given = now
+
+            def add_pair(index):
+                z, c = index // self.chips, lax.rem(index, self.chips)
+                total = given[z, c, core].astype(f32) + buf["pair_got"][z, c].astype(f32)
+                buf["pair_sum"][z, c] = total.astype(bf16)
+
+            each(0, self.zs * self.chips, add_pair)
+            now = buf["pair_sum"]
+        if "plane" in self.stages:
+            partial = now
+
+            def plane_copy(k):
+                peer = lax.rem(chip + k, self.chips)
+                return remote(
+                    partial.at[:, peer],
+                    buf["plane_got"].at[k - 1],
+                    buf["plane_sent"].at[k],
+                    buf["plane_arrived"].at[k],
+                    {"chip": peer},
+                )
+
+            each(1, self.chips, lambda k: plane_copy(k).start())
+            if self.from_hbm:
+                own = pltpu.make_async_copy(
+                    partial.at[:, chip], buf["plane_own"], buf["own_sems"].at[0]
+                )
+                own.start()
+            yield
+            each(1, self.chips, lambda k: plane_copy(k).wait_recv())
+            if self.from_hbm:
+                own.wait()
+            target = out if last == "plane" else buf["plane_sum"]
+
+            def add_plane(z):
+                total = (buf["plane_own"][z] if self.from_hbm else partial[z, chip]).astype(f32)
+                for k in range(self.chips - 1):
+                    total = total + buf["plane_got"][k, z].astype(f32)
+                target[z] = total.astype(bf16)
+
+            each(0, self.zs, add_plane)
+            sent.append(lambda: each(1, self.chips, lambda k: plane_copy(k).wait_send()))
+            now = target
+        if "shard" in self.stages:
+            summed = now
+
+            def slot(index):
+                return lax.rem(index, self.slots) if self.half else index
+
+            def shard_copy(k):
+                peer = lax.rem(shard + k, self.shards)
+                return peer, remote(
+                    summed.at[slot(peer)],
+                    buf["shard_got"].at[k - 1],
+                    buf["shard_sent"].at[k],
+                    buf["shard_arrived"].at[k],
+                    {"shard": peer},
+                )
+
+            def shard_each(act):
+                def one(k):
+                    peer, copy = shard_copy(k)
+                    if self.half:
+                        pl.when(carrying(peer))(lambda: act(copy))
+                    else:
+                        act(copy)
+
+                each(1, self.shards, one)
+
+            shard_each(lambda copy: copy.start())
+            yield
+
+            def add_shard():
+                each(1, self.shards, lambda k: shard_copy(k)[1].wait_recv())
+                target = mine if last == "spread" else out
+                for part in range(target.shape[0]):
+                    total = summed[slot(shard), part].astype(f32)
+                    for k in range(self.shards - 1):
+                        total = total + buf["shard_got"][k, part].astype(f32)
+                    target[part] = total.astype(bf16)
+
+            guard(0, add_shard)
+            sent.append(lambda: shard_each(lambda copy: copy.wait_send()))
+        if last == "spread":
+            if "shard" not in self.stages:
+                mine[...] = now[...]
+            self.plane.bind(
+                lambda t, c, k: out.at[c, t] if self.half else out.at[c, k, t],
+                lambda t: lax.rem(t, 2),
+                guard,
+                other,
+                [buf["spread%d" % index] for index in range(4)],
+            )
+            self.plane.start()
+            yield
+            self.plane.forward()
+            yield
+            self.plane.finish()
+        for wait in sent:
+            wait()
 
 
 class Compute:
@@ -382,6 +583,9 @@
 
         each(1, count, greet)
     pl.semaphore_wait(barrier, total)
+
+
+DONE = object()
 
 
 def run(collective_id, name, sizes, items, compute=None):
@@ -421,18 +625,25 @@
             )
 
         greet_all(sizes, wide)
+        going = {}
         for index, item in enumerate(items):
             if not item.late:
-                item.start(*parts(index))
+                going[index] = item.steps(*parts(index))
+                next(going[index])
         for index, item in enumerate(items):
-            item.middle(*parts(index))
+            if not item.late:
+                for _ in range(item.pre):
+                    next(going[index])
         if compute.body is not None:
             compute.body(ins[own[0] :], outs[own[1] :], tmp[own[2] :])
         for index, item in enumerate(items):
             if item.late:
-                item.start(*parts(index))
-        for index, item in enumerate(items):
-            item.finish(*parts(index))
+                going[index] = item.steps(*parts(index))
+                next(going[index])
+        for final in (False, True):
+            left = [index for index, item in enumerate(items) if item.final == final]
+            while left:
+                left = [index for index in left if next(going[index], DONE) is not DONE]
 
     return pl.pallas_call(
         kernel,
@@ -470,26 +681,29 @@
     qkv_ref, info_ref = ins
     out_ref, keep_ref, lse_ref = outs
     bias, acc, stat = tmp
-    blocks, _, slots = qkv_ref.shape[:3]
+    blocks, slots = qkv_ref.shape[0], qkv_ref.shape[1] // 3
+    source = key_slots(slots)
+    key = [key_unit(slots, source[m]) for m in range(slots)]
+    value = [value_unit(slots, source[m]) for m in range(slots)]
 
     @pl.loop(0, blocks)
     def _(i):
         bias[...] = diagonal_bias(info_ref[i])
         seg = segment_rows(info_ref[i, 1:2])
-        qa = [jnp.concatenate([qkv_ref[i, 0, m], seg], axis=0) for m in range(slots)]
+        qa = [jnp.concatenate([qkv_ref[i, m], seg], axis=0) for m in range(slots)]
         for m in range(slots):
-            s = dot(jnp.transpose(qkv_ref[i, 1, m]), qkv_ref[i, 0, m]) + bias[...]
+            s = dot(jnp.transpose(qkv_ref[i, key[m]]), qkv_ref[i, m]) + bias[...]
             top = jnp.max(s, axis=0, keepdims=True)
             p = jnp.exp(s - top)
             stat[2 * m : 2 * m + 1] = top
             stat[2 * m + 1 : 2 * m + 2] = jnp.sum(p, axis=0, keepdims=True)
-            acc[m] = dot(qkv_ref[i, 2, m], p.astype(bf16))
+            acc[m] = dot(qkv_ref[i, value[m]], p.astype(bf16))
 
         @pl.loop(0, i)
         def _(j):
             mask = mask_rows(info_ref[j, 0:1])
             for m in range(slots):
-                ka = jnp.transpose(jnp.concatenate([qkv_ref[j, 1, m], mask], axis=0))
+                ka = jnp.transpose(jnp.concatenate([qkv_ref[j, key[m]], mask], axis=0))
                 s = dot(ka, qa[m])
                 old = stat[2 * m : 2 * m + 1]
                 top = jnp.maximum(old, jnp.max(s, axis=0, keepdims=True))
@@ -499,7 +713,7 @@
                 stat[2 * m + 1 : 2 * m + 2] = stat[2 * m + 1 : 2 * m + 2] * factor + jnp.sum(
                     p, axis=0, keepdims=True
                 )
-                acc[m] = acc[m] * factor + dot(qkv_ref[j, 2, m], p.astype(bf16))
+                acc[m] = acc[m] * factor + dot(qkv_ref[j, value[m]], p.astype(bf16))
 
         for m in range(slots):
             total = stat[2 * m + 1 : 2 * m + 2]
@@ -513,12 +727,15 @@
     qkv_ref, do_ref, keep_ref, lse_ref, info_ref = ins
     (out_ref,) = outs
     bias, dq, qn, don, delta = tmp
-    blocks, _, slots = qkv_ref.shape[:3]
+    blocks, slots = qkv_ref.shape[0], qkv_ref.shape[1] // 3
+    source = key_slots(slots)
+    key = [key_unit(slots, source[m]) for m in range(slots)]
+    value = [value_unit(slots, source[m]) for m in range(slots)]
 
     @pl.loop(0, blocks)
     def _(i):
         for m in range(slots):
-            qn[i, m] = jnp.transpose(qkv_ref[i, 0, m])
+            qn[i, m] = jnp.transpose(qkv_ref[i, m])
             don[i, m] = jnp.transpose(do_ref[i, m])
             delta[i, m : m + 1] = jnp.sum(
                 do_ref[i, m].astype(f32) * keep_ref[i, m], axis=0, keepdims=True
@@ -529,49 +746,55 @@
     def _(j):
         bias[...] = diagonal_bias(info_ref[j])
         mask = mask_rows(info_ref[j, 0:1])
-        kn = [jnp.transpose(qkv_ref[j, 1, m]) for m in range(slots)]
+        kn = [jnp.transpose(qkv_ref[j, key[m]]) for m in range(slots)]
         ka = [
-            jnp.transpose(jnp.concatenate([qkv_ref[j, 1, m], mask], axis=0)) for m in range(slots)
+            jnp.transpose(jnp.concatenate([qkv_ref[j, key[m]], mask], axis=0)) for m in range(slots)
         ]
-        vn = [jnp.transpose(qkv_ref[j, 2, m]) for m in range(slots)]
+        vn = [jnp.transpose(qkv_ref[j, value[m]]) for m in range(slots)]
 
         def tile(i, m, s):
             p = jnp.exp(s - lse_ref[i, m : m + 1])
             dp = dot(vn[m], do_ref[i, m])
             ds = (p * (dp - delta[i, m : m + 1])).astype(bf16)
-            dq[i, m] += dot(qkv_ref[j, 1, m], ds)
+            dq[i, m] += dot(qkv_ref[j, key[m]], ds)
             return dot(ds, qn[i, m]), dot(p.astype(bf16), don[i, m])
 
         start = []
         for m in range(slots):
-            start += list(tile(j, m, dot(kn[m], qkv_ref[j, 0, m]) + bias[...]))
+            start += list(tile(j, m, dot(kn[m], qkv_ref[j, m]) + bias[...]))
 
         def later(i, carry):
             seg = segment_rows(info_ref[i, 1:2])
             new = []
             for m in range(slots):
-                qa = jnp.concatenate([qkv_ref[i, 0, m], seg], axis=0)
+                qa = jnp.concatenate([qkv_ref[i, m], seg], axis=0)
                 a, b = tile(i, m, dot(ka[m], qa))
                 new += [carry[2 * m] + a, carry[2 * m + 1] + b]
             return tuple(new)
 
         done = lax.fori_loop(j + 1, blocks, later, tuple(start))
+        done = [jnp.transpose(value) for value in done]
+        if slots == 2:
+            shared = (1 - source[1]).astype(f32)
+            done[0] = done[0] + done[2] * shared
+            done[1] = done[1] + done[3] * shared
         for m in range(slots):
-            out_ref[j, 1, m] = jnp.transpose(done[2 * m]).astype(bf16)
-            out_ref[j, 2, m] = jnp.transpose(done[2 * m + 1]).astype(bf16)
-
+            out_ref[j, key_unit(slots, m)] = done[2 * m].astype(bf16)
+            out_ref[j, value_unit(slots, m)] = done[2 * m + 1].astype(bf16)
 
     @pl.loop(0, blocks)
     def _(i):
         for m in range(slots):
-            out_ref[i, 0, m] = (dq[i, m] * HEAD_DIM ** (-0.5)).astype(bf16)
+            out_ref[i, m] = (dq[i, m] * HEAD_DIM ** (-0.5)).astype(bf16)
 
 
 def ffn_kernel(x_ref, gf_ref, gu_ref, down_ref, part_ref, gu_grad_ref, down_grad_ref, ffn, dx):
     k = pl.program_id(0)
-    half = gu_ref.shape[1] // 2
+    half = gu_ref.shape[2] // 2
     x, gf = x_ref[...], gf_ref[...]
-    both = dot(x, gu_ref[...])
+    filled = x.shape[1] // gu_ref.shape[0]
+    weight = jnp.concatenate([gu_ref[z, :filled] for z in range(gu_ref.shape[0])], axis=0)
+    both = dot(x, weight)
     gate, up = both[:, :half], both[:, half:]
     sig = 1.0 / (1.0 + jnp.exp(-gate))
     act = gate * sig
@@ -581,7 +804,7 @@
     grad_up = (grad_hidden * act).astype(bf16)
     grads = jnp.concatenate([grad_gate, grad_up], axis=1)
     ffn_now = dot(hidden, down_ref[...])
-    dx_now = dot(grads, gu_ref[...], 1, 1)
+    dx_now = dot(grads, weight, 1, 1)
 
     @pl.when(k == 0)
     def _():
@@ -595,7 +818,6 @@
 
     gu_grad = dot(x, grads, 0, 0)
     shards, padded = gu_grad_ref.shape[:2]
-    filled = x.shape[1] // shards
     for z in range(shards):
         gu_grad_ref[z, :filled] = gu_grad[z * filled : (z + 1) * filled].astype(bf16)
         if padded > filled:
@@ -610,17 +832,18 @@
             part_ref[c, 1] = ffn[c * rows : (c + 1) * rows].astype(bf16)
 
 
-def feed_forward(x, gf, gate_up, down, shards, padded):
+def feed_forward(x, gf, gate_up, down):
     tokens, width = x.shape
     hidden, columns = FF_CHUNK, 2 * FF_CHUNK
-    chunks = gate_up.shape[1] // columns
+    shards, padded = gate_up.shape[:2]
+    chunks = gate_up.shape[2] // columns
     return pl.pallas_call(
         ffn_kernel,
         grid=(chunks,),
         in_specs=[
             pl.BlockSpec((tokens, width), lambda k: (0, 0)),
             pl.BlockSpec((tokens, width), lambda k: (0, 0)),
-            pl.BlockSpec((width, columns), lambda k: (0, k)),
+            pl.BlockSpec((shards, padded, columns), lambda k: (0, 0, k)),
             pl.BlockSpec((hidden, width), lambda k: (k, 0)),
         ],
         out_specs=[
@@ -659,20 +882,25 @@
 
 def project_body(ins, outs, tmp):
     hidden_ref, weight_ref, gain_ref, cos_ref, sin_ref = ins
-    sent_ref, normed_ref = outs
-    reps, _, slots, _, rows = sent_ref.shape
+    sent_ref, normed_ref, full_ref = outs
+    reps, units, _, rows = sent_ref.shape
+    slots, filled = units // 3, full_ref.shape[0] // weight_ref.shape[0]
+    for z in range(weight_ref.shape[0]):
+        full_ref[z * filled : (z + 1) * filled] = weight_ref[z, :filled]
     hidden = hidden_ref[...].astype(f32)
     normed = rms_scale(hidden, gain_ref[...]).astype(bf16)
     normed_ref[...] = normed
     cosines, sines = cos_ref[...], sin_ref[...]
-    half, columns = HEAD_DIM // 2, weight_ref.shape[1]
+    half, columns = HEAD_DIM // 2, full_ref.shape[1]
 
     def put(kind, head, value):
-        sent_ref[head // slots, kind, head % slots] = value
+        slot = head % slots
+        unit = (slot, key_unit(slots, slot), value_unit(slots, slot))[kind]
+        sent_ref[head // slots, unit] = value
 
     for start in range(0, columns, 256):
         stop = min(start + 256, columns)
-        block = jnp.transpose(dot(normed, weight_ref[:, start:stop]))
+        block = jnp.transpose(dot(normed, full_ref[:, start:stop]))
         for head in range(start // HEAD_DIM, stop // HEAD_DIM):
             at = head * HEAD_DIM - start
             a, b = block[at : at + half], block[at + half : at + HEAD_DIM]
@@ -704,14 +932,17 @@
 
 
 def project_back_body(ins, outs, tmp):
-    grads_ref, cos_ref, sin_ref, weight_ref, hidden_ref, normed_ref, gain_ref, base_ref = ins
-    sent_ref, weight_grad_ref, gain_grad_ref = outs
+    (grads_ref, cos_ref, sin_ref, weight_ref, hidden_ref, normed_ref, gain_ref, base_ref) = ins[:8]
+    vectors_ref = ins[8]
+    sent_ref, weight_grad_ref, vectors_grad_ref = outs
     (dt,) = tmp
-    slots, half = grads_ref.shape[2], HEAD_DIM // 2
+    slots, half = grads_ref.shape[1] // 3, HEAD_DIM // 2
     cosines, sines = cos_ref[...], sin_ref[...]
 
     def get(kind, head):
-        return grads_ref[head // slots, kind, head % slots].astype(f32)
+        slot = head % slots
+        unit = (slot, key_unit(slots, slot), value_unit(slots, slot))[kind]
+        return grads_ref[head // slots, unit].astype(f32)
 
     def back(value):
         a, b = value[:half], value[half:]
@@ -722,33 +953,81 @@
     for group in range(KEY_VALUE_HEADS):
         for kind in (1, 2):
             value = get(kind, group * GROUP)
-            for m in range(1, GROUP):
-                value = value + get(kind, group * GROUP + m)
+            for head in range(group * GROUP + 1, (group + 1) * GROUP):
+                if slots != 2 or head % 2 == 0:
+                    value = value + get(kind, head)
             if kind == 1:
                 value = back(value)
             at = (QUERY_HEADS + (kind - 1) * KEY_VALUE_HEADS + group) * HEAD_DIM
             dt[at : at + HEAD_DIM] = value.astype(bf16)
     grad = dot(dt[...], weight_ref[...], 0, 1)
     norm_grad, gain_grad = norm_back(hidden_ref[...].astype(f32), gain_ref[...], grad)
-    gain_grad_ref[...] = jnp.broadcast_to(gain_grad[None], gain_grad_ref.shape)
+    index = lax.broadcasted_iota(jnp.int32, vectors_ref.shape, 0)
+    vectors = jnp.where(index == 0, gain_grad[None], vectors_ref[...])
+    piece = vectors_grad_ref.shape[2]
+    for z in range(vectors_grad_ref.shape[0]):
+        vectors_grad_ref[z] = vectors[:, z * piece : (z + 1) * piece]
     total = (base_ref[...] + norm_grad).astype(bf16)
     devices, per_pair = sent_ref.shape[:2]
     sent_ref[...] = total.reshape(sent_ref.shape)
-    shards, reps, unit, columns = weight_grad_ref.shape
+    shards, chips, cores, parts, unit, columns = weight_grad_ref.shape
     filled = normed_ref.shape[1] // shards
+    places = [(c, k, p) for c in range(chips) for k in range(cores) for p in range(parts)]
     for start in range(0, columns, 256):
         stop = min(start + 256, columns)
         block = dot(normed_ref[...], dt[start:stop], 0, 1)
         for z in range(shards):
-            for r in range(reps):
+            for r, place in enumerate(places):
                 size = max(0, min(unit, filled - r * unit))
                 at = z * filled + r * unit
+                here = weight_grad_ref.at[z, *place]
                 if size:
-                    weight_grad_ref[z, r, :size, start:stop] = block[at : at + size].astype(bf16)
+                    here[:size, start:stop] = block[at : at + size].astype(bf16)
                 if size < unit:
-                    weight_grad_ref[z, r, size:, start:stop] = jnp.zeros(
-                        (unit - size, stop - start), bf16
-                    )
+                    here[size:, start:stop] = jnp.zeros((unit - size, stop - start), bf16)
+
+
+def finalize_kernel(gate_up_ref, down_ref, out_ref, qkv_ref, gate, up, down, out, query, key, value):
+    cores, rows, columns = gate_up_ref.shape[1:]
+    half = columns // 2
+    for core in range(cores):
+        for start in range(0, columns, 2 * FF_CHUNK):
+            at = core * half + start // 2
+            middle = start + FF_CHUNK
+            gate[:, at : at + FF_CHUNK] = gate_up_ref[0, core, :, start:middle].astype(f32)
+            up[:, at : at + FF_CHUNK] = gate_up_ref[0, core, :, middle : middle + FF_CHUNK].astype(f32)
+    down[...] = down_ref[0].astype(f32)
+    out[...] = out_ref[0].astype(f32)
+    ends = (query.shape[1], query.shape[1] + key.shape[1])
+    qkv = qkv_ref[0].astype(f32)
+    query[...] = qkv[:, : ends[0]]
+    key[...] = qkv[:, ends[0] : ends[1]]
+    value[...] = qkv[:, ends[1] :]
+
+
+def finalize(gate_up, down, out, qkv, shard_rows, key_width):
+    chips, rows = gate_up.shape[0], gate_up.shape[2]
+    width, hidden = out.shape[2], gate_up.shape[3]
+    columns = (hidden, hidden, None, width, width, key_width, key_width)
+
+    def out_spec(array_columns):
+        shape = tuple(down.shape[1:]) if array_columns is None else (rows, array_columns)
+        return pl.BlockSpec(shape, lambda c: (c, 0))
+
+    def out_type(array_columns):
+        shape = (chips * down.shape[1], down.shape[2])
+        shape = shape if array_columns is None else (shard_rows, array_columns)
+        return jax.ShapeDtypeStruct(shape, f32)
+
+    return pl.pallas_call(
+        finalize_kernel,
+        grid=(chips,),
+        in_specs=[pl.BlockSpec((1, 2, rows, hidden), lambda c: (c, 0, 0, 0))]
+        + [pl.BlockSpec((1,) + tuple(a.shape[1:]), lambda c: (c, 0, 0)) for a in (down, out, qkv)],
+        out_specs=[out_spec(c) for c in columns],
+        out_shape=[out_type(c) for c in columns],
+        name="finalize",
+    )(gate_up, down, out, qkv)
 
 
 def rounded_up(value, unit):
@@ -831,15 +1110,15 @@
         "first",
         sizes,
         [
-            AllToAll(sizes, by_slot(hidden_in), ALL),
-            AllToAll(sizes, place_sent, ALL),
+            AllToAll(sizes, by_slot(hidden_in), ALL, late=True),
+            AllToAll(sizes, place_sent, ALL, late=True),
             AllToAll(sizes, vectors, ("shard",), spread=True),
             Gather(sizes, qkv_shard, REP, "both"),
         ],
     )
     hidden = got_hidden.reshape(rows, width)
     place = got_place[:, 0, :per_pair].reshape(rows)
-    qkv_full = full_rows(qkv_full)
+    qkv_full = qkv_full.reshape(shards, padded, -1)
     vectors_full = jnp.transpose(vectors_got[:, :3], (1, 0, 2)).reshape(3, width)
     gain_one, gain_two, full_router = vectors_full[0], vectors_full[1], vectors_full[2]
 
@@ -856,9 +1135,9 @@
     angles = frequency[:, None] * within.astype(f32)[None, :]
     cosines, sines = jnp.cos(angles), jnp.sin(angles)
 
-    heads_shape = (reps, 3, slots, HEAD_DIM, rows)
+    heads_shape = (reps, 3 * slots, HEAD_DIM, rows)
     heads_type = jax.ShapeDtypeStruct(heads_shape, bf16)
-    gate_up_z, down_z, out_z, info_got, qkv_got, _, first_normalized = run(
+    gate_up_z, down_z, out_z, info_got, qkv_got, _, first_normalized, qkv_weights = run(
         2,
         "project",
         sizes,
@@ -867,12 +1146,16 @@
             Gather(sizes, down_shard, ("chip",), "z", half=True),
             Gather(sizes, out_shard, REP, "z"),
             AllToAll(sizes, info, REP, spread=True),
-            AllToAll(sizes, heads_type, REP, late=True, source=0),
+            Heads(sizes, heads_type, True, 0),
         ],
         Compute(
             project_body,
             [hidden, qkv_full, gain_one[None], cosines, sines],
-            [heads_type, jax.ShapeDtypeStruct((rows, width), bf16)],
+            [
+                heads_type,
+                jax.ShapeDtypeStruct((rows, width), bf16),
+                jax.ShapeDtypeStruct((width, qkv_full.shape[2]), bf16),
+            ],
         ),
     )
     slot_type = jax.ShapeDtypeStruct((reps, slots, HEAD_DIM, rows), bf16)
@@ -904,7 +1187,7 @@
     )
     attn_out_t = att_home.reshape(padded_heads * HEAD_DIM, rows)[:width]
     full_out = full_rows(out_full)
-    gate_up = full_rows(gate_up_full)
+    gate_up = gate_up_full.reshape(shards, padded, 2 * ff_half)
     down = down_full.reshape(ff_half, width)
 
     hidden_f = hidden.astype(f32)
@@ -931,8 +1214,6 @@
         gf_pair.reshape(2 * rows, width),
         gate_up,
         down,
-        shards,
-        padded,
     )
     (parts_got,) = run(5, "parts", sizes, [AllToAll(sizes, parts, ("core",))])
     grad_normed_two = parts_got[0, 0].astype(f32) + parts_got[1, 0].astype(f32)
@@ -949,22 +1230,23 @@
     (grad_got,) = run(6, "grads", sizes, [AllToAll(sizes, grad_attention_t, REP)])
 
     out_grad = jnp.einsum("dt,te->de", attn_out_t, grad_attn, preferred_element_type=f32)
+    parts = 2 if chips == 4 else 1
     out_grad = jnp.pad(
         out_grad.astype(bf16).reshape(shards, shard_rows, width),
         ((0, 0), (0, padded - shard_rows), (0, 0)),
-    ).reshape(shards, reps, rep_unit, width)
-    gate_up_grad = gate_up_grad.reshape(shards, chips, chip_unit, 2 * ff_half)
-    down_grad = down_grad.reshape(shards // 2, chips, down_unit, width)
-    gate_up_recv, down_recv, out_recv, home_out, heads_home, _ = run(
+    ).reshape(shards, chips, 2, parts, rep_unit // parts, width)
+    gate_up_grad = gate_up_grad.reshape(shards, chips, parts, chip_unit // parts, 2 * ff_half)
+    down_grad = down_grad.reshape(shards // 2, chips, parts, down_unit // parts, width)
+    gate_up_sum, down_sum, out_sum, home_out, heads_home, _ = run(
         7,
         "attend_back",
         sizes,
         [
-            Scatter(sizes, gate_up_grad, ("chip",), 1),
-            Scatter(sizes, down_grad, ("chip",), 1),
-            Scatter(sizes, out_grad, REP, 1),
+            Reduce(sizes, gate_up_grad, ("plane", "shard")),
+            Reduce(sizes, down_grad, ("plane",)),
+            Reduce(sizes, out_grad, ("pair", "plane")),
             AllToAll(sizes, result.reshape(devices, per_pair, width), ALL),
-            AllToAll(sizes, heads_type, REP, late=True, source=0),
+            Heads(sizes, heads_type, False, 0),
         ],
         Compute(
             backward_body,
@@ -980,32 +1262,26 @@
         ),
     )
 
-    def summed(own, got):
-        total = own.astype(f32)
-        for index in range(got.shape[0]):
-            total = total + got[index].astype(f32)
-        return total.astype(bf16)
-
-    def taken(array, index, dim):
-        return lax.dynamic_index_in_dim(array, index, dim, keepdims=False)
-
-    gate_up_sum = summed(taken(gate_up_grad, chip, 1), gate_up_recv)
-    down_sum = summed(taken(down_grad, chip, 1), down_recv)
-    out_sum = summed(taken(out_grad, rep, 1), out_recv)
-
     base = grad_out + grad_middle + grad_logit[:, None] * full_router
+    router_grad = jnp.sum(grad_logit[:, None] * hidden_f, axis=0)
+    vector_grads = jnp.pad(jnp.stack([grad_gain_ffn, router_grad]), ((1, 5), (0, 0)))
     tokens_type = jax.ShapeDtypeStruct((devices, per_pair, width), bf16)
-    qkv_grad_type = jax.ShapeDtypeStruct((shards, reps, rep_unit, qkv_full.shape[1]), bf16)
-    gate_up_recv, down_recv, out_recv, home_grad, qkv_recv, _, qkv_grad, gain_grad = run(
+    qkv_columns = qkv_weights.shape[1]
+    qkv_grad_type = jax.ShapeDtypeStruct(
+        (shards, chips, 2, parts, rep_unit // parts, qkv_columns), bf16
+    )
+    vectors_type = jax.ShapeDtypeStruct((shards, 8, shard_rows), f32)
+    qkv_home, gate_up_home, down_home, out_home, home_grad, vectors_home = run(
         8,
         "project_back",
         sizes,
         [
-            Scatter(sizes, gate_up_sum, ("shard",), 0),
-            Scatter(sizes, down_sum, ("shard",), 0, half=True),
-            Scatter(sizes, out_sum, ("shard",), 0),
+            Reduce(sizes, qkv_grad_type, ("pair", "plane", "shard", "spread"), late=True, source=1),
+            Reduce(sizes, gate_up_sum, ("spread",)),
+            Reduce(sizes, down_sum, ("shard", "spread"), half=True),
+            Reduce(sizes, out_sum, ("shard", "spread")),
             AllToAll(sizes, tokens_type, ALL, late=True, source=0),
-            Scatter(sizes, qkv_grad_type, REP, 1, late=True, source=1),
+            AllToAll(sizes, vectors_type, ALL, by_shard=True, late=True, source=2),
         ],
         Compute(
             project_back_body,
@@ -1013,51 +1289,27 @@
                 heads_home,
                 cosines,
                 sines,
-                qkv_full,
+                qkv_weights,
                 hidden,
                 first_normalized,
                 gain_one[None],
                 base,
+                vector_grads,
             ],
-            [tokens_type, qkv_grad_type, jax.ShapeDtypeStruct((8, width), f32)],
-            [pltpu.VMEM((qkv_full.shape[1], rows), bf16)],
+            [tokens_type, qkv_grad_type, vectors_type],
+            [pltpu.VMEM((qkv_columns, rows), bf16)],
         ),
+    )[:6]
+    weight_grads = finalize(
+        gate_up_home.reshape(chips, 2, chip_unit, 2 * ff_half),
+        down_home.reshape(chips, down_unit, width),
+        out_home.reshape(chips, chip_unit, width),
+        qkv_home.reshape(chips, chip_unit, qkv_columns),
+        shard_rows,
+        key_matrix.shape[1],
     )
-    gate_up_sum = summed(taken(gate_up_sum, shard, 0), gate_up_recv)
-    down_sum = summed(taken(down_sum, lax.rem(shard, shards // 2), 0), down_recv)
-    out_sum = summed(taken(out_sum, shard, 0), out_recv)
-    qkv_sum = summed(taken(qkv_grad, rep, 1), qkv_recv)
-    router_grad = jnp.sum(grad_logit[:, None] * hidden_f, axis=0)
-    vector_grads = jnp.stack([gain_grad[0], grad_gain_ffn, router_grad])
-    vector_grads = jnp.pad(vector_grads, ((0, 5), (0, 0))).reshape(8, shards, shard_rows)
-    vector_grads = jnp.broadcast_to(
-        jnp.transpose(vector_grads, (1, 0, 2))[None], (reps, shards, 8, shard_rows)
-    ).reshape(devices, 8, shard_rows)
-    gate_up_home, down_home, out_home, vectors_home, qkv_recv = run(
-        9,
-        "totals",
-        sizes,
-        [
-            AllToAll(sizes, gate_up_sum, REP, spread=True),
-            SpreadHalf(sizes, down_sum),
-            AllToAll(sizes, out_sum, REP, spread=True),
-            AllToAll(sizes, vector_grads, ALL),
-            Scatter(sizes, qkv_sum, ("shard",), 0),
-        ],
-    )
-    qkv_sum = summed(taken(qkv_sum, shard, 0), qkv_recv)
-    (qkv_home,) = run(10, "last", sizes, [AllToAll(sizes, qkv_sum, REP, spread=True)])
-
-    qkv_total = qkv_home.reshape(padded, -1)[:shard_rows].astype(f32)
-    out_total = out_home.reshape(padded, width)[:shard_rows].astype(f32)
-    gate_up_total = gate_up_home.reshape(chips, 2, chip_unit, chunks, 2, FF_CHUNK)
-
-    def half_total(which):
-        total = jnp.transpose(gate_up_total[:, :, :, :, which], (0, 2, 1, 3, 4))
-        return total.reshape(padded, 2 * ff_half)[:shard_rows].astype(f32)
-
+    gate_total, up_total, down_total, out_total, query_total, key_total, value_total = weight_grads
     vector_total = jnp.sum(vectors_home, axis=0)
-    q_end, k_end = query_weight.shape[1], query_weight.shape[1] + key_matrix.shape[1]
 
     def home_rows(home):
         home = home.reshape(rows, width)
@@ -1066,13 +1318,13 @@
     return (
         home_rows(home_out),
         home_rows(home_grad),
-        qkv_total[:, :q_end],
-        qkv_total[:, q_end:k_end],
-        qkv_total[:, k_end:],
+        query_total,
+        key_total,
+        value_total,
         out_total,
-        half_total(0),
-        half_total(1),
-        down_home.reshape(-1, width).astype(f32),
+        gate_total,
+        up_total,
+        down_total,
         vector_total[0],
         vector_total[1],
         vector_total[2],

time: 774 us -> 588 us (0.76)
  Pallas kernels: 642 us -> 518 us
  local copies, waits for them, and re-layouts: 60.4 us -> 27.2 us
  other arithmetic: 50.1 us -> 23.5 us
    pallas_call x10 -> x8, Pallas kernels: 606 us -> 475 us  [run(): pl.pallas_call(kernel, out_shape=out_shapes, in_specs=in_specs, out_specs...]
    convert_element_type x8 -> x0, other arithmetic: 21.7 us -> none  [the longest x4 12.5 us: summed(): return total.astype(bf16)]
    reshape x4 -> x0, local copies, waits for them, and re-layouts: 11.3 us -> none  [the longest x1 6.6 us: local(): gate_up_home.reshape(chips, 2, chip_unit, chunks, 2, FF_CHUNK)]
    slice x5 -> x0, local copies, waits for them, and re-layouts: 10.6 us -> none  [the longest x1 7.68 us: half_total(): total = jnp.transpose(gate_up_total[:, :, :, :, which], (0, 2, 1, 3, 4))]
    slice x3 -> x1, local copies, waits for them, and re-layouts: 9.02 us -> 0.16 us  [full_rows(): return full[:, :shard_rows].reshape(width, full.shape[-1])]
where the time goes in v3:
time: 588 us; the launch traced here: 581 us
  Pallas kernels  518 us (88%)
  local copies, waits for them, and re-layouts  27.2 us (5%)
  other arithmetic  23.5 us (4%)
  matrix products  11.2 us (2%)
    pallas_call x8, Pallas kernels, run(): pl.pallas_call(kernel, out_shape=out_shapes, in_specs=in_specs, out_specs...  475 us
    pallas_call x1, Pallas kernels, feed_forward(): pl.pallas_call(ffn_kernel, grid=(chunks,), in_specs=[pl.BlockSpec((tokens...  36.2 us

profile of v3, /device:TPU:0, one launch (start us, length us, event | category | flops | bytes accessed | tf_op | source)
XLA Modules:
  0.0 581.4 jit_solution(15365346868643308247)
XLA Ops:
  3.4 1.3 copy.109
  7.1 47.4 %first.1 = (bf16[32,16,960]{2,1,0:T(8,128)(2,1)}, s32[32,1,128]{2,1,0:T(1,128)}, f32[4,8,240]{2,1,0:T(8,128)}, bf16[4,8,32,1600]{3,2,1,0:T(8,128)(2,1)}) custom-call(bf16[32,16,960]{2,1,0:T(8,128)(2,1)} %bitcast.108, s32[32,1,128]{2,1,0:T(1,128)} %pad.38.refs_1_, f32[8,240]{1,0:T(8,128)} %fusion.26.refs_2_, bf16[8,32,1600]{2,1,0:T(8,128)(2,1)} %bitcast.112), custom_call_target="tpu_custom_call" | custom-call | tf_op jit(solution)/shard_map/first/pallas_call | solution.py:648
  55.4 1.5 fusion.4
  58.9 1.2 broadcast_select_fusion
  61.5 1.0 multiply_sine_fusion
  62.5 1.2 constant_dynamic-slice_fusion
  64.4 1.3 copy.115
  66.6 1.1 pad.42
  68.4 1.9 copy.116
  71.2 53.6 %project.1 = (bf16[4,4,64,2560]{3,2,1,0:T(8,128)(2,1)}, bf16[2,4,160,960]{3,2,1,0:T(8,128)(2,1)}, bf16[4,8,32,960]{3,2,1,0:T(8,128)(2,1)}, s32[8,8,512]{2,1,0:T(...) custom-call(bf16[4,64,2560]{2,1,0:T(8,128)(2,1)} %bitcast.106, ...), custom_call_target="tpu_custom_call" | custom-call | tf_op jit(solution)/shard_map/project/pallas_call | solution.py:648
  125.5 1.3 copy.117
  126.8 107.4 %attend.1 = (bf16[4,4,64,2560]{3,2,1,0:T(8,128)(2,1)}, bf16[2,4,160,960]{3,2,1,0:T(8,128)(2,1)}, bf16[4,8,32,960]{3,2,1,0:T(8,128)(2,1)}, bf16[32,16,960]{2,1,0:...) custom-call(bf16[4,4,64,2560]{3,2,1,0:T(8,128)(2,1)} %get-tuple-elem, ...), custom_call_target="tpu_custom_call", output_to_operand_aliasing={{0}: (0, {}), {1}: (1, {}), {2}: (2, {})} | custom-call | tf_op jit(solution)/shard_map/attend/pallas_call | solution.py:648
  234.2 2.6 fusion.1.refs_1_
  237.0 1.4 copy-done.2
  239.1 2.6 multiply_reduce_fusion.1
  241.8 2.9 multiply_convert_fusion.refs_0_
  244.7 8.4 %pair.1 = (bf16[2,512,960]{2,1,0:T(8,128)(2,1)}, bf16[2,512,960]{2,1,0:T(8,128)(2,1)}) custom-call(bf16[512,960]{1,0:T(8,128)(2,1)} %multiply_convert_fusion.refs_0_, bf16[512,960]{1,0:T(8,128)(2,1)} %fusion.1.refs_1_), custom_call_target="tpu_custom_call" | custom-call | tf_op jit(solution)/shard_map/pair/pallas_call | solution.py:648
  253.0 36.2 %feed_forward.1 = (bf16[2,2,512,960]{3,2,1,0:T(8,128)(2,1)}, bf16[4,256,2560]{2,1,0:T(8,128)(2,1)}, bf16[1280,960]{1,0:T(8,128)(2,1)}) custom-call(bf16[1024,960]{1,0:T(8,128)(2,1)} %bitcast.118, bf16[1024,960]{1,0:T(8,128)(2,1)} %bitcast.119, bf16[4,256,2560]{2,1,0:T(8,128)(2,1)} %bitcast.100, bf16[1280,960]{1,0:T(8,128)(2,1)} %bitcast.101), custom_call_target="tpu_custom_call" | custom-call | tf_op jit(solution)/shard_map/feed_forward/pallas_call | solution.py:840
  289.2 11.0 %parts.1 = bf16[2,2,512,960]{3,2,1,0:T(8,128)(2,1)} custom-call(bf16[2,2,512,960]{3,2,1,0:T(8,128)(2,1)} %get-tuple-element.71.refs_0_), custom_call_target="tpu_custom_call" | custom-call | tf_op jit(solution)/shard_map/parts/pallas_call | solution.py:648
  300.3 4.3 fusion.9
  306.4 5.1 fusion.6
  311.5 1.2 convolution_convert_fusion.3
  312.8 1.0 pad.46
  313.8 15.3 %grads.1.refs_5_ = bf16[8,2,64,512]{3,2,1,0:T(8,128)(2,1)} custom-call(bf16[8,2,64,512]{3,2,1,0:T(8,128)(2,1)} %bitcast.109), custom_call_target="tpu_custom_call" | custom-call | tf_op jit(solution)/shard_map/grads/pallas_call | solution.py:648
  329.2 1.2 convolution_convert_fusion
  330.4 1.6 pad.45
  331.9 146.0 %attend_back.1 = (bf16[2,32,2560]{2,1,0:T(8,128)(2,1)}, bf16[2,2,80,960]{3,2,1,0:T(8,128)(2,1)}, bf16[4,2,16,960]{3,2,1,0:T(8,128)(2,1)}, bf16[32,16,960]{2,1,0:...) custom-call(bf16[4,4,2,32,2560]{4,3,2,1,0:T(8,128)(2,1)} %bitcast.105, ...), custom_call_target="tpu_custom_call" | custom-call | tf_op jit(solution)/shard_map/attend_back/pallas_call | solution.py:648
  478.0 85.9 %project_back.1 = (bf16[4,2,2,16,1600]{4,3,2,1,0:T(8,128)(2,1)}, bf16[4,2,2,32,2560]{4,3,2,1,0:T(8,128)(2,1)}, bf16[4,2,80,960]{3,2,1,0:T(8,128)(2,1)}, bf16[4,2...) custom-call(bf16[2,32,2560]{2,1,0:T(8,128)(2,1)} %get-tuple-element., ...), custom_call_target="tpu_custom_call" | custom-call | tf_op jit(solution)/shard_map/project_back/pallas_call | solution.py:648
  563.9 6.8 %finalize.1 = (f32[240,2560]{1,0:T(8,128)}, f32[240,2560]{1,0:T(8,128)}, f32[640,960]{1,0:T(8,128)}, f32[240,960]{1,0:T(8,128)}, f32[240,960]{1,0:T(8,128)}, /*index=5*/f32[240,320]{1,0:T(8,128)}, f32[240,320]{1,0:T(8,128)}) custom-call(bf16[4,2,64,2560]{3,2,1,0:T(8,128)(2,1)} %bitcast.115, bf16[4,160,960]{2,1,0:T(8,128)(2,1)} %bitcast.123, ...), custom_call_target="tpu_custom_call" | custom-call | tf_op jit(solution)/shard_map/finalize/pallas_call | solution.py:1022
  570.7 3.2 copy.125
  575.7 3.0 convolution_convert_fusion.1
  579.3 1.7 convolution_convert_fusion.2
  (119 shorter events, 18.3 us)
Async XLA Ops:
  0.6 2.0 copy-start
  1.7 3.0 copy-start.19
  2.6 2.1 copy-start.16
  2.6 2.3 copy-start.17
  2.6 2.4 copy-start.11
  4.7 1.7 copy-start.29
  4.7 1.8 copy-start.30
  4.7 1.8 copy-start.31
  5.4 52.4 %copy-start.23 = (s32[512]{0:T(512)S(1)}, s32[512]{0:T(512)}, u32[]{:S(2)}) copy-start(s32[512]{0:T(512)} %param.19) | copy-start | bytes 6148
  5.4 52.6 %copy-start.32 = (s32[1,8]{1,0:T(1,128)S(1)}, s32[1,8]{1,0:T(1,128)}, u32[]{:S(2)}) copy-start(s32[1,8]{1,0:T(1,128)} %param.18) | copy-start | bytes 100
  6.4 56.1 %copy-start.14 = (bf16[240,2560]{1,0:T(8,128)(2,1)S(1)}, bf16[240,2560]{1,0:T(8,128)(2,1)}, u32[]{:S(2)}) copy-start(bf16[240,2560]{1,0:T(8,128)(2,1)} %param.25) | copy-start | bytes 3686404
  60.0 4.1 copy-start.21
  66.6 1.8 copy-start.7
  66.6 3.7 copy-start.10
  71.1 53.6 %copy-start.20 = (s32[512]{0:T(512)S(1)}, s32[512]{0:T(512)}, u32[]{:S(2)}) copy-start(s32[512]{0:T(512)} %copy-done.19) | copy-start | bytes 6148
  71.1 53.6 %copy-start.28 = (bf16[512,960]{0,1:T(8,128)(2,1)S(1)}, bf16[512,960]{0,1:T(8,128)(2,1)}, u32[]{:S(2)}) copy-start(bf16[512,960]{0,1:T(8,128)(2,1)} %param.16) | copy-start | bytes 2949124
  234.2 2.6 copy-start.4
  236.8 1.5 copy-start.2
  236.8 2.2 copy-start.25
  237.0 4.7 copy-start.5
  289.2 11.0 %copy-start.3 = (bf16[32,16,960]{2,1,0:T(8,128)(2,1)S(1)}, bf16[32,16,960]{2,1,0:T(8,128)(2,1)}, u32[]{:S(2)}) copy-start(bf16[32,16,960]{2,1,0:T(8,128)(2,1)} %get-tuple-element.64) | copy-start | bytes 2949124
  300.3 4.4 copy-start.22
  300.3 4.5 copy-start.18
  300.3 6.1 %copy-start.24 = (pred[512]{0:T(512)(128)(4,1)S(1)}, pred[512]{0:T(512)(128)(4,1)}, u32[]{:S(2)}) copy-start(pred[512]{0:T(512)(128)(4,1)} %get-tuple-element.175) | copy-start | bytes 1540
  306.4 5.1 copy-start.6
  312.8 16.4 %copy-start.26 = (bf16[8,2,64,512]{3,2,1,0:T(8,128)(2,1)S(1)}, bf16[8,2,64,512]{3,2,1,0:T(8,128)(2,1)}, u32[]{:S(2)}) copy-start(bf16[8,2,64,512]{3,2,1,0:T(8,128)(2,1)} %get-tuple-element.62) | copy-start | bytes 3145732
  313.8 15.4 %copy-start.9 = (bf16[512,960]{1,0:T(8,128)(2,1)S(1)}, bf16[512,960]{1,0:T(8,128)(2,1)}, u32[]{:S(2)}) copy-start(bf16[512,960]{1,0:T(8,128)(2,1)} %copy-done.8) | copy-start | bytes 2949124
  570.7 3.2 copy-start.13
  570.7 4.1 copy-start.12
  573.9 4.8 copy-start.15
  573.9 5.4 copy-start.27
  575.7 5.3 copy-start.1
  (1 other events, 1.2 us)
